TPU v7x, 512 devices: a whole 4x8x8 slice. The times are simulated.
512 devices in a mesh: section: 8 (over y), sec: 64 (over x, z, core).
Axes of the slice: x: 4, y: 8, z: 8, core: 2. Of those that a mesh axis runs over, the one named last changes fastest.
Arguments:
- saved_inputs: bfloat16 [8, 2, 64, 128, 256], P('section', None, 'sec'), may hold values from -6 to 6
- weights: bfloat16 [8, 2304, 256], P('section', 'sec'), may hold values from -0.25 to 0.25
- biases: float32 [8, 256], P('section'), may hold values from -3 to 3
- cotangent: bfloat16 [2, 64, 128, 256], P(None, 'sec'), may hold values from -6 to 6
- tile_list: int32 [64, 6], P('sec'), may hold values from 0 to 7, as said below
- tile_count: int32 [64], P('sec'), may hold values from 1 to 6, as said below
- order: int32 [2], replicated, may hold values from 0 to 1, each once
Outputs:
- grad_inputs: bfloat16 [8, 2, 64, 128, 256], P('section', None, 'sec')
- weight_grads: float32 [8, 2304, 256], P('section', 'sec')
- bias_grads: float32 [8, 256], P('section', 'sec')
Inputs may be any that keep to these rules, and one draw needn't show every extreme that they name: Each row of tile_list holds distinct tile indices; entries past the band's tile_count are other tiles and stand for nothing. `tile_count`: some row band has exactly 6 on-limb tiles. `order`: A permutation of the images.
All inputs are finite; a program needn't handle non-finite values.
Results may differ from a plain program's by a relative error of at most 0.03.
Values may be sent and summed in bfloat16 or wider, within the bound.
No kernel may reach another device: no remote copies, remote signals or barrier semaphores. Data moves between devices by JAX's collectives and lax.ppermute only.
A program may use at most 64 MiB of HBM per device.

v0:
```python
import jax
import jax.numpy as jnp
from jax import lax
from jax.sharding import PartitionSpec as P

TILE = 16


def padded_2(array, sides, width):
    for axis, dim in sides:
        size, length = (lax.axis_size(axis), array.shape[dim])
        up = [(i, (i + 1) % size) for i in range(size - 1)]
        down = [(j, i) for i, j in up]
        last = lax.slice_in_dim(array, length - width, length, axis=dim)
        initial = lax.slice_in_dim(array, 0, width, axis=dim)
        before = lax.ppermute(last, axis, up)
        after = lax.ppermute(initial, axis, down)
        array = jnp.concatenate([before, array, after], axis=dim)
    return array


def from_behind(array, axis, by):
    length = lax.axis_size(axis)
    pairs = [(i, i + by) for i in range(length) if 0 <= i + by < length]
    return lax.ppermute(array, axis, pairs)


def patches(padded, rows, cols):
    return jnp.concatenate(
        [padded[..., a : a + rows, b : b + cols, :] for a in range(3) for b in range(3)], -1
    )


def silu_grad(pre, upstream):
    sig = jax.nn.sigmoid(pre)
    return upstream.astype(jnp.float32) * (sig * (1.0 + pre * (1.0 - sig)))


def outer_sum(columns, gpre):
    return lax.dot_general(
        columns, gpre, (((0,), (0,)), ((), ())), preferred_element_type=jnp.float32
    )


def body(saved_inputs, weights, biases, cotangent, tile_list, tile_count, order):
    n_section = lax.axis_size("section")
    section = lax.axis_index("section")
    inputs = saved_inputs[0]
    slots_n, rows, cols, chans = inputs.shape
    tiles = cols // TILE
    most = tile_list.shape[1]
    rimmed = padded_2(inputs, (("sec", 1),), 1)
    padded_in = jnp.pad(rimmed, ((0, 0), (0, 0), (1, 1), (0, 0)))
    bias = biases[0]
    live = jnp.arange(most) < tile_count[0]
    select = (live[:, None] & (tile_list[0][:, None] == jnp.arange(tiles)[None, :])).astype(
        jnp.float32
    )
    pixel_mask = jnp.tile(jnp.repeat(jnp.sum(select, axis=0), TILE), rows)[:, None]
    wfull = lax.all_gather(weights[0], "sec", axis=0, tiled=True)
    flipped = wfull.reshape(9, chans, chans)[::-1]

    def work(upstream, padded_x, active, first_acc, second_acc):
        columns = patches(padded_x, rows, cols).reshape(-1, 9 * chans)
        pre = jnp.dot(columns, wfull, preferred_element_type=jnp.float32) + bias
        gpre = (silu_grad(pre, upstream.reshape(-1, chans)) * pixel_mask).astype(jnp.bfloat16)
        rim = padded_2(gpre.reshape(rows, cols, chans), (("sec", 0),), 1)
        gpad = jnp.pad(rim, ((0, 0), (1, 1), (0, 0)))
        gcols = patches(gpad, rows, cols).reshape(-1, 9, chans)
        back = (
            jnp.einsum("nkc,kdc->nd", gcols, flipped, preferred_element_type=jnp.float32)
            * pixel_mask
        )
        back = back.astype(jnp.bfloat16).reshape(rows, cols, chans)
        new_first = first_acc + outer_sum(columns, gpre)
        new_second = second_acc + jnp.sum(gpre.astype(jnp.float32), axis=0)
        first_acc = jnp.where(active, new_first, first_acc)
        second_acc = jnp.where(active, new_second, second_acc)
        return (back, first_acc, second_acc)

    def advance(step, carry):
        received, first_acc, second_acc, grads = carry
        slot = step - (n_section - 1 - section)
        active = (slot >= 0) & (slot < slots_n)
        slot_c = jnp.clip(slot, 0, slots_n - 1)
        image = lax.dynamic_index_in_dim(order, slot_c, 0, False)
        arriving = lax.dynamic_index_in_dim(cotangent, slot_c, 0, False)
        upstream = jnp.where(section == n_section - 1, arriving, received)
        padded_x = lax.dynamic_index_in_dim(padded_in, image, 0, False)
        back, first_acc, second_acc = work(upstream, padded_x, active, first_acc, second_acc)
        back = jnp.where(active, back, jnp.zeros_like(back))
        grads = jnp.where(active, lax.dynamic_update_index_in_dim(grads, back, image, 0), grads)
        received = from_behind(back, "section", -1)
        return (received, first_acc, second_acc, grads)

    accs = (jnp.zeros((9 * chans, chans), jnp.float32), jnp.zeros((chans,), jnp.float32))
    start = (
        jnp.zeros((rows, cols, chans), jnp.bfloat16),
        accs[0],
        accs[1],
        jnp.zeros((slots_n, rows, cols, chans), jnp.bfloat16),
    )
    received, first_acc, second_acc, grads = lax.fori_loop(
        0, slots_n + n_section - 1, advance, start
    )
    wpart, bpart = (
        lax.psum_scatter(first_acc, "sec", scatter_dimension=0, tiled=True),
        lax.psum_scatter(second_acc, "sec", scatter_dimension=0, tiled=True),
    )
    return (grads[None], wpart[None], bpart[None])


def solution(mesh):
    placed = (
        P("section", None, "sec", None, None),
        P("section", "sec", None),
        P("section", None),
        P(None, "sec", None, None),
        P("sec", None),
        P("sec"),
        P(),
    )
    return jax.shard_map(
        body,
        mesh=mesh,
        in_specs=placed,
        out_specs=(
            P("section", None, "sec", None, None),
            P("section", "sec", None),
            P("section", "sec"),
        ),
        check_vma=False,
    )
```

profile of v0, /device:TPU:24, one launch (start us, length us, event | category | flops | bytes accessed | tf_op | source)
XLA Modules:
  0.0 617.1 jit_solution(7965061102600201071)
XLA Ops:
  17.8 82.1 %all-gather.3.cloned.1.call-done = bf16[1,2304,256]{2,0,1:T(2,128)(2,1)} async-done(((bf16[1,36,256]{2,0,1:T(2,128)(2,1)}), bf16[1,2304,256]{2,0,1:T(2,128)(2,1)}) %all-gather.3.cloned.1.call-update) | async-done | bytes 1179664 | tf_op jit(solution)/shard_map/all_gather | solution.py:60
  102.9 2.9 copy.29
  106.5 212.5 %while.22 = (s32[]{:T(128)}, bf16[1,128,256]{2,1,0:T(8,128)(2,1)S(1)}, f32[2304,256]{1,0:T(8,128)S(1)}, f32[256]{0:T(256)S(1)}, bf16[2,1,128,256]{3,2,1,0:T(8,12...) while((s32[]{:T(128)}, ...), condition=%wide.region_3.4_spmd.clone, body=%wide.region_1.3_spmd.clone.sunk | while | flops 456575488 | bytes 14436786 | solution.py:103
  113.9 3.0 collective-permute-start.1
  123.7 5.1 collective-permute-done.2
  136.2 3.0 collective-permute-start.1
  145.4 5.4 collective-permute-done.2
  158.3 4.8 collective-permute-start.1
  169.2 5.4 collective-permute-done.2
  182.1 5.0 collective-permute-start.1
  193.3 5.4 collective-permute-done.2
  206.2 5.0 collective-permute-start.1
  217.3 5.4 collective-permute-done.2
  230.2 5.0 collective-permute-start.1
  241.4 5.4 collective-permute-done.2
  254.3 5.0 collective-permute-start.1
  265.4 5.4 collective-permute-done.2
  278.3 5.0 collective-permute-start.1
  289.5 5.4 collective-permute-done.2
  302.4 5.0 collective-permute-start.1
  313.5 5.4 collective-permute-done.2
  319.0 148.2 %fusion.2 = f32[40,256]{1,0:T(8,128)S(1)} fusion(f32[2304,256]{1,0:T(8,128)S(1)} %get-tuple-element.321), kind=kCustom, calls=%all-reduce-scatter | all-reduce-scatter fusion | flops 655361 | bytes 2402304
  473.0 5.7 collective-permute-start.6
  480.3 124.1 %all-reduce.3 = f32[256]{0:T(256)S(1)} all-reduce(f32[256]{0:T(256)S(1)} %get-tuple-element.322), channel_id=4, replica_groups=mesh['section'=8,'sec'=64] {'sec'}, use_global_device_ids=true, to_apply=%region_5.6.clone | all-reduce | flops 256 | bytes 2048
  (325 shorter events, 129.2 us)
Async XLA Ops:
  7.2 92.7 %all-gather.3.cloned.1.call-start = ((), (), s32[]{:S(2)}) async-start(), calls=%async_computation | async-start | bytes 2396160 | tf_op jit(solution)/shard_map/all_gather | solution.py:60
  121.2 7.5 %collective-permute-start.2 = (bf16[1,128,256]{2,1,0:T(8,128)(2,1)S(1)}, bf16[1,128,256]{2,1,0:T(8,128)(2,1)S(1)}, u32[]{:S(2)}, u32[]{:S(2)}) collective-permute-start(bf16[1,128,256]{2,1,0:T(8,128)(2,1)S(1)} %bitcast.89), channel_id=1, source_target_pairs={{64,0},{128,64},{192,128},{256,192},{320,256},{384,320},{448,384},... | collective-permute-start | bytes 196616 | tf_op jit(solution)/shard_map/while/body/eval_jaxpr/ppermute | solution.py:25
  143.5 7.4 %collective-permute-start.2 = (bf16[1,128,256]{2,1,0:T(8,128)(2,1)S(1)}, bf16[1,128,256]{2,1,0:T(8,128)(2,1)S(1)}, u32[]{:S(2)}, u32[]{:S(2)}) collective-permute-start(bf16[1,128,256]{2,1,0:T(8,128)(2,1)S(1)} %bitcast.89), channel_id=1, source_target_pairs={{64,0},{128,64},{192,128},{256,192},{320,256},{384,320},{448,384},... | collective-permute-start | bytes 196616 | tf_op jit(solution)/shard_map/while/body/eval_jaxpr/ppermute | solution.py:25
  157.0 7.3 %collective-permute-start = (bf16[1,128,256]{2,1,0:T(8,128)(2,1)S(1)}, bf16[1,128,256]{2,1,0:T(8,128)(2,1)S(1)}, u32[]{:S(2)}, u32[]{:S(2)}) collective-permute-start(bf16[1,128,256]{2,1,0:T(8,128)(2,1)S(1)} %bitcast.85), channel_id=1, source_target_pairs={{1,0},{2,1},{3,2},{4,3},{5,4},{6,5},{7,6},{8,7},{9,8},{10,9},{11,1... | collective-permute-start | bytes 196616 | tf_op jit(solution)/shard_map/while/body/eval_jaxpr/ppermute | solution.py:17
  167.3 7.4 %collective-permute-start.2 = (bf16[1,128,256]{2,1,0:T(8,128)(2,1)S(1)}, bf16[1,128,256]{2,1,0:T(8,128)(2,1)S(1)}, u32[]{:S(2)}, u32[]{:S(2)}) collective-permute-start(bf16[1,128,256]{2,1,0:T(8,128)(2,1)S(1)} %bitcast.89), channel_id=1, source_target_pairs={{64,0},{128,64},{192,128},{256,192},{320,256},{384,320},{448,384},... | collective-permute-start | bytes 196616 | tf_op jit(solution)/shard_map/while/body/eval_jaxpr/ppermute | solution.py:25
  180.8 7.5 %collective-permute-start = (bf16[1,128,256]{2,1,0:T(8,128)(2,1)S(1)}, bf16[1,128,256]{2,1,0:T(8,128)(2,1)S(1)}, u32[]{:S(2)}, u32[]{:S(2)}) collective-permute-start(bf16[1,128,256]{2,1,0:T(8,128)(2,1)S(1)} %bitcast.85), channel_id=1, source_target_pairs={{1,0},{2,1},{3,2},{4,3},{5,4},{6,5},{7,6},{8,7},{9,8},{10,9},{11,1... | collective-permute-start | bytes 196616 | tf_op jit(solution)/shard_map/while/body/eval_jaxpr/ppermute | solution.py:17
  182.1 6.2 %collective-permute-start.1 = (bf16[1,128,256]{2,1,0:T(8,128)(2,1)S(1)}, bf16[1,128,256]{2,1,0:T(8,128)(2,1)S(1)}, u32[]{:S(2)}, u32[]{:S(2)}) collective-permute-start(bf16[1,128,256]{2,1,0:T(8,128)(2,1)S(1)} %bitcast.86), channel_id=1, source_target_pairs={{0,1},{1,2},{2,3},{3,4},{4,5},{5,6},{6,7},{7,8},{8,9},{9,10},{10,1... | collective-permute-start | bytes 196616 | tf_op jit(solution)/shard_map/while/body/eval_jaxpr/ppermute | solution.py:16
  191.4 7.4 %collective-permute-start.2 = (bf16[1,128,256]{2,1,0:T(8,128)(2,1)S(1)}, bf16[1,128,256]{2,1,0:T(8,128)(2,1)S(1)}, u32[]{:S(2)}, u32[]{:S(2)}) collective-permute-start(bf16[1,128,256]{2,1,0:T(8,128)(2,1)S(1)} %bitcast.89), channel_id=1, source_target_pairs={{64,0},{128,64},{192,128},{256,192},{320,256},{384,320},{448,384},... | collective-permute-start | bytes 196616 | tf_op jit(solution)/shard_map/while/body/eval_jaxpr/ppermute | solution.py:25
  204.9 7.5 %collective-permute-start = (bf16[1,128,256]{2,1,0:T(8,128)(2,1)S(1)}, bf16[1,128,256]{2,1,0:T(8,128)(2,1)S(1)}, u32[]{:S(2)}, u32[]{:S(2)}) collective-permute-start(bf16[1,128,256]{2,1,0:T(8,128)(2,1)S(1)} %bitcast.85), channel_id=1, source_target_pairs={{1,0},{2,1},{3,2},{4,3},{5,4},{6,5},{7,6},{8,7},{9,8},{10,9},{11,1... | collective-permute-start | bytes 196616 | tf_op jit(solution)/shard_map/while/body/eval_jaxpr/ppermute | solution.py:17
  215.4 7.4 %collective-permute-start.2 = (bf16[1,128,256]{2,1,0:T(8,128)(2,1)S(1)}, bf16[1,128,256]{2,1,0:T(8,128)(2,1)S(1)}, u32[]{:S(2)}, u32[]{:S(2)}) collective-permute-start(bf16[1,128,256]{2,1,0:T(8,128)(2,1)S(1)} %bitcast.89), channel_id=1, source_target_pairs={{64,0},{128,64},{192,128},{256,192},{320,256},{384,320},{448,384},... | collective-permute-start | bytes 196616 | tf_op jit(solution)/shard_map/while/body/eval_jaxpr/ppermute | solution.py:25
  228.9 7.5 %collective-permute-start = (bf16[1,128,256]{2,1,0:T(8,128)(2,1)S(1)}, bf16[1,128,256]{2,1,0:T(8,128)(2,1)S(1)}, u32[]{:S(2)}, u32[]{:S(2)}) collective-permute-start(bf16[1,128,256]{2,1,0:T(8,128)(2,1)S(1)} %bitcast.85), channel_id=1, source_target_pairs={{1,0},{2,1},{3,2},{4,3},{5,4},{6,5},{7,6},{8,7},{9,8},{10,9},{11,1... | collective-permute-start | bytes 196616 | tf_op jit(solution)/shard_map/while/body/eval_jaxpr/ppermute | solution.py:17
  239.5 7.4 %collective-permute-start.2 = (bf16[1,128,256]{2,1,0:T(8,128)(2,1)S(1)}, bf16[1,128,256]{2,1,0:T(8,128)(2,1)S(1)}, u32[]{:S(2)}, u32[]{:S(2)}) collective-permute-start(bf16[1,128,256]{2,1,0:T(8,128)(2,1)S(1)} %bitcast.89), channel_id=1, source_target_pairs={{64,0},{128,64},{192,128},{256,192},{320,256},{384,320},{448,384},... | collective-permute-start | bytes 196616 | tf_op jit(solution)/shard_map/while/body/eval_jaxpr/ppermute | solution.py:25
  253.0 7.5 %collective-permute-start = (bf16[1,128,256]{2,1,0:T(8,128)(2,1)S(1)}, bf16[1,128,256]{2,1,0:T(8,128)(2,1)S(1)}, u32[]{:S(2)}, u32[]{:S(2)}) collective-permute-start(bf16[1,128,256]{2,1,0:T(8,128)(2,1)S(1)} %bitcast.85), channel_id=1, source_target_pairs={{1,0},{2,1},{3,2},{4,3},{5,4},{6,5},{7,6},{8,7},{9,8},{10,9},{11,1... | collective-permute-start | bytes 196616 | tf_op jit(solution)/shard_map/while/body/eval_jaxpr/ppermute | solution.py:17
  263.5 7.4 %collective-permute-start.2 = (bf16[1,128,256]{2,1,0:T(8,128)(2,1)S(1)}, bf16[1,128,256]{2,1,0:T(8,128)(2,1)S(1)}, u32[]{:S(2)}, u32[]{:S(2)}) collective-permute-start(bf16[1,128,256]{2,1,0:T(8,128)(2,1)S(1)} %bitcast.89), channel_id=1, source_target_pairs={{64,0},{128,64},{192,128},{256,192},{320,256},{384,320},{448,384},... | collective-permute-start | bytes 196616 | tf_op jit(solution)/shard_map/while/body/eval_jaxpr/ppermute | solution.py:25
  277.0 7.5 %collective-permute-start = (bf16[1,128,256]{2,1,0:T(8,128)(2,1)S(1)}, bf16[1,128,256]{2,1,0:T(8,128)(2,1)S(1)}, u32[]{:S(2)}, u32[]{:S(2)}) collective-permute-start(bf16[1,128,256]{2,1,0:T(8,128)(2,1)S(1)} %bitcast.85), channel_id=1, source_target_pairs={{1,0},{2,1},{3,2},{4,3},{5,4},{6,5},{7,6},{8,7},{9,8},{10,9},{11,1... | collective-permute-start | bytes 196616 | tf_op jit(solution)/shard_map/while/body/eval_jaxpr/ppermute | solution.py:17
  287.6 7.4 %collective-permute-start.2 = (bf16[1,128,256]{2,1,0:T(8,128)(2,1)S(1)}, bf16[1,128,256]{2,1,0:T(8,128)(2,1)S(1)}, u32[]{:S(2)}, u32[]{:S(2)}) collective-permute-start(bf16[1,128,256]{2,1,0:T(8,128)(2,1)S(1)} %bitcast.89), channel_id=1, source_target_pairs={{64,0},{128,64},{192,128},{256,192},{320,256},{384,320},{448,384},... | collective-permute-start | bytes 196616 | tf_op jit(solution)/shard_map/while/body/eval_jaxpr/ppermute | solution.py:25
  301.1 7.5 %collective-permute-start = (bf16[1,128,256]{2,1,0:T(8,128)(2,1)S(1)}, bf16[1,128,256]{2,1,0:T(8,128)(2,1)S(1)}, u32[]{:S(2)}, u32[]{:S(2)}) collective-permute-start(bf16[1,128,256]{2,1,0:T(8,128)(2,1)S(1)} %bitcast.85), channel_id=1, source_target_pairs={{1,0},{2,1},{3,2},{4,3},{5,4},{6,5},{7,6},{8,7},{9,8},{10,9},{11,1... | collective-permute-start | bytes 196616 | tf_op jit(solution)/shard_map/while/body/eval_jaxpr/ppermute | solution.py:17
  302.4 6.2 %collective-permute-start.1 = (bf16[1,128,256]{2,1,0:T(8,128)(2,1)S(1)}, bf16[1,128,256]{2,1,0:T(8,128)(2,1)S(1)}, u32[]{:S(2)}, u32[]{:S(2)}) collective-permute-start(bf16[1,128,256]{2,1,0:T(8,128)(2,1)S(1)} %bitcast.86), channel_id=1, source_target_pairs={{0,1},{1,2},{2,3},{3,4},{4,5},{5,6},{6,7},{7,8},{8,9},{9,10},{10,1... | collective-permute-start | bytes 196616 | tf_op jit(solution)/shard_map/while/body/eval_jaxpr/ppermute | solution.py:16
  311.6 7.4 %collective-permute-start.2 = (bf16[1,128,256]{2,1,0:T(8,128)(2,1)S(1)}, bf16[1,128,256]{2,1,0:T(8,128)(2,1)S(1)}, u32[]{:S(2)}, u32[]{:S(2)}) collective-permute-start(bf16[1,128,256]{2,1,0:T(8,128)(2,1)S(1)} %bitcast.89), channel_id=1, source_target_pairs={{64,0},{128,64},{192,128},{256,192},{320,256},{384,320},{448,384},... | collective-permute-start | bytes 196616 | tf_op jit(solution)/shard_map/while/body/eval_jaxpr/ppermute | solution.py:25
  467.2 138.5 %collective-permute-start.10 = (f32[40,256]{1,0:T(8,128)S(1)}, f32[40,256]{1,0:T(8,128)S(1)}, u32[]{:S(2)}, u32[]{:S(2)}) collective-permute-start(f32[40,256]{1,0:T(8,128)S(1)} %fusion.2), channel_id=1, source_target_pairs={{0,6},{1,7},{2,8},{3,9},{4,10},{5,11},{6,12},{7,13},{8,14},{9,15},... | collective-permute-start | bytes 122888
  468.5 135.9 %collective-permute-start.11 = (f32[12,256]{1,0:T(8,128)S(1)}, f32[12,256]{1,0:T(8,128)S(1)}, u32[]{:S(2)}, u32[]{:S(2)}) collective-permute-start(f32[12,256]{1,0:T(8,128)S(1)} %slice.192), channel_id=1, source_target_pairs={{0,7},{1,8},{2,9},{3,10},{4,11},{5,12},{6,13},{7,14},{8,15},{9,16}... | collective-permute-start | bytes 36872
  471.7 135.8 %collective-permute-start.5 = (f32[40,256]{1,0:T(8,128)S(1)}, f32[40,256]{1,0:T(8,128)S(1)}, u32[]{:S(2)}, u32[]{:S(2)}) collective-permute-start(f32[40,256]{1,0:T(8,128)S(1)} %fusion.2), channel_id=1, source_target_pairs={{0,1},{1,2},{2,3},{3,4},{4,5},{5,6},{6,7},{7,8},{8,9},{9,10},{10,1... | collective-permute-start | bytes 122888
  473.0 134.5 %collective-permute-start.6 = (f32[40,256]{1,0:T(8,128)S(1)}, f32[40,256]{1,0:T(8,128)S(1)}, u32[]{:S(2)}, u32[]{:S(2)}) collective-permute-start(f32[40,256]{1,0:T(8,128)S(1)} %fusion.2), channel_id=1, source_target_pairs={{0,2},{1,3},{2,4},{3,5},{4,6},{5,7},{6,8},{7,9},{8,10},{9,11},{10,... | collective-permute-start | bytes 122888
  478.8 128.8 %collective-permute-start.7 = (f32[40,256]{1,0:T(8,128)S(1)}, f32[40,256]{1,0:T(8,128)S(1)}, u32[]{:S(2)}, u32[]{:S(2)}) collective-permute-start(f32[40,256]{1,0:T(8,128)S(1)} %fusion.2), channel_id=1, source_target_pairs={{0,3},{1,4},{2,5},{3,6},{4,7},{5,8},{6,9},{7,10},{8,11},{9,12},{10... | collective-permute-start | bytes 122888
  (14 other events, 217.5 us)
Sparse Core Ops, SparseCore 0:
  11.8 88.0 all-gather.2
where the time goes:
time: 619 us; the launch traced here: 617 us
  blocking collectives  272 us (44%)
  waiting for transfers between devices  135 us (22%)
  starting transfers between devices  86.8 us (14%)
  matrix products  48 us (8%)
  local copies, waits for them, and re-layouts  36.6 us (6%)
  loops' own time  19.5 us (3%)
  between operations  16.2 us (3%)
    unnamed x2, blocking collectives  272 us
    all_gather x1, waiting for transfers between devices, body(): wfull = lax.all_gather(weights[0], 'sec', axis=0, tiled=True)  82.1 us
    ppermute x9, waiting for transfers between devices, from_behind(): return lax.ppermute(array, axis, pairs)  48.4 us
    ppermute x10, starting transfers between devices, padded_2(): before = lax.ppermute(last, axis, up)  42.4 us
    dot_general x9, matrix products, work(): jnp.einsum('nkc,kdc->nd', gcols, flipped, preferred_element_type=jnp.floa...  22.3 us
    another operation x1, loops' own time, body(): lax.fori_loop(0, slots_n + n_section - 1, advance, start)  19.5 us
    ppermute x9, starting transfers between devices, from_behind(): return lax.ppermute(array, axis, pairs)  17.7 us
    dot_general x9, matrix products, work(): pre = jnp.dot(columns, wfull, preferred_element_type=jnp.float32) + bias  15.1 us
  transfers between devices with their start and end apart: 37, of which 12 were waited for; matrix products, arithmetic and copies ran while one was open for 2% of the time, Pallas kernels for 0%

commit v1 on v0

v1 whole, which is shorter than its diff:
```python
import jax
import jax.numpy as jnp
from jax import lax
from jax.experimental import pallas as pl
from jax.experimental.pallas import tpu as pltpu
from jax.sharding import Mesh
from jax.sharding import PartitionSpec as P

TILE = 16
COLS = 128
CH = 256
PART = 36
WIN = 40
GROUPS = 32
BF = jnp.bfloat16
F32 = jnp.float32
VMEM = pl.BlockSpec(memory_space=pltpu.VMEM)
SMEM = pl.BlockSpec(memory_space=pltpu.SMEM)
ALL = ("y", "x", "z", "c")
SEC = ("x", "z", "c")


def call(kernel, ins, outs, operands, aliases=None, scratch=(), flops=1, moved=1):
    return pl.pallas_call(
        kernel,
        out_shape=outs,
        in_specs=ins,
        out_specs=[VMEM] * len(outs),
        scratch_shapes=scratch,
        input_output_aliases=aliases or {},
        compiler_params=pltpu.CompilerParams(vmem_limit_bytes=24 << 20),
        cost_estimate=pl.CostEstimate(flops=flops, bytes_accessed=moved, transcendentals=0),
    )(*operands)


def out(shape, dtype):
    return jax.ShapeDtypeStruct(shape, dtype)


def from_left(x):
    return jnp.concatenate([jnp.zeros_like(x[:1]), x[:-1]], axis=0)


def from_right(x):
    return jnp.concatenate([x[1:], jnp.zeros_like(x[:1])], axis=0)


def pack_kernel(tiles, count, order, x, cot, w, pack, mask, wide, gacc, grads):
    gacc[...] = jnp.zeros_like(gacc)
    grads[...] = jnp.zeros_like(grads)
    most = tiles.shape[1]
    for tile in range(COLS // TILE):
        live = jnp.int32(0)
        for k in range(most):
            live = live | ((tiles[0, k] == tile) & (k < count[0])).astype(jnp.int32)
        value = live.astype(F32)
        mask[tile * TILE : (tile + 1) * TILE, :] = jnp.full((TILE, CH), value, F32)
    on = mask[...]
    for slot in range(2):
        pack[slot] = x[order[slot]]
        pack[2 + slot] = (cot[slot].astype(F32) * on).astype(BF)
    core = lax.axis_index("c")
    rows = w[...].astype(F32)
    gap = jnp.zeros((WIN - PART, CH), F32)
    first = jnp.concatenate([rows, gap], axis=0)
    second = jnp.concatenate([gap, rows], axis=0)
    part = jnp.where(core == 0, first, second).astype(BF)
    for k in range(GROUPS):
        wide[k] = part


def prep_kernel(mine, other, bias, own, up1, down1, up2, down2, deriv, weights):
    core = lax.axis_index("c")

    def assemble(even, odd):
        for k in range(GROUPS):
            base = 72 * k
            weights[base : base + 32] = even[k, 0:32]
            both = even[k, 32:40].astype(F32) + odd[k, 0:8].astype(F32)
            weights[base + 32 : base + 40] = both.astype(BF)
            weights[base + 40 : base + 72] = odd[k, 8:40]

    @pl.when(core == 0)
    def _():
        assemble(mine, other)

    @pl.when(core == 1)
    def _():
        assemble(other, mine)

    shift = jnp.broadcast_to(bias[...], (COLS, CH))
    for slot in range(2):
        x = jnp.concatenate([up2[slot], up1[slot], own[slot], down1[slot], down2[slot]], axis=0)
        sums = []
        for b in range(3):
            total = None
            for a in range(3):
                tap = (3 * a + b) * CH
                term = jnp.dot(
                    x[a * COLS : (a + 3) * COLS],
                    weights[tap : tap + CH],
                    preferred_element_type=F32,
                )
                total = term if total is None else total + term
            sums.append(total)
        for r in range(3):
            rows = slice(r * COLS, (r + 1) * COLS)
            pre = from_left(sums[0][rows]) + sums[1][rows] + from_right(sums[2][rows]) + shift
            sig = jax.nn.sigmoid(pre)
            deriv[slot, r] = sig * (1.0 + pre * (1.0 - sig))


def step_kernel(step, sections, *refs):
    order, mask, deriv, weights = refs[:4]
    rest = refs[4:]
    if step <= 1:
        cots, rest = rest[:3], rest[3:]
    if step >= 1:
        got, rest = rest[:3], rest[3:]
    gacc_in, grads_in, back, gacc, grads = rest
    gacc[...] = gacc_in[...]
    grads[...] = grads_in[...]
    section = lax.axis_index("y")
    slot = step - (sections - 1 - section)

    @pl.when((slot >= 0) & (slot < 2))
    def _():
        gpre = []
        for r in range(3):
            if step == 0:
                upstream = cots[r][2]
            elif step == 1:
                upstream = jnp.where(section == sections - 1, cots[r][3], got[r][...])
            else:
                upstream = got[r][...]
            gpre.append((upstream.astype(F32) * deriv[slot, r]).astype(BF))
        gacc[slot] = gpre[1]
        sums = []
        for b in range(3):
            total = None
            for a in range(3):
                tap = (3 * a + b) * CH
                term = lax.dot_general(
                    gpre[2 - a],
                    weights[tap : tap + CH],
                    (((1,), (1,)), ((), ())),
                    preferred_element_type=F32,
                )
                total = term if total is None else total + term
            sums.append(total)
        value = from_right(sums[0]) + sums[1] + from_left(sums[2])
        value = (value * mask[...]).astype(BF)
        back[...] = value
        grads[order[slot]] = value


def wgrad_kernel(own, up, down, gacc, mine, theirs, total):
    core = lax.axis_index("c")
    g = [gacc[slot].astype(F32) for slot in range(2)]
    shifted = [
        jnp.concatenate([from_right(g[0]), from_right(g[1])], axis=0).astype(BF),
        jnp.concatenate([gacc[0], gacc[1]], axis=0),
        jnp.concatenate([from_left(g[0]), from_left(g[1])], axis=0).astype(BF),
    ]
    for a, rows in enumerate((up, own, down)):
        x = jnp.concatenate([rows[0], rows[1]], axis=0)
        for b in range(3):
            tap = (3 * a + b) * CH
            total[tap : tap + CH] = lax.dot_general(
                x, shifted[b], (((0,), (0,)), ((), ())), preferred_element_type=F32
            )
    bias = jnp.sum(g[0] + g[1], axis=0, keepdims=True)
    high = bias.astype(BF).astype(F32)
    low = (bias - high).astype(BF).astype(F32)
    row = lax.broadcasted_iota(jnp.int32, (WIN, CH), 0)

    def window(which, start):
        at = jnp.where(which == 0, PART, 0)
        return total[pl.ds(pl.multiple_of(start, 8), WIN), :], at

    for k in range(GROUPS):
        value, at = window(core, 72 * k + 32 * core)
        value = jnp.where(row == at, bias, value)
        mine[k] = jnp.where(row == at + 1, 0.0, value)
        value, at = window(1 - core, 72 * k + 32 * (1 - core))
        value = jnp.where(row == at, high, value)
        theirs[k] = jnp.where(row == at + 1, low, value).astype(BF)


def pair_kernel(mine, got, both):
    core = lax.axis_index("c")
    row = lax.broadcasted_iota(jnp.int32, (WIN, CH), 0)
    at = jnp.where(core == 0, PART, 0)
    lead = mine[0] + got[0].astype(F32)
    here = (row == at) | (row == at + 1)
    bias = jnp.sum(jnp.where(here, lead, 0.0), axis=0, keepdims=True)
    high = bias.astype(BF).astype(F32)
    low = bias - high
    for k in range(GROUPS):
        value = mine[k] + got[k].astype(F32)
        value = jnp.where(row == at, high, value)
        both[k] = jnp.where(row == at + 1, low, value).astype(BF)


def total_kernel(parts, wgrad, bgrad):
    core = lax.axis_index("c")
    me = (lax.axis_index("x") * lax.axis_size("z") + lax.axis_index("z")) * 2 + core
    value = parts[0].astype(F32)
    for k in range(1, GROUPS):
        value = value + parts[k].astype(F32)
    wgrad[...] = jnp.where(core == 0, value[:PART], value[WIN - PART :])
    row = lax.broadcasted_iota(jnp.int32, (WIN, CH), 0)
    at = jnp.where(core == 0, PART, 0)
    here = (row == at) | (row == at + 1)
    bias = jnp.sum(jnp.where(here, value, 0.0), axis=0, keepdims=True)
    lane = lax.broadcasted_iota(jnp.int32, (1, CH), 1)
    spot = lax.broadcasted_iota(jnp.int32, (1, 4), 1)
    result = jnp.zeros((1, 4), F32)
    for j in range(4):
        one = jnp.sum(jnp.where(lane == 4 * me + j, bias, 0.0), axis=1, keepdims=True)
        result = jnp.where(spot == j, one, result)
    bgrad[...] = result


def shift_pairs(size, by):
    return [(s, s + by) for s in range(size) if 0 <= s + by < size]


def hop_pairs(planes, size, by):
    return [
        (p * size + s, (p - 1) * size + s + by)
        for p in planes
        for s in range(size)
        if 0 <= s + by < size
    ]


def body(saved_inputs, weights, biases, cotangent, tile_list, tile_count, order):
    sections = lax.axis_size("y")
    size = 64
    image = (2, COLS, CH)
    inputs = saved_inputs.reshape(image)
    cot = cotangent.reshape(image)

    pack, mask, wide, gacc, grads = call(
        pack_kernel,
        [SMEM, SMEM, SMEM, VMEM, VMEM, VMEM],
        [out((4, COLS, CH), BF), out((COLS, CH), F32), out((GROUPS, WIN, CH), BF)]
        + [out(image, BF)] * 2,
        (tile_list, tile_count, order, inputs, cot, weights[0]),
        moved=3 << 20,
    )
    up1 = lax.ppermute(pack, SEC, shift_pairs(size, 1))
    down1 = lax.ppermute(pack, SEC, shift_pairs(size, -1))
    xs = pack[:2]
    up2 = lax.ppermute(xs, SEC, shift_pairs(size, 2))
    down2 = lax.ppermute(xs, SEC, shift_pairs(size, -2))

    swap = [(0, 1), (1, 0)]
    mine = lax.all_to_all(wide, ("x", "z"), 0, 0)
    other = lax.ppermute(mine, "c", swap)

    deriv, wfull = call(
        prep_kernel,
        [VMEM] * 8,
        [out((2, 3, COLS, CH), F32), out((9 * CH, CH), BF)],
        (mine, other, biases, pack, up1, down1, up2, down2),
        flops=1 << 30,
        moved=4 << 20,
    )

    got = None
    for step in range(sections + 1):
        operands = [order, mask, deriv, wfull]
        if step <= 1:
            operands += [up1, pack, down1]
        if step >= 1:
            operands += got
        count = len(operands)
        back, gacc, grads = call(
            lambda *refs, step=step: step_kernel(step, sections, *refs),
            [SMEM] + [VMEM] * (count + 1),
            [out((COLS, CH), BF), out(image, BF), out(image, BF)],
            (*operands, gacc, grads),
            aliases={count: 1, count + 1: 2},
            flops=1 << 27,
            moved=2 << 20,
        )
        if step < sections:
            planes = [p for p in (sections - 1 - step, sections - step) if 0 < p < sections]
            got = [
                lax.ppermute(back, ALL, hop_pairs(planes, size, by)) for by in (1, 0, -1)
            ]

    mine, theirs = call(
        wgrad_kernel,
        [VMEM] * 4,
        [out((GROUPS, WIN, CH), F32), out((GROUPS, WIN, CH), BF)],
        (pack, up1, down1, gacc),
        scratch=[pltpu.VMEM((9 * CH, CH), F32)],
        flops=1 << 28,
        moved=4 << 20,
    )
    received = lax.ppermute(theirs, "c", swap)
    (both,) = call(
        pair_kernel,
        [VMEM] * 2,
        [out((GROUPS, WIN, CH), BF)],
        (mine, received),
        moved=3 << 20,
    )
    parts = lax.all_to_all(both, ("x", "z"), 0, 0)
    wgrad, bgrad = call(
        total_kernel,
        [VMEM],
        [out((PART, CH), F32), out((1, 4), F32)],
        (parts,),
        moved=1 << 20,
    )
    return grads.reshape(1, 2, 1, COLS, CH), wgrad[None], bgrad


def solution(mesh):
    fine = Mesh(mesh.devices.reshape(8, 4, 8, 2), ALL)
    placed = (
        P("y", None, SEC, None, None),
        P("y", SEC, None),
        P("y", None),
        P(None, SEC, None, None),
        P(SEC, None),
        P(SEC),
        P(),
    )
    return jax.shard_map(
        body,
        mesh=fine,
        in_specs=placed,
        out_specs=(P("y", None, SEC, None, None), P("y", SEC, None), P("y", SEC)),
        check_vma=False,
    )
```

time: 619 us -> 190 us (0.31)
  the two profiles are of different devices: /device:TPU:24 before, /device:TPU:64 now
where the time goes in v1:
time: 190 us; the launch traced here: 189 us
  blocking collectives  73.7 us (39%)
  waiting for transfers between devices  54 us (28%)
  starting transfers between devices  35.4 us (19%)
  Pallas kernels  20.1 us (11%)
  local copies, waits for them, and re-layouts  4.51 us (2%)
    ppermute x24, waiting for transfers between devices, body(): lax.ppermute(back, ALL, hop_pairs(planes, size, by))  48 us
    all_to_all x1, blocking collectives, body(): parts = lax.all_to_all(both, ('x', 'z'), 0, 0)  41.1 us
    all_to_all x1, blocking collectives, body(): mine = lax.all_to_all(wide, ('x', 'z'), 0, 0)  32.6 us
    pallas_call x14, Pallas kernels, call(): pl.pallas_call(kernel, out_shape=outs, in_specs=ins, out_specs=[VMEM] * l...  20.1 us
    ppermute x24, starting transfers between devices, body(): lax.ppermute(back, ALL, hop_pairs(planes, size, by))  19.6 us
    unnamed x13, local copies, waits for them, and re-layouts  4.5 us
  transfers between devices with their start and end apart: 30, of which 6 were waited for; matrix products, arithmetic and copies ran while one was open for 0% of the time, Pallas kernels for 0%

profile of v1, /device:TPU:64, one launch (start us, length us, event | category | flops | bytes accessed | tf_op | source)
XLA Modules:
  0.0 189.5 jit_solution(15539165100226374306)
XLA Ops:
  6.4 32.6 %all_to_all.10.mine = bf16[32,40,256]{2,1,0:T(8,128)(2,1)S(1)} all-to-all(bf16[32,40,256]{2,1,0:T(8,128)(2,1)S(1)} %get-tuple-element.41), channel_id=1, replica_groups=mesh['y'=8,'x'=4,'z'=8,'c'=2] {'x','z'}, dimensions={0} | all-to-all | bytes 1310720 | tf_op jit(solution)/shard_map/all_to_all | solution.py:260
  39.1 1.9 %collective-permute-start = (bf16[32,40,256]{2,1,0:T(8,128)(2,1)S(1)}, bf16[32,40,256]{2,1,0:T(8,128)(2,1)S(1)}, u32[]{:S(2)}, u32[]{:S(2)}) collective-permute-start(bf16[32,40,256]{2,1,0:T(8,128)(2,1)S(1)} %all_to_all.10.mine), channel_id=1, source_target_pairs={{0,1},{1,0},{2,3},{3,2},{4,5},{5,4},{6,7},{7,6},{8,9},{9,8},{10,11... | collective-permute-start | bytes 1966088 | tf_op jit(solution)/shard_map/ppermute | solution.py:261
  41.0 2.4 %collective-permute-start.2 = (bf16[4,128,256]{2,1,0:T(8,128)(2,1)S(1)}, bf16[4,128,256]{2,1,0:T(8,128)(2,1)S(1)}, u32[]{:S(2)}, u32[]{:S(2)}) collective-permute-start(bf16[4,128,256]{2,1,0:T(8,128)(2,1)S(1)} %get-tuple-element.42.own.refs_5_), channel_id=1, source_target_pairs={{1,0},{2,1},{3,2},{4,3},{5,4},{6,5},{7,6},{8,7},{9,8},{10,9},{11,1... | collective-permute-start | bytes 786440 | tf_op jit(solution)/shard_map/ppermute | solution.py:254
  43.4 1.9 %collective-permute-start.1 = (bf16[4,128,256]{2,1,0:T(8,128)(2,1)S(1)}, bf16[4,128,256]{2,1,0:T(8,128)(2,1)S(1)}, u32[]{:S(2)}, u32[]{:S(2)}) collective-permute-start(bf16[4,128,256]{2,1,0:T(8,128)(2,1)S(1)} %get-tuple-element.42.own.refs_5_), channel_id=1, source_target_pairs={{0,1},{1,2},{2,3},{3,4},{4,5},{5,6},{6,7},{7,8},{8,9},{9,10},{10,1... | collective-permute-start | bytes 786440 | tf_op jit(solution)/shard_map/ppermute | solution.py:253
  45.4 2.3 %collective-permute-start.4 = (bf16[2,128,256]{2,1,0:T(8,128)(2,1)S(1)}, bf16[2,128,256]{2,1,0:T(8,128)(2,1)S(1)}, u32[]{:S(2)}, u32[]{:S(2)}) collective-permute-start(bf16[2,128,256]{2,1,0:T(8,128)(2,1)S(1)} %slice.3), channel_id=1, source_target_pairs={{2,0},{3,1},{4,2},{5,3},{6,4},{7,5},{8,6},{9,7},{10,8},{11,9},{12,... | collective-permute-start | bytes 393224 | tf_op jit(solution)/shard_map/ppermute | solution.py:257
  47.7 3.5 %collective-permute-start.3 = (bf16[2,128,256]{2,1,0:T(8,128)(2,1)S(1)}, bf16[2,128,256]{2,1,0:T(8,128)(2,1)S(1)}, u32[]{:S(2)}, u32[]{:S(2)}) collective-permute-start(bf16[2,128,256]{2,1,0:T(8,128)(2,1)S(1)} %slice.3), channel_id=1, source_target_pairs={{0,2},{1,3},{2,4},{3,5},{4,6},{5,7},{6,8},{7,9},{8,10},{9,11},{10,... | collective-permute-start | bytes 393224 | tf_op jit(solution)/shard_map/ppermute | solution.py:256
  51.2 1.7 collective-permute-done.4.down2
  52.9 2.6 %collective-permute-done.3.up2 = bf16[2,128,256]{2,1,0:T(8,128)(2,1)S(1)} collective-permute-done((bf16[2,128,256]{2,1,0:T(8,128)(2,1)S(1)}, bf16[2,128,256]{2,1,0:T(8,128)(2,1)S(1)}, u32[]{:S(2)}, u32[]{:S(2)}) %collective-permute-start.3) | collective-permute-done | bytes 131104 | tf_op jit(solution)/shard_map/ppermute | solution.py:256
  56.9 1.6 shard_map.96
  60.5 1.6 shard_map.97
  64.1 1.6 shard_map.98
  67.8 1.6 shard_map.99
  71.4 1.6 shard_map.100
  75.1 1.6 shard_map.101
  78.7 1.6 shard_map.102
  84.2 41.4 %collective-permute-done.25.refs_6_ = bf16[128,256]{1,0:T(8,128)(2,1)S(1)} collective-permute-done((bf16[128,256]{1,0:T(8,128)(2,1)S(1)}, bf16[128,256]{1,0:T(8,128)(2,1)S(1)}, u32[]{:S(2)}, u32[]{:S(2)}) %collective-permute-start.25) | collective-permute-done | bytes 65568 | tf_op jit(solution)/shard_map/ppermute | solution.py:292
  126.2 2.1 %shard_map.103 = (bf16[128,256]{1,0:T(8,128)(2,1)S(1)}, bf16[2,128,256]{2,1,0:T(8,128)(2,1)S(1)}, bf16[2,128,256]{2,1,0:T(8,128)(2,1)}) custom-call(s32[2]{0:T(128)S(1)} %copy-done.2, f32[128,256]{1,0:T(8,128)S(1)} %get-tuple-element.40.refs_1_, f32[2,3,128,256]{3,2,1,0:T(8,128)S(1)} %get-tuple-element.43.refs_2_, ...), custom_call_target="tpu_custom_call", output_to_operand_aliasing={{1}: (7, {}), {2}: (8, {})} | custom-call | flops 134217728 | bytes 2097152 | tf_op jit(solution)/shard_map/pallas_call | solution.py:24
  129.7 1.3 collective-permute-start.27
  131.0 1.3 collective-permute-start.26
  132.3 5.9 %collective-permute-done.28.refs_6_ = bf16[128,256]{1,0:T(8,128)(2,1)S(1)} collective-permute-done((bf16[128,256]{1,0:T(8,128)(2,1)S(1)}, bf16[128,256]{1,0:T(8,128)(2,1)S(1)}, u32[]{:S(2)}, u32[]{:S(2)}) %collective-permute-start.28) | collective-permute-done | bytes 65568 | tf_op jit(solution)/shard_map/ppermute | solution.py:292
  138.2 2.2 %shard_map.104 = (bf16[128,256]{1,0:T(8,128)(2,1)}, bf16[2,128,256]{2,1,0:T(8,128)(2,1)S(1)}, bf16[2,128,256]{2,1,0:T(8,128)(2,1)}) custom-call(s32[2]{0:T(128)S(1)} %copy-done.2, f32[128,256]{1,0:T(8,128)S(1)} %get-tuple-element.40.refs_1_, f32[2,3,128,256]{3,2,1,0:T(8,128)S(1)} %get-tuple-element.43.refs_2_, ...), custom_call_target="tpu_custom_call", output_to_operand_aliasing={{1}: (7, {}), {2}: (8, {})} | custom-call | flops 134217728 | bytes 2097152 | tf_op jit(solution)/shard_map/pallas_call | solution.py:24
  141.5 3.7 %collective-permute-start.29 = (bf16[32,40,256]{2,1,0:T(8,128)(2,1)S(1)}, bf16[32,40,256]{2,1,0:T(8,128)(2,1)S(1)}, u32[]{:S(2)}, u32[]{:S(2)}) collective-permute-start(bf16[32,40,256]{2,1,0:T(8,128)(2,1)S(1)} %get-tuple-element.74), channel_id=1, source_target_pairs={{0,1},{1,0},{2,3},{3,2},{4,5},{5,4},{6,7},{7,6},{8,9},{9,8},{10,11... | collective-permute-start | bytes 1966088 | tf_op jit(solution)/shard_map/ppermute | solution.py:304
  145.2 1.7 collective-permute-done.29.got
  147.1 41.1 %all_to_all.11.parts = bf16[32,40,256]{2,1,0:T(8,128)(2,1)S(1)} all-to-all(bf16[32,40,256]{2,1,0:T(8,128)(2,1)S(1)} %shard_map.106), channel_id=1, replica_groups=mesh['y'=8,'x'=4,'z'=8,'c'=2] {'x','z'}, dimensions={0} | all-to-all | bytes 1310720 | tf_op jit(solution)/shard_map/all_to_all | solution.py:312
  (66 shorter events, 26.8 us)
Async XLA Ops:
  39.1 16.5 %collective-permute-start = (bf16[32,40,256]{2,1,0:T(8,128)(2,1)S(1)}, bf16[32,40,256]{2,1,0:T(8,128)(2,1)S(1)}, u32[]{:S(2)}, u32[]{:S(2)}) collective-permute-start(bf16[32,40,256]{2,1,0:T(8,128)(2,1)S(1)} %all_to_all.10.mine), channel_id=1, source_target_pairs={{0,1},{1,0},{2,3},{3,2},{4,5},{5,4},{6,7},{7,6},{8,9},{9,8},{10,11... | collective-permute-start | bytes 1966088 | tf_op jit(solution)/shard_map/ppermute | solution.py:261
  41.0 14.6 %collective-permute-start.2 = (bf16[4,128,256]{2,1,0:T(8,128)(2,1)S(1)}, bf16[4,128,256]{2,1,0:T(8,128)(2,1)S(1)}, u32[]{:S(2)}, u32[]{:S(2)}) collective-permute-start(bf16[4,128,256]{2,1,0:T(8,128)(2,1)S(1)} %get-tuple-element.42.own.refs_5_), channel_id=1, source_target_pairs={{1,0},{2,1},{3,2},{4,3},{5,4},{6,5},{7,6},{8,7},{9,8},{10,9},{11,1... | collective-permute-start | bytes 786440 | tf_op jit(solution)/shard_map/ppermute | solution.py:254
  43.4 12.1 %collective-permute-start.1 = (bf16[4,128,256]{2,1,0:T(8,128)(2,1)S(1)}, bf16[4,128,256]{2,1,0:T(8,128)(2,1)S(1)}, u32[]{:S(2)}, u32[]{:S(2)}) collective-permute-start(bf16[4,128,256]{2,1,0:T(8,128)(2,1)S(1)} %get-tuple-element.42.own.refs_5_), channel_id=1, source_target_pairs={{0,1},{1,2},{2,3},{3,4},{4,5},{5,6},{6,7},{7,8},{8,9},{9,10},{10,1... | collective-permute-start | bytes 786440 | tf_op jit(solution)/shard_map/ppermute | solution.py:253
  45.4 7.6 %collective-permute-start.4 = (bf16[2,128,256]{2,1,0:T(8,128)(2,1)S(1)}, bf16[2,128,256]{2,1,0:T(8,128)(2,1)S(1)}, u32[]{:S(2)}, u32[]{:S(2)}) collective-permute-start(bf16[2,128,256]{2,1,0:T(8,128)(2,1)S(1)} %slice.3), channel_id=1, source_target_pairs={{2,0},{3,1},{4,2},{5,3},{6,4},{7,5},{8,6},{9,7},{10,8},{11,9},{12,... | collective-permute-start | bytes 393224 | tf_op jit(solution)/shard_map/ppermute | solution.py:257
  47.7 7.9 %collective-permute-start.3 = (bf16[2,128,256]{2,1,0:T(8,128)(2,1)S(1)}, bf16[2,128,256]{2,1,0:T(8,128)(2,1)S(1)}, u32[]{:S(2)}, u32[]{:S(2)}) collective-permute-start(bf16[2,128,256]{2,1,0:T(8,128)(2,1)S(1)} %slice.3), channel_id=1, source_target_pairs={{0,2},{1,3},{2,4},{3,5},{4,6},{5,7},{6,8},{7,9},{8,10},{9,11},{10,... | collective-permute-start | bytes 393224 | tf_op jit(solution)/shard_map/ppermute | solution.py:256
  58.5 2.0 %collective-permute-start.7 = (bf16[128,256]{1,0:T(8,128)(2,1)S(1)}, bf16[128,256]{1,0:T(8,128)(2,1)S(1)}, u32[]{:S(2)}, u32[]{:S(2)}) collective-permute-start(bf16[128,256]{1,0:T(8,128)(2,1)S(1)} %get-tuple-element.47), channel_id=1, source_target_pairs={{449,384},{450,385},{451,386},{452,387},{453,388},{454,389},{455,3... | collective-permute-start | bytes 196616 | tf_op jit(solution)/shard_map/ppermute | solution.py:292
  59.1 1.4 collective-permute-start.6
  62.1 2.0 %collective-permute-start.10 = (bf16[128,256]{1,0:T(8,128)(2,1)S(1)}, bf16[128,256]{1,0:T(8,128)(2,1)S(1)}, u32[]{:S(2)}, u32[]{:S(2)}) collective-permute-start(bf16[128,256]{1,0:T(8,128)(2,1)S(1)} %get-tuple-element.50), channel_id=1, source_target_pairs={{385,320},{386,321},{387,322},{388,323},{389,324},{390,325},{391,3... | collective-permute-start | bytes 196616 | tf_op jit(solution)/shard_map/ppermute | solution.py:292
  62.8 1.4 collective-permute-start.9
  65.8 2.0 %collective-permute-start.13 = (bf16[128,256]{1,0:T(8,128)(2,1)S(1)}, bf16[128,256]{1,0:T(8,128)(2,1)S(1)}, u32[]{:S(2)}, u32[]{:S(2)}) collective-permute-start(bf16[128,256]{1,0:T(8,128)(2,1)S(1)} %get-tuple-element.53), channel_id=1, source_target_pairs={{321,256},{322,257},{323,258},{324,259},{325,260},{326,261},{327,2... | collective-permute-start | bytes 196616 | tf_op jit(solution)/shard_map/ppermute | solution.py:292
  66.4 1.4 collective-permute-start.12
  69.4 2.0 %collective-permute-start.16 = (bf16[128,256]{1,0:T(8,128)(2,1)S(1)}, bf16[128,256]{1,0:T(8,128)(2,1)S(1)}, u32[]{:S(2)}, u32[]{:S(2)}) collective-permute-start(bf16[128,256]{1,0:T(8,128)(2,1)S(1)} %get-tuple-element.56), channel_id=1, source_target_pairs={{257,192},{258,193},{259,194},{260,195},{261,196},{262,197},{263,1... | collective-permute-start | bytes 196616 | tf_op jit(solution)/shard_map/ppermute | solution.py:292
  70.1 1.4 collective-permute-start.15
  73.0 2.0 %collective-permute-start.19 = (bf16[128,256]{1,0:T(8,128)(2,1)S(1)}, bf16[128,256]{1,0:T(8,128)(2,1)S(1)}, u32[]{:S(2)}, u32[]{:S(2)}) collective-permute-start(bf16[128,256]{1,0:T(8,128)(2,1)S(1)} %get-tuple-element.59), channel_id=1, source_target_pairs={{193,128},{194,129},{195,130},{196,131},{197,132},{198,133},{199,1... | collective-permute-start | bytes 196616 | tf_op jit(solution)/shard_map/ppermute | solution.py:292
  73.7 1.4 collective-permute-start.18
  76.7 2.0 %collective-permute-start.22 = (bf16[128,256]{1,0:T(8,128)(2,1)S(1)}, bf16[128,256]{1,0:T(8,128)(2,1)S(1)}, u32[]{:S(2)}, u32[]{:S(2)}) collective-permute-start(bf16[128,256]{1,0:T(8,128)(2,1)S(1)} %get-tuple-element.62), channel_id=1, source_target_pairs={{129,64},{130,65},{131,66},{132,67},{133,68},{134,69},{135,70},{13... | collective-permute-start | bytes 196616 | tf_op jit(solution)/shard_map/ppermute | solution.py:292
  77.4 1.4 collective-permute-start.21
  80.3 45.3 %collective-permute-start.25 = (bf16[128,256]{1,0:T(8,128)(2,1)S(1)}, bf16[128,256]{1,0:T(8,128)(2,1)S(1)}, u32[]{:S(2)}, u32[]{:S(2)}) collective-permute-start(bf16[128,256]{1,0:T(8,128)(2,1)S(1)} %get-tuple-element.65), channel_id=1, source_target_pairs={{65,0},{66,1},{67,2},{68,3},{69,4},{70,5},{71,6},{72,7},{73,8},{74... | collective-permute-start | bytes 196616 | tf_op jit(solution)/shard_map/ppermute | solution.py:292
  81.6 44.6 %collective-permute-start.24 = (bf16[128,256]{1,0:T(8,128)(2,1)S(1)}, bf16[128,256]{1,0:T(8,128)(2,1)S(1)}, u32[]{:S(2)}, u32[]{:S(2)}) collective-permute-start(bf16[128,256]{1,0:T(8,128)(2,1)S(1)} %get-tuple-element.65), channel_id=1, source_target_pairs={{64,0},{65,1},{66,2},{67,3},{68,4},{69,5},{70,6},{71,7},{72,8},{73... | collective-permute-start | bytes 196616 | tf_op jit(solution)/shard_map/ppermute | solution.py:292
  82.9 43.3 %collective-permute-start.23 = (bf16[128,256]{1,0:T(8,128)(2,1)S(1)}, bf16[128,256]{1,0:T(8,128)(2,1)S(1)}, u32[]{:S(2)}, u32[]{:S(2)}) collective-permute-start(bf16[128,256]{1,0:T(8,128)(2,1)S(1)} %get-tuple-element.65), channel_id=1, source_target_pairs={{64,1},{65,2},{66,3},{67,4},{68,5},{69,6},{70,7},{71,8},{72,9},{73... | collective-permute-start | bytes 196616 | tf_op jit(solution)/shard_map/ppermute | solution.py:292
  128.4 9.8 %collective-permute-start.28 = (bf16[128,256]{1,0:T(8,128)(2,1)S(1)}, bf16[128,256]{1,0:T(8,128)(2,1)S(1)}, u32[]{:S(2)}, u32[]{:S(2)}) collective-permute-start(bf16[128,256]{1,0:T(8,128)(2,1)S(1)} %get-tuple-element.68), channel_id=1, source_target_pairs={{65,0},{66,1},{67,2},{68,3},{69,4},{70,5},{71,6},{72,7},{73,8},{74... | collective-permute-start | bytes 196616 | tf_op jit(solution)/shard_map/ppermute | solution.py:292
  129.7 8.5 %collective-permute-start.27 = (bf16[128,256]{1,0:T(8,128)(2,1)S(1)}, bf16[128,256]{1,0:T(8,128)(2,1)S(1)}, u32[]{:S(2)}, u32[]{:S(2)}) collective-permute-start(bf16[128,256]{1,0:T(8,128)(2,1)S(1)} %get-tuple-element.68), channel_id=1, source_target_pairs={{64,0},{65,1},{66,2},{67,3},{68,4},{69,5},{70,6},{71,7},{72,8},{73... | collective-permute-start | bytes 196616 | tf_op jit(solution)/shard_map/ppermute | solution.py:292
  131.0 7.2 %collective-permute-start.26 = (bf16[128,256]{1,0:T(8,128)(2,1)S(1)}, bf16[128,256]{1,0:T(8,128)(2,1)S(1)}, u32[]{:S(2)}, u32[]{:S(2)}) collective-permute-start(bf16[128,256]{1,0:T(8,128)(2,1)S(1)} %get-tuple-element.68), channel_id=1, source_target_pairs={{64,1},{65,2},{66,3},{67,4},{68,5},{69,6},{70,7},{71,8},{72,9},{73... | collective-permute-start | bytes 196616 | tf_op jit(solution)/shard_map/ppermute | solution.py:292
  141.5 5.4 %collective-permute-start.29 = (bf16[32,40,256]{2,1,0:T(8,128)(2,1)S(1)}, bf16[32,40,256]{2,1,0:T(8,128)(2,1)S(1)}, u32[]{:S(2)}, u32[]{:S(2)}) collective-permute-start(bf16[32,40,256]{2,1,0:T(8,128)(2,1)S(1)} %get-tuple-element.74), channel_id=1, source_target_pairs={{0,1},{1,0},{2,3},{3,2},{4,5},{5,4},{6,7},{7,6},{8,9},{9,8},{10,11... | collective-permute-start | bytes 1966088 | tf_op jit(solution)/shard_map/ppermute | solution.py:304
  (12 other events, 63.0 us)

commit v2 on v1

--- a/solution.py
+++ b/solution.py
@@ -16,6 +16,8 @@
 F32 = jnp.float32
 VMEM = pl.BlockSpec(memory_space=pltpu.VMEM)
 SMEM = pl.BlockSpec(memory_space=pltpu.SMEM)
+HBM = pl.BlockSpec(memory_space=pltpu.HBM)
+ANY = pl.BlockSpec(memory_space=pl.ANY)
 ALL = ("y", "x", "z", "c")
 SEC = ("x", "z", "c")
 
@@ -45,28 +47,47 @@
     return jnp.concatenate([x[1:], jnp.zeros_like(x[:1])], axis=0)
 
 
-def pack_kernel(tiles, count, order, x, cot, w, pack, mask, wide, gacc, grads):
-    gacc[...] = jnp.zeros_like(gacc)
-    grads[...] = jnp.zeros_like(grads)
+def pack_kernel(order, count, tiles, x, cot, w, pack, xs, mask, part, state, cotv, wv, tv, sems):
+    copies = [
+        pltpu.make_async_copy(tiles, tv, sems.at[0]),
+        pltpu.make_async_copy(cot, cotv, sems.at[1]),
+        pltpu.make_async_copy(w, wv, sems.at[2]),
+    ]
+    for slot in range(2):
+        source = x.at[order[slot]]
+        copies.append(pltpu.make_async_copy(source, xs.at[slot], sems.at[3 + slot]))
+        copies.append(pltpu.make_async_copy(source, pack.at[slot], sems.at[5 + slot]))
+    for copy in copies:
+        copy.start()
+    state[...] = jnp.zeros_like(state)
+    copies[0].wait()
     most = tiles.shape[1]
     for tile in range(COLS // TILE):
         live = jnp.int32(0)
         for k in range(most):
-            live = live | ((tiles[0, k] == tile) & (k < count[0])).astype(jnp.int32)
+            live = live | ((tv[0, k] == tile) & (k < count[0])).astype(jnp.int32)
         value = live.astype(F32)
         mask[tile * TILE : (tile + 1) * TILE, :] = jnp.full((TILE, CH), value, F32)
+    copies[1].wait()
     on = mask[...]
     for slot in range(2):
-        pack[slot] = x[order[slot]]
-        pack[2 + slot] = (cot[slot].astype(F32) * on).astype(BF)
-    core = lax.axis_index("c")
-    rows = w[...].astype(F32)
+        pack[2 + slot] = (cotv[slot].astype(F32) * on).astype(BF)
+    copies[2].wait()
+    core = lax.axis_index("c")
+    rows = wv[...].astype(F32)
     gap = jnp.zeros((WIN - PART, CH), F32)
     first = jnp.concatenate([rows, gap], axis=0)
     second = jnp.concatenate([gap, rows], axis=0)
-    part = jnp.where(core == 0, first, second).astype(BF)
+    part[...] = jnp.where(core == 0, first, second).astype(BF)
+    for copy in copies[3:]:
+        copy.wait()
+
+
+def wide_kernel(part, *refs):
+    wide = refs[-1]
+    value = part[...]
     for k in range(GROUPS):
-        wide[k] = part
+        wide[k] = value
 
 
 def prep_kernel(mine, other, bias, own, up1, down1, up2, down2, deriv, weights):
@@ -111,15 +132,14 @@
 
 
 def step_kernel(step, sections, *refs):
-    order, mask, deriv, weights = refs[:4]
-    rest = refs[4:]
+    mask, deriv, weights = refs[:3]
+    rest = refs[3:]
     if step <= 1:
         cots, rest = rest[:3], rest[3:]
     if step >= 1:
         got, rest = rest[:3], rest[3:]
-    gacc_in, grads_in, back, gacc, grads = rest
-    gacc[...] = gacc_in[...]
-    grads[...] = grads_in[...]
+    state_in, back, state = rest
+    state[...] = state_in[...]
     section = lax.axis_index("y")
     slot = step - (sections - 1 - section)
 
@@ -134,7 +154,7 @@
             else:
                 upstream = got[r][...]
             gpre.append((upstream.astype(F32) * deriv[slot, r]).astype(BF))
-        gacc[slot] = gpre[1]
+        state[slot] = gpre[1]
         sums = []
         for b in range(3):
             total = None
@@ -151,7 +171,12 @@
         value = from_right(sums[0]) + sums[1] + from_left(sums[2])
         value = (value * mask[...]).astype(BF)
         back[...] = value
-        grads[order[slot]] = value
+        state[2 + slot] = value
+
+
+def grads_kernel(order, state, grads):
+    for slot in range(2):
+        grads[order[slot]] = state[2 + slot]
 
 
 def wgrad_kernel(own, up, down, gacc, mine, theirs, total):
@@ -242,19 +267,36 @@
     inputs = saved_inputs.reshape(image)
     cot = cotangent.reshape(image)
 
-    pack, mask, wide, gacc, grads = call(
+    pack, xs, mask, part, state = call(
         pack_kernel,
-        [SMEM, SMEM, SMEM, VMEM, VMEM, VMEM],
-        [out((4, COLS, CH), BF), out((COLS, CH), F32), out((GROUPS, WIN, CH), BF)]
-        + [out(image, BF)] * 2,
-        (tile_list, tile_count, order, inputs, cot, weights[0]),
+        [SMEM, SMEM] + [HBM] * 4,
+        [
+            out((4, COLS, CH), BF),
+            out(image, BF),
+            out((COLS, CH), F32),
+            out((WIN, CH), BF),
+            out((4, COLS, CH), BF),
+        ],
+        (order, tile_count, tile_list, inputs, cot, weights[0]),
+        scratch=[
+            pltpu.VMEM(image, BF),
+            pltpu.VMEM((PART, CH), BF),
+            pltpu.SMEM(tile_list.shape, jnp.int32),
+            pltpu.SemaphoreType.DMA((7,)),
+        ],
         moved=3 << 20,
     )
     up1 = lax.ppermute(pack, SEC, shift_pairs(size, 1))
     down1 = lax.ppermute(pack, SEC, shift_pairs(size, -1))
-    xs = pack[:2]
     up2 = lax.ppermute(xs, SEC, shift_pairs(size, 2))
     down2 = lax.ppermute(xs, SEC, shift_pairs(size, -2))
+    (wide,) = call(
+        wide_kernel,
+        [VMEM] + [ANY] * 4,
+        [out((GROUPS, WIN, CH), BF)],
+        (part, up1, down1, up2, down2),
+        moved=1 << 20,
+    )
 
     swap = [(0, 1), (1, 0)]
     mine = lax.all_to_all(wide, ("x", "z"), 0, 0)
@@ -271,18 +313,18 @@
 
     got = None
     for step in range(sections + 1):
-        operands = [order, mask, deriv, wfull]
+        operands = [mask, deriv, wfull]
         if step <= 1:
             operands += [up1, pack, down1]
         if step >= 1:
             operands += got
         count = len(operands)
-        back, gacc, grads = call(
+        back, state = call(
             lambda *refs, step=step: step_kernel(step, sections, *refs),
-            [SMEM] + [VMEM] * (count + 1),
-            [out((COLS, CH), BF), out(image, BF), out(image, BF)],
-            (*operands, gacc, grads),
-            aliases={count: 1, count + 1: 2},
+            [VMEM] * (count + 1),
+            [out((COLS, CH), BF), out((4, COLS, CH), BF)],
+            (*operands, state),
+            aliases={count: 1},
             flops=1 << 27,
             moved=2 << 20,
         )
@@ -296,12 +338,13 @@
         wgrad_kernel,
         [VMEM] * 4,
         [out((GROUPS, WIN, CH), F32), out((GROUPS, WIN, CH), BF)],
-        (pack, up1, down1, gacc),
+        (pack, up1, down1, state),
         scratch=[pltpu.VMEM((9 * CH, CH), F32)],
         flops=1 << 28,
         moved=4 << 20,
     )
     received = lax.ppermute(theirs, "c", swap)
+    (grads,) = call(grads_kernel, [SMEM, VMEM], [out(image, BF)], (order, state), moved=1 << 18)
     (both,) = call(
         pair_kernel,
         [VMEM] * 2,

time: 190 us -> 180 us (0.947)
  blocking collectives: 73.7 us -> 30.5 us
  starting transfers between devices: 35.4 us -> 57.8 us
  waiting for transfers between devices: 54 us -> 75.4 us
  Pallas kernels: 20.1 us -> 8.74 us
    all_to_all x1 -> x0, blocking collectives: 41.1 us -> none  [body(): parts = lax.all_to_all(both, ('x', 'z'), 0, 0)]
    all_to_all x0 -> x1, waiting for transfers between devices: none -> 19.4 us  [body(): parts = lax.all_to_all(both, ('x', 'z'), 0, 0)]
    all_to_all x0 -> x1, starting transfers between devices: none -> 18.2 us  [body(): parts = lax.all_to_all(both, ('x', 'z'), 0, 0)]
    pallas_call x14 -> x16, Pallas kernels: 20.1 us -> 8.74 us  [call(): pl.pallas_call(kernel, out_shape=outs, in_specs=ins, out_specs=[VMEM] * l...]
    ppermute x1, starting transfers between devices: 2.32 us -> 6.95 us  [body(): down2 = lax.ppermute(xs, SEC, shift_pairs(size, -2))]
    all_to_all x1, blocking collectives: 32.6 us -> 30.5 us  [body(): mine = lax.all_to_all(wide, ('x', 'z'), 0, 0)]
    unnamed x13 -> x15, local copies, waits for them, and re-layouts: 4.5 us -> 4.5 us
  transfers between devices with their start and end apart: 30 -> 31, of which waited for: 6 -> 8; matrix products, arithmetic and copies ran while one was open for 0% -> 0% of each run, Pallas kernels for 0% -> 1%
where the time goes in v2:
time: 180 us; the launch traced here: 179 us
  waiting for transfers between devices  75.4 us (42%)
  starting transfers between devices  57.8 us (32%)
  blocking collectives  30.5 us (17%)
  Pallas kernels  8.74 us (5%)
  local copies, waits for them, and re-layouts  4.5 us (2%)
    ppermute x24, waiting for transfers between devices, body(): lax.ppermute(back, ALL, hop_pairs(planes, size, by))  47.5 us
    all_to_all x1, blocking collectives, body(): mine = lax.all_to_all(wide, ('x', 'z'), 0, 0)  30.5 us
    ppermute x24, starting transfers between devices, body(): lax.ppermute(back, ALL, hop_pairs(planes, size, by))  19.7 us
    all_to_all x1, waiting for transfers between devices, body(): parts = lax.all_to_all(both, ('x', 'z'), 0, 0)  19.4 us
    all_to_all x1, starting transfers between devices, body(): parts = lax.all_to_all(both, ('x', 'z'), 0, 0)  18.2 us
    pallas_call x16, Pallas kernels, call(): pl.pallas_call(kernel, out_shape=outs, in_specs=ins, out_specs=[VMEM] * l...  8.74 us
    ppermute x1, starting transfers between devices, body(): down2 = lax.ppermute(xs, SEC, shift_pairs(size, -2))  6.95 us
    unnamed x15, local copies, waits for them, and re-layouts  4.5 us
  transfers between devices with their start and end apart: 31, of which 8 were waited for; matrix products, arithmetic and copies ran while one was open for 0% of the time, Pallas kernels for 1%

profile of v2, /device:TPU:64, one launch (start us, length us, event | category | flops | bytes accessed | tf_op | source)
XLA Modules:
  0.0 178.7 jit_solution(8886284418105449491)
XLA Ops:
  5.1 1.3 shard_map.94
  6.4 1.9 %collective-permute-start.1 = (bf16[4,128,256]{2,1,0:T(8,128)(2,1)S(1)}, bf16[4,128,256]{2,1,0:T(8,128)(2,1)S(1)}, u32[]{:S(2)}, u32[]{:S(2)}) collective-permute-start(bf16[4,128,256]{2,1,0:T(8,128)(2,1)S(1)} %get-tuple-element.33.own.refs_4_), channel_id=1, source_target_pairs={{1,0},{2,1},{3,2},{4,3},{5,4},{6,5},{7,6},{8,7},{9,8},{10,9},{11,1... | collective-permute-start | bytes 786440 | tf_op jit(solution)/shard_map/ppermute | solution.py:290
  8.3 2.4 %collective-permute-start = (bf16[4,128,256]{2,1,0:T(8,128)(2,1)S(1)}, bf16[4,128,256]{2,1,0:T(8,128)(2,1)S(1)}, u32[]{:S(2)}, u32[]{:S(2)}) collective-permute-start(bf16[4,128,256]{2,1,0:T(8,128)(2,1)S(1)} %get-tuple-element.33.own.refs_4_), channel_id=1, source_target_pairs={{0,1},{1,2},{2,3},{3,4},{4,5},{5,6},{6,7},{7,8},{8,9},{9,10},{10,1... | collective-permute-start | bytes 786440 | tf_op jit(solution)/shard_map/ppermute | solution.py:289
  10.8 6.9 %collective-permute-start.3 = (bf16[2,128,256]{2,1,0:T(8,128)(2,1)S(1)}, bf16[2,128,256]{2,1,0:T(8,128)(2,1)S(1)}, u32[]{:S(2)}, u32[]{:S(2)}) collective-permute-start(bf16[2,128,256]{2,1,0:T(8,128)(2,1)S(1)} %get-tuple-element.34), channel_id=1, source_target_pairs={{2,0},{3,1},{4,2},{5,3},{6,4},{7,5},{8,6},{9,7},{10,8},{11,9},{12,... | collective-permute-start | bytes 393224 | tf_op jit(solution)/shard_map/ppermute | solution.py:292
  17.7 1.9 %collective-permute-start.2 = (bf16[2,128,256]{2,1,0:T(8,128)(2,1)S(1)}, bf16[2,128,256]{2,1,0:T(8,128)(2,1)S(1)}, u32[]{:S(2)}, u32[]{:S(2)}) collective-permute-start(bf16[2,128,256]{2,1,0:T(8,128)(2,1)S(1)} %get-tuple-element.34), channel_id=1, source_target_pairs={{0,2},{1,3},{2,4},{3,5},{4,6},{5,7},{6,8},{7,9},{8,10},{9,11},{10,... | collective-permute-start | bytes 393224 | tf_op jit(solution)/shard_map/ppermute | solution.py:291
  20.6 4.1 %collective-permute-done.2.refs_2_.up2 = bf16[2,128,256]{2,1,0:T(8,128)(2,1)S(1)} collective-permute-done((bf16[2,128,256]{2,1,0:T(8,128)(2,1)S(1)}, bf16[2,128,256]{2,1,0:T(8,128)(2,1)S(1)}, u32[]{:S(2)}, u32[]{:S(2)}) %collective-permute-start.2) | collective-permute-done | bytes 131104 | tf_op jit(solution)/shard_map/ppermute | solution.py:291
  24.8 30.5 %all_to_all.10.mine = bf16[32,40,256]{2,1,0:T(8,128)(2,1)S(1)} all-to-all(bf16[32,40,256]{2,1,0:T(8,128)(2,1)S(1)} %shard_map.95), channel_id=1, replica_groups=mesh['y'=8,'x'=4,'z'=8,'c'=2] {'x','z'}, dimensions={0} | all-to-all | bytes 1310720 | tf_op jit(solution)/shard_map/all_to_all | solution.py:302
  55.3 2.7 %collective-permute-start.4 = (bf16[32,40,256]{2,1,0:T(8,128)(2,1)S(1)}, bf16[32,40,256]{2,1,0:T(8,128)(2,1)S(1)}, u32[]{:S(2)}, u32[]{:S(2)}) collective-permute-start(bf16[32,40,256]{2,1,0:T(8,128)(2,1)S(1)} %all_to_all.10.mine), channel_id=1, source_target_pairs={{0,1},{1,0},{2,3},{3,2},{4,5},{5,4},{6,7},{7,6},{8,9},{9,8},{10,11... | collective-permute-start | bytes 1966088 | tf_op jit(solution)/shard_map/ppermute | solution.py:303
  58.0 1.7 collective-permute-done.4.other
  59.7 1.3 shard_map.96
  73.7 1.3 collective-permute-start.25
  75.0 1.3 collective-permute-start.24
  76.2 1.3 collective-permute-start.23
  77.5 41.0 %collective-permute-done.25.refs_5_ = bf16[128,256]{1,0:T(8,128)(2,1)S(1)} collective-permute-done((bf16[128,256]{1,0:T(8,128)(2,1)S(1)}, bf16[128,256]{1,0:T(8,128)(2,1)S(1)}, u32[]{:S(2)}, u32[]{:S(2)}) %collective-permute-start.25) | collective-permute-done | bytes 65568 | tf_op jit(solution)/shard_map/ppermute | solution.py:334
  119.7 1.3 collective-permute-start.28
  121.0 1.3 collective-permute-start.27
  122.3 1.3 collective-permute-start.26
  123.6 5.8 %collective-permute-done.28.refs_5_ = bf16[128,256]{1,0:T(8,128)(2,1)S(1)} collective-permute-done((bf16[128,256]{1,0:T(8,128)(2,1)S(1)}, bf16[128,256]{1,0:T(8,128)(2,1)S(1)}, u32[]{:S(2)}, u32[]{:S(2)}) %collective-permute-start.28) | collective-permute-done | bytes 65568 | tf_op jit(solution)/shard_map/ppermute | solution.py:334
  129.5 1.2 shard_map.105
  131.8 4.0 %collective-permute-start.29 = (bf16[32,40,256]{2,1,0:T(8,128)(2,1)S(1)}, bf16[32,40,256]{2,1,0:T(8,128)(2,1)S(1)}, u32[]{:S(2)}, u32[]{:S(2)}) collective-permute-start(bf16[32,40,256]{2,1,0:T(8,128)(2,1)S(1)} %get-tuple-element.56), channel_id=1, source_target_pairs={{0,1},{1,0},{2,3},{3,2},{4,5},{5,4},{6,7},{7,6},{8,9},{9,8},{10,11... | collective-permute-start | bytes 1966088 | tf_op jit(solution)/shard_map/ppermute | solution.py:346
  135.8 1.7 collective-permute-done.29.got
  138.5 18.2 %all-to-all-start.1 = ((bf16[32,40,256]{2,1,0:T(8,128)(2,1)}), bf16[32,40,256]{2,1,0:T(8,128)(2,1)S(1)}, u32[]{:S(2)}, u32[]{:S(2)}) async-start(bf16[32,40,256]{2,1,0:T(8,128)(2,1)} %shard_map.108), calls=%async_computation.1 | async-start | bytes 1310720 | tf_op jit(solution)/shard_map/all_to_all | solution.py:355
  156.8 1.2 shard_map.106
  158.0 19.4 %all-to-all-done.1.parts = bf16[32,40,256]{2,1,0:T(8,128)(2,1)S(1)} async-done(((bf16[32,40,256]{2,1,0:T(8,128)(2,1)}), bf16[32,40,256]{2,1,0:T(8,128)(2,1)S(1)}, u32[]{:S(2)}, u32[]{:S(2)}) %all-to-all-start.1) | async-done | bytes 655392 | tf_op jit(solution)/shard_map/all_to_all | solution.py:355
  (70 shorter events, 21.9 us)
Async XLA Ops:
  6.4 18.3 %collective-permute-start.1 = (bf16[4,128,256]{2,1,0:T(8,128)(2,1)S(1)}, bf16[4,128,256]{2,1,0:T(8,128)(2,1)S(1)}, u32[]{:S(2)}, u32[]{:S(2)}) collective-permute-start(bf16[4,128,256]{2,1,0:T(8,128)(2,1)S(1)} %get-tuple-element.33.own.refs_4_), channel_id=1, source_target_pairs={{1,0},{2,1},{3,2},{4,3},{5,4},{6,5},{7,6},{8,7},{9,8},{10,9},{11,1... | collective-permute-start | bytes 786440 | tf_op jit(solution)/shard_map/ppermute | solution.py:290
  8.3 16.4 %collective-permute-start = (bf16[4,128,256]{2,1,0:T(8,128)(2,1)S(1)}, bf16[4,128,256]{2,1,0:T(8,128)(2,1)S(1)}, u32[]{:S(2)}, u32[]{:S(2)}) collective-permute-start(bf16[4,128,256]{2,1,0:T(8,128)(2,1)S(1)} %get-tuple-element.33.own.refs_4_), channel_id=1, source_target_pairs={{0,1},{1,2},{2,3},{3,4},{4,5},{5,6},{6,7},{7,8},{8,9},{9,10},{10,1... | collective-permute-start | bytes 786440 | tf_op jit(solution)/shard_map/ppermute | solution.py:289
  10.8 9.9 %collective-permute-start.3 = (bf16[2,128,256]{2,1,0:T(8,128)(2,1)S(1)}, bf16[2,128,256]{2,1,0:T(8,128)(2,1)S(1)}, u32[]{:S(2)}, u32[]{:S(2)}) collective-permute-start(bf16[2,128,256]{2,1,0:T(8,128)(2,1)S(1)} %get-tuple-element.34), channel_id=1, source_target_pairs={{2,0},{3,1},{4,2},{5,3},{6,4},{7,5},{8,6},{9,7},{10,8},{11,9},{12,... | collective-permute-start | bytes 393224 | tf_op jit(solution)/shard_map/ppermute | solution.py:292
  17.7 7.0 %collective-permute-start.2 = (bf16[2,128,256]{2,1,0:T(8,128)(2,1)S(1)}, bf16[2,128,256]{2,1,0:T(8,128)(2,1)S(1)}, u32[]{:S(2)}, u32[]{:S(2)}) collective-permute-start(bf16[2,128,256]{2,1,0:T(8,128)(2,1)S(1)} %get-tuple-element.34), channel_id=1, source_target_pairs={{0,2},{1,3},{2,4},{3,5},{4,6},{5,7},{6,8},{7,9},{8,10},{9,11},{10,... | collective-permute-start | bytes 393224 | tf_op jit(solution)/shard_map/ppermute | solution.py:291
  55.3 4.4 %collective-permute-start.4 = (bf16[32,40,256]{2,1,0:T(8,128)(2,1)S(1)}, bf16[32,40,256]{2,1,0:T(8,128)(2,1)S(1)}, u32[]{:S(2)}, u32[]{:S(2)}) collective-permute-start(bf16[32,40,256]{2,1,0:T(8,128)(2,1)S(1)} %all_to_all.10.mine), channel_id=1, source_target_pairs={{0,1},{1,0},{2,3},{3,2},{4,5},{5,4},{6,7},{7,6},{8,9},{9,8},{10,11... | collective-permute-start | bytes 1966088 | tf_op jit(solution)/shard_map/ppermute | solution.py:303
  61.0 2.0 %collective-permute-start.7 = (bf16[128,256]{1,0:T(8,128)(2,1)S(1)}, bf16[128,256]{1,0:T(8,128)(2,1)S(1)}, u32[]{:S(2)}, u32[]{:S(2)}) collective-permute-start(bf16[128,256]{1,0:T(8,128)(2,1)S(1)} %get-tuple-element.38), channel_id=1, source_target_pairs={{449,384},{450,385},{451,386},{452,387},{453,388},{454,389},{455,3... | collective-permute-start | bytes 196616 | tf_op jit(solution)/shard_map/ppermute | solution.py:334
  61.7 1.4 collective-permute-start.6
  63.1 2.0 %collective-permute-start.10 = (bf16[128,256]{1,0:T(8,128)(2,1)S(1)}, bf16[128,256]{1,0:T(8,128)(2,1)S(1)}, u32[]{:S(2)}, u32[]{:S(2)}) collective-permute-start(bf16[128,256]{1,0:T(8,128)(2,1)S(1)} %get-tuple-element.40), channel_id=1, source_target_pairs={{385,320},{386,321},{387,322},{388,323},{389,324},{390,325},{391,3... | collective-permute-start | bytes 196616 | tf_op jit(solution)/shard_map/ppermute | solution.py:334
  63.8 1.4 collective-permute-start.9
  65.2 2.0 %collective-permute-start.13 = (bf16[128,256]{1,0:T(8,128)(2,1)S(1)}, bf16[128,256]{1,0:T(8,128)(2,1)S(1)}, u32[]{:S(2)}, u32[]{:S(2)}) collective-permute-start(bf16[128,256]{1,0:T(8,128)(2,1)S(1)} %get-tuple-element.42), channel_id=1, source_target_pairs={{321,256},{322,257},{323,258},{324,259},{325,260},{326,261},{327,2... | collective-permute-start | bytes 196616 | tf_op jit(solution)/shard_map/ppermute | solution.py:334
  65.9 1.4 collective-permute-start.12
  67.3 2.0 %collective-permute-start.16 = (bf16[128,256]{1,0:T(8,128)(2,1)S(1)}, bf16[128,256]{1,0:T(8,128)(2,1)S(1)}, u32[]{:S(2)}, u32[]{:S(2)}) collective-permute-start(bf16[128,256]{1,0:T(8,128)(2,1)S(1)} %get-tuple-element.44), channel_id=1, source_target_pairs={{257,192},{258,193},{259,194},{260,195},{261,196},{262,197},{263,1... | collective-permute-start | bytes 196616 | tf_op jit(solution)/shard_map/ppermute | solution.py:334
  68.0 1.4 collective-permute-start.15
  69.4 2.0 %collective-permute-start.19 = (bf16[128,256]{1,0:T(8,128)(2,1)S(1)}, bf16[128,256]{1,0:T(8,128)(2,1)S(1)}, u32[]{:S(2)}, u32[]{:S(2)}) collective-permute-start(bf16[128,256]{1,0:T(8,128)(2,1)S(1)} %get-tuple-element.46), channel_id=1, source_target_pairs={{193,128},{194,129},{195,130},{196,131},{197,132},{198,133},{199,1... | collective-permute-start | bytes 196616 | tf_op jit(solution)/shard_map/ppermute | solution.py:334
  70.1 1.4 collective-permute-start.18
  71.5 2.0 %collective-permute-start.22 = (bf16[128,256]{1,0:T(8,128)(2,1)S(1)}, bf16[128,256]{1,0:T(8,128)(2,1)S(1)}, u32[]{:S(2)}, u32[]{:S(2)}) collective-permute-start(bf16[128,256]{1,0:T(8,128)(2,1)S(1)} %get-tuple-element.48), channel_id=1, source_target_pairs={{129,64},{130,65},{131,66},{132,67},{133,68},{134,69},{135,70},{13... | collective-permute-start | bytes 196616 | tf_op jit(solution)/shard_map/ppermute | solution.py:334
  73.7 44.9 %collective-permute-start.25 = (bf16[128,256]{1,0:T(8,128)(2,1)S(1)}, bf16[128,256]{1,0:T(8,128)(2,1)S(1)}, u32[]{:S(2)}, u32[]{:S(2)}) collective-permute-start(bf16[128,256]{1,0:T(8,128)(2,1)S(1)} %get-tuple-element.50), channel_id=1, source_target_pairs={{65,0},{66,1},{67,2},{68,3},{69,4},{70,5},{71,6},{72,7},{73,8},{74... | collective-permute-start | bytes 196616 | tf_op jit(solution)/shard_map/ppermute | solution.py:334
  75.0 44.2 %collective-permute-start.24 = (bf16[128,256]{1,0:T(8,128)(2,1)S(1)}, bf16[128,256]{1,0:T(8,128)(2,1)S(1)}, u32[]{:S(2)}, u32[]{:S(2)}) collective-permute-start(bf16[128,256]{1,0:T(8,128)(2,1)S(1)} %get-tuple-element.50), channel_id=1, source_target_pairs={{64,0},{65,1},{66,2},{67,3},{68,4},{69,5},{70,6},{71,7},{72,8},{73... | collective-permute-start | bytes 196616 | tf_op jit(solution)/shard_map/ppermute | solution.py:334
  76.2 42.9 %collective-permute-start.23 = (bf16[128,256]{1,0:T(8,128)(2,1)S(1)}, bf16[128,256]{1,0:T(8,128)(2,1)S(1)}, u32[]{:S(2)}, u32[]{:S(2)}) collective-permute-start(bf16[128,256]{1,0:T(8,128)(2,1)S(1)} %get-tuple-element.50), channel_id=1, source_target_pairs={{64,1},{65,2},{66,3},{67,4},{68,5},{69,6},{70,7},{71,8},{72,9},{73... | collective-permute-start | bytes 196616 | tf_op jit(solution)/shard_map/ppermute | solution.py:334
  119.7 9.7 %collective-permute-start.28 = (bf16[128,256]{1,0:T(8,128)(2,1)S(1)}, bf16[128,256]{1,0:T(8,128)(2,1)S(1)}, u32[]{:S(2)}, u32[]{:S(2)}) collective-permute-start(bf16[128,256]{1,0:T(8,128)(2,1)S(1)} %get-tuple-element.52), channel_id=1, source_target_pairs={{65,0},{66,1},{67,2},{68,3},{69,4},{70,5},{71,6},{72,7},{73,8},{74... | collective-permute-start | bytes 196616 | tf_op jit(solution)/shard_map/ppermute | solution.py:334
  121.0 8.5 %collective-permute-start.27 = (bf16[128,256]{1,0:T(8,128)(2,1)S(1)}, bf16[128,256]{1,0:T(8,128)(2,1)S(1)}, u32[]{:S(2)}, u32[]{:S(2)}) collective-permute-start(bf16[128,256]{1,0:T(8,128)(2,1)S(1)} %get-tuple-element.52), channel_id=1, source_target_pairs={{64,0},{65,1},{66,2},{67,3},{68,4},{69,5},{70,6},{71,7},{72,8},{73... | collective-permute-start | bytes 196616 | tf_op jit(solution)/shard_map/ppermute | solution.py:334
  122.3 7.2 %collective-permute-start.26 = (bf16[128,256]{1,0:T(8,128)(2,1)S(1)}, bf16[128,256]{1,0:T(8,128)(2,1)S(1)}, u32[]{:S(2)}, u32[]{:S(2)}) collective-permute-start(bf16[128,256]{1,0:T(8,128)(2,1)S(1)} %get-tuple-element.52), channel_id=1, source_target_pairs={{64,1},{65,2},{66,3},{67,4},{68,5},{69,6},{70,7},{71,8},{72,9},{73... | collective-permute-start | bytes 196616 | tf_op jit(solution)/shard_map/ppermute | solution.py:334
  131.8 5.7 %collective-permute-start.29 = (bf16[32,40,256]{2,1,0:T(8,128)(2,1)S(1)}, bf16[32,40,256]{2,1,0:T(8,128)(2,1)S(1)}, u32[]{:S(2)}, u32[]{:S(2)}) collective-permute-start(bf16[32,40,256]{2,1,0:T(8,128)(2,1)S(1)} %get-tuple-element.56), channel_id=1, source_target_pairs={{0,1},{1,0},{2,3},{3,2},{4,5},{5,4},{6,7},{7,6},{8,9},{9,8},{10,11... | collective-permute-start | bytes 1966088 | tf_op jit(solution)/shard_map/ppermute | solution.py:346
  138.5 38.8 %all-to-all-start.1 = ((bf16[32,40,256]{2,1,0:T(8,128)(2,1)}), bf16[32,40,256]{2,1,0:T(8,128)(2,1)S(1)}, u32[]{:S(2)}, u32[]{:S(2)}) async-start(bf16[32,40,256]{2,1,0:T(8,128)(2,1)} %shard_map.108), calls=%async_computation.1 | async-start | bytes 1310720 | tf_op jit(solution)/shard_map/all_to_all | solution.py:355
  (14 other events, 62.6 us)

commit v3 on v2

--- a/solution.py
+++ b/solution.py
@@ -47,47 +47,32 @@
     return jnp.concatenate([x[1:], jnp.zeros_like(x[:1])], axis=0)
 
 
-def pack_kernel(order, count, tiles, x, cot, w, pack, xs, mask, part, state, cotv, wv, tv, sems):
-    copies = [
-        pltpu.make_async_copy(tiles, tv, sems.at[0]),
-        pltpu.make_async_copy(cot, cotv, sems.at[1]),
-        pltpu.make_async_copy(w, wv, sems.at[2]),
-    ]
-    for slot in range(2):
-        source = x.at[order[slot]]
-        copies.append(pltpu.make_async_copy(source, xs.at[slot], sems.at[3 + slot]))
-        copies.append(pltpu.make_async_copy(source, pack.at[slot], sems.at[5 + slot]))
-    for copy in copies:
-        copy.start()
+def wide_kernel(w, wide):
+    core = lax.axis_index("c")
+    rows = w[...].astype(F32)
+    gap = jnp.zeros((WIN - PART, CH), F32)
+    first = jnp.concatenate([rows, gap], axis=0)
+    second = jnp.concatenate([gap, rows], axis=0)
+    part = jnp.where(core == 0, first, second).astype(BF)
+    for k in range(GROUPS):
+        wide[k] = part
+
+
+def pack_kernel(order, count, tiles, x, cot, pack, xs, mask, state):
     state[...] = jnp.zeros_like(state)
-    copies[0].wait()
     most = tiles.shape[1]
     for tile in range(COLS // TILE):
         live = jnp.int32(0)
         for k in range(most):
-            live = live | ((tv[0, k] == tile) & (k < count[0])).astype(jnp.int32)
+            live = live | ((tiles[0, k] == tile) & (k < count[0])).astype(jnp.int32)
         value = live.astype(F32)
         mask[tile * TILE : (tile + 1) * TILE, :] = jnp.full((TILE, CH), value, F32)
-    copies[1].wait()
     on = mask[...]
     for slot in range(2):
-        pack[2 + slot] = (cotv[slot].astype(F32) * on).astype(BF)
-    copies[2].wait()
-    core = lax.axis_index("c")
-    rows = wv[...].astype(F32)
-    gap = jnp.zeros((WIN - PART, CH), F32)
-    first = jnp.concatenate([rows, gap], axis=0)
-    second = jnp.concatenate([gap, rows], axis=0)
-    part[...] = jnp.where(core == 0, first, second).astype(BF)
-    for copy in copies[3:]:
-        copy.wait()
-
-
-def wide_kernel(part, *refs):
-    wide = refs[-1]
-    value = part[...]
-    for k in range(GROUPS):
-        wide[k] = value
+        image = x[order[slot]]
+        xs[slot] = image
+        pack[slot] = image
+        pack[2 + slot] = (cot[slot].astype(F32) * on).astype(BF)
 
 
 def prep_kernel(mine, other, bias, own, up1, down1, up2, down2, deriv, weights):
@@ -267,39 +252,30 @@
     inputs = saved_inputs.reshape(image)
     cot = cotangent.reshape(image)
 
-    pack, xs, mask, part, state = call(
+    (wide,) = call(
+        wide_kernel, [VMEM], [out((GROUPS, WIN, CH), BF)], (weights[0],), moved=1 << 20
+    )
+    swap = [(0, 1), (1, 0)]
+    mine = lax.all_to_all(wide, ("x", "z"), 0, 0)
+
+    pack, xs, mask, state = call(
         pack_kernel,
-        [SMEM, SMEM] + [HBM] * 4,
+        [SMEM] * 3 + [VMEM] * 2,
         [
             out((4, COLS, CH), BF),
             out(image, BF),
             out((COLS, CH), F32),
-            out((WIN, CH), BF),
             out((4, COLS, CH), BF),
         ],
-        (order, tile_count, tile_list, inputs, cot, weights[0]),
-        scratch=[
-            pltpu.VMEM(image, BF),
-            pltpu.VMEM((PART, CH), BF),
-            pltpu.SMEM(tile_list.shape, jnp.int32),
-            pltpu.SemaphoreType.DMA((7,)),
-        ],
+        (order, tile_count, tile_list, inputs, cot),
+        flops=1 << 28,
         moved=3 << 20,
     )
     up1 = lax.ppermute(pack, SEC, shift_pairs(size, 1))
     down1 = lax.ppermute(pack, SEC, shift_pairs(size, -1))
     up2 = lax.ppermute(xs, SEC, shift_pairs(size, 2))
     down2 = lax.ppermute(xs, SEC, shift_pairs(size, -2))
-    (wide,) = call(
-        wide_kernel,
-        [VMEM] + [ANY] * 4,
-        [out((GROUPS, WIN, CH), BF)],
-        (part, up1, down1, up2, down2),
-        moved=1 << 20,
-    )
-
-    swap = [(0, 1), (1, 0)]
-    mine = lax.all_to_all(wide, ("x", "z"), 0, 0)
+    mine, up1, down1, up2, down2 = lax.optimization_barrier((mine, up1, down1, up2, down2))
     other = lax.ppermute(mine, "c", swap)
 
     deriv, wfull = call(

time: 180 us -> 162 us (0.900)
  blocking collectives: 30.5 us -> 0 us
  starting transfers between devices: 57.8 us -> 66.7 us
  waiting for transfers between devices: 75.4 us -> 82.3 us
  local copies, waits for them, and re-layouts: 4.5 us -> 1.41 us
    all_to_all x1 -> x0, blocking collectives: 30.5 us -> none  [body(): mine = lax.all_to_all(wide, ('x', 'z'), 0, 0)]
    all_to_all x0 -> x1, starting transfers between devices: none -> 12.7 us  [body(): mine = lax.all_to_all(wide, ('x', 'z'), 0, 0)]
    ppermute x1, waiting for transfers between devices: 0.97 us -> 9.89 us  [body(): down2 = lax.ppermute(xs, SEC, shift_pairs(size, -2))]
    ppermute x1, starting transfers between devices: 6.95 us -> 2.16 us  [body(): down2 = lax.ppermute(xs, SEC, shift_pairs(size, -2))]
    ppermute x1, waiting for transfers between devices: 4.12 us -> 0.01 us  [body(): up2 = lax.ppermute(xs, SEC, shift_pairs(size, 2))]
    unnamed x15 -> x13, local copies, waits for them, and re-layouts: 4.5 us -> 1.41 us
  transfers between devices with their start and end apart: 31 -> 32, of which waited for: 8 -> 7; matrix products, arithmetic and copies ran while one was open for 0% -> 0% of each run, Pallas kernels for 1% -> 1%
where the time goes in v3:
time: 162 us; the launch traced here: 161 us
  waiting for transfers between devices  82.3 us (51%)
  starting transfers between devices  66.7 us (41%)
  Pallas kernels  8.97 us (6%)
  between operations  1.83 us (1%)
    ppermute x24, waiting for transfers between devices, body(): lax.ppermute(back, ALL, hop_pairs(planes, size, by))  49.2 us
    ppermute x24, starting transfers between devices, body(): lax.ppermute(back, ALL, hop_pairs(planes, size, by))  19.7 us
    all_to_all x1, waiting for transfers between devices, body(): parts = lax.all_to_all(both, ('x', 'z'), 0, 0)  19.4 us
    all_to_all x1, starting transfers between devices, body(): parts = lax.all_to_all(both, ('x', 'z'), 0, 0)  17.9 us
    all_to_all x1, starting transfers between devices, body(): mine = lax.all_to_all(wide, ('x', 'z'), 0, 0)  12.7 us
    ppermute x1, waiting for transfers between devices, body(): down2 = lax.ppermute(xs, SEC, shift_pairs(size, -2))  9.89 us
    pallas_call x16, Pallas kernels, call(): pl.pallas_call(kernel, out_shape=outs, in_specs=ins, out_specs=[VMEM] * l...  8.97 us
    ppermute x1, starting transfers between devices, body(): received = lax.ppermute(theirs, 'c', swap)  4.26 us
  transfers between devices with their start and end apart: 32, of which 7 were waited for; matrix products, arithmetic and copies ran while one was open for 0% of the time, Pallas kernels for 1%

profile of v3, /device:TPU:64, one launch (start us, length us, event | category | flops | bytes accessed | tf_op | source)
XLA Modules:
  0.0 161.2 jit_solution(8936688712377075389)
XLA Ops:
  2.3 12.7 %all-to-all-start = ((bf16[32,40,256]{2,1,0:T(8,128)(2,1)}), bf16[32,40,256]{2,1,0:T(8,128)(2,1)S(1)}, u32[]{:S(2)}, u32[]{:S(2)}) async-start(bf16[32,40,256]{2,1,0:T(8,128)(2,1)} %shard_map.95), calls=%async_computation | async-start | bytes 1310720 | tf_op jit(solution)/shard_map/all_to_all | solution.py:259
  16.4 1.9 %collective-permute-start.1 = (bf16[4,128,256]{2,1,0:T(8,128)(2,1)S(1)}, bf16[4,128,256]{2,1,0:T(8,128)(2,1)S(1)}, u32[]{:S(2)}, u32[]{:S(2)}) collective-permute-start(bf16[4,128,256]{2,1,0:T(8,128)(2,1)S(1)} %get-tuple-element.36.own.refs_4_), channel_id=1, source_target_pairs={{1,0},{2,1},{3,2},{4,3},{5,4},{6,5},{7,6},{8,7},{9,8},{10,9},{11,1... | collective-permute-start | bytes 786440 | tf_op jit(solution)/shard_map/ppermute | solution.py:275
  18.3 2.4 %collective-permute-start = (bf16[4,128,256]{2,1,0:T(8,128)(2,1)S(1)}, bf16[4,128,256]{2,1,0:T(8,128)(2,1)S(1)}, u32[]{:S(2)}, u32[]{:S(2)}) collective-permute-start(bf16[4,128,256]{2,1,0:T(8,128)(2,1)S(1)} %get-tuple-element.36.own.refs_4_), channel_id=1, source_target_pairs={{0,1},{1,2},{2,3},{3,4},{4,5},{5,6},{6,7},{7,8},{8,9},{9,10},{10,1... | collective-permute-start | bytes 786440 | tf_op jit(solution)/shard_map/ppermute | solution.py:274
  20.7 2.2 %collective-permute-start.3 = (bf16[2,128,256]{2,1,0:T(8,128)(2,1)S(1)}, bf16[2,128,256]{2,1,0:T(8,128)(2,1)S(1)}, u32[]{:S(2)}, u32[]{:S(2)}) collective-permute-start(bf16[2,128,256]{2,1,0:T(8,128)(2,1)S(1)} %get-tuple-element.37), channel_id=1, source_target_pairs={{2,0},{3,1},{4,2},{5,3},{6,4},{7,5},{8,6},{9,7},{10,8},{11,9},{12,... | collective-permute-start | bytes 393224 | tf_op jit(solution)/shard_map/ppermute | solution.py:277
  22.9 3.7 %collective-permute-start.2 = (bf16[2,128,256]{2,1,0:T(8,128)(2,1)S(1)}, bf16[2,128,256]{2,1,0:T(8,128)(2,1)S(1)}, u32[]{:S(2)}, u32[]{:S(2)}) collective-permute-start(bf16[2,128,256]{2,1,0:T(8,128)(2,1)S(1)} %get-tuple-element.37), channel_id=1, source_target_pairs={{0,2},{1,3},{2,4},{3,5},{4,6},{5,7},{6,8},{7,9},{8,10},{9,11},{10,... | collective-permute-start | bytes 393224 | tf_op jit(solution)/shard_map/ppermute | solution.py:276
  26.6 9.9 %collective-permute-done.3.down2 = bf16[2,128,256]{2,1,0:T(8,128)(2,1)S(1)} collective-permute-done((bf16[2,128,256]{2,1,0:T(8,128)(2,1)S(1)}, bf16[2,128,256]{2,1,0:T(8,128)(2,1)S(1)}, u32[]{:S(2)}, u32[]{:S(2)}) %collective-permute-start.3) | collective-permute-done | bytes 131104 | tf_op jit(solution)/shard_map/ppermute | solution.py:277
  36.5 1.9 %collective-permute-start.4 = (bf16[32,40,256]{2,1,0:T(8,128)(2,1)S(1)}, bf16[32,40,256]{2,1,0:T(8,128)(2,1)S(1)}, u32[]{:S(2)}, u32[]{:S(2)}) collective-permute-start(bf16[32,40,256]{2,1,0:T(8,128)(2,1)S(1)} %all-to-all-done.mine), channel_id=1, source_target_pairs={{0,1},{1,0},{2,3},{3,2},{4,5},{5,4},{6,7},{7,6},{8,9},{9,8},{10,11... | collective-permute-start | bytes 1966088 | tf_op jit(solution)/shard_map/ppermute | solution.py:279
  38.4 2.1 %collective-permute-done.4.other = bf16[32,40,256]{2,1,0:T(8,128)(2,1)S(1)} collective-permute-done((bf16[32,40,256]{2,1,0:T(8,128)(2,1)S(1)}, bf16[32,40,256]{2,1,0:T(8,128)(2,1)S(1)}, u32[]{:S(2)}, u32[]{:S(2)}) %collective-permute-start.4) | collective-permute-done | bytes 655392 | tf_op jit(solution)/shard_map/ppermute | solution.py:279
  40.5 1.2 shard_map.96
  54.4 1.3 collective-permute-start.25
  55.7 1.3 collective-permute-start.24
  57.0 1.3 collective-permute-start.23
  58.3 42.5 %collective-permute-done.25.refs_5_ = bf16[128,256]{1,0:T(8,128)(2,1)S(1)} collective-permute-done((bf16[128,256]{1,0:T(8,128)(2,1)S(1)}, bf16[128,256]{1,0:T(8,128)(2,1)S(1)}, u32[]{:S(2)}, u32[]{:S(2)}) %collective-permute-start.25) | collective-permute-done | bytes 65568 | tf_op jit(solution)/shard_map/ppermute | solution.py:310
  102.1 1.3 collective-permute-start.28
  103.4 1.3 collective-permute-start.27
  104.7 1.3 collective-permute-start.26
  106.0 6.0 %collective-permute-done.28.refs_5_ = bf16[128,256]{1,0:T(8,128)(2,1)S(1)} collective-permute-done((bf16[128,256]{1,0:T(8,128)(2,1)S(1)}, bf16[128,256]{1,0:T(8,128)(2,1)S(1)}, u32[]{:S(2)}, u32[]{:S(2)}) %collective-permute-start.28) | collective-permute-done | bytes 65568 | tf_op jit(solution)/shard_map/ppermute | solution.py:310
  112.0 1.2 shard_map.105
  113.2 1.1 shard_map.107
  114.3 4.3 %collective-permute-start.29 = (bf16[32,40,256]{2,1,0:T(8,128)(2,1)S(1)}, bf16[32,40,256]{2,1,0:T(8,128)(2,1)S(1)}, u32[]{:S(2)}, u32[]{:S(2)}) collective-permute-start(bf16[32,40,256]{2,1,0:T(8,128)(2,1)S(1)} %get-tuple-element.64), channel_id=1, source_target_pairs={{0,1},{1,0},{2,3},{3,2},{4,5},{5,4},{6,7},{7,6},{8,9},{9,8},{10,11... | collective-permute-start | bytes 1966088 | tf_op jit(solution)/shard_map/ppermute | solution.py:322
  118.6 1.7 %collective-permute-done.29.got = bf16[32,40,256]{2,1,0:T(8,128)(2,1)S(1)} collective-permute-done((bf16[32,40,256]{2,1,0:T(8,128)(2,1)S(1)}, bf16[32,40,256]{2,1,0:T(8,128)(2,1)S(1)}, u32[]{:S(2)}, u32[]{:S(2)}) %collective-permute-start.29) | collective-permute-done | bytes 655392 | tf_op jit(solution)/shard_map/ppermute | solution.py:322
  121.4 17.9 %all-to-all-start.1 = ((bf16[32,40,256]{2,1,0:T(8,128)(2,1)}), bf16[32,40,256]{2,1,0:T(8,128)(2,1)S(1)}, u32[]{:S(2)}, u32[]{:S(2)}) async-start(bf16[32,40,256]{2,1,0:T(8,128)(2,1)} %shard_map.108), calls=%async_computation.1 | async-start | bytes 1310720 | tf_op jit(solution)/shard_map/all_to_all | solution.py:331
  139.3 1.2 shard_map.106
  140.5 19.4 %all-to-all-done.1.parts = bf16[32,40,256]{2,1,0:T(8,128)(2,1)S(1)} async-done(((bf16[32,40,256]{2,1,0:T(8,128)(2,1)}), bf16[32,40,256]{2,1,0:T(8,128)(2,1)S(1)}, u32[]{:S(2)}, u32[]{:S(2)}) %all-to-all-start.1) | async-done | bytes 655392 | tf_op jit(solution)/shard_map/all_to_all | solution.py:331
  (69 shorter events, 18.4 us)
Async XLA Ops:
  2.3 34.2 %all-to-all-start = ((bf16[32,40,256]{2,1,0:T(8,128)(2,1)}), bf16[32,40,256]{2,1,0:T(8,128)(2,1)S(1)}, u32[]{:S(2)}, u32[]{:S(2)}) async-start(bf16[32,40,256]{2,1,0:T(8,128)(2,1)} %shard_map.95), calls=%async_computation | async-start | bytes 1310720 | tf_op jit(solution)/shard_map/all_to_all | solution.py:259
  16.4 20.1 %collective-permute-start.1 = (bf16[4,128,256]{2,1,0:T(8,128)(2,1)S(1)}, bf16[4,128,256]{2,1,0:T(8,128)(2,1)S(1)}, u32[]{:S(2)}, u32[]{:S(2)}) collective-permute-start(bf16[4,128,256]{2,1,0:T(8,128)(2,1)S(1)} %get-tuple-element.36.own.refs_4_), channel_id=1, source_target_pairs={{1,0},{2,1},{3,2},{4,3},{5,4},{6,5},{7,6},{8,7},{9,8},{10,9},{11,1... | collective-permute-start | bytes 786440 | tf_op jit(solution)/shard_map/ppermute | solution.py:275
  18.3 18.2 %collective-permute-start = (bf16[4,128,256]{2,1,0:T(8,128)(2,1)S(1)}, bf16[4,128,256]{2,1,0:T(8,128)(2,1)S(1)}, u32[]{:S(2)}, u32[]{:S(2)}) collective-permute-start(bf16[4,128,256]{2,1,0:T(8,128)(2,1)S(1)} %get-tuple-element.36.own.refs_4_), channel_id=1, source_target_pairs={{0,1},{1,2},{2,3},{3,4},{4,5},{5,6},{6,7},{7,8},{8,9},{9,10},{10,1... | collective-permute-start | bytes 786440 | tf_op jit(solution)/shard_map/ppermute | solution.py:274
  20.7 15.8 %collective-permute-start.3 = (bf16[2,128,256]{2,1,0:T(8,128)(2,1)S(1)}, bf16[2,128,256]{2,1,0:T(8,128)(2,1)S(1)}, u32[]{:S(2)}, u32[]{:S(2)}) collective-permute-start(bf16[2,128,256]{2,1,0:T(8,128)(2,1)S(1)} %get-tuple-element.37), channel_id=1, source_target_pairs={{2,0},{3,1},{4,2},{5,3},{6,4},{7,5},{8,6},{9,7},{10,8},{11,9},{12,... | collective-permute-start | bytes 393224 | tf_op jit(solution)/shard_map/ppermute | solution.py:277
  22.9 13.6 %collective-permute-start.2 = (bf16[2,128,256]{2,1,0:T(8,128)(2,1)S(1)}, bf16[2,128,256]{2,1,0:T(8,128)(2,1)S(1)}, u32[]{:S(2)}, u32[]{:S(2)}) collective-permute-start(bf16[2,128,256]{2,1,0:T(8,128)(2,1)S(1)} %get-tuple-element.37), channel_id=1, source_target_pairs={{0,2},{1,3},{2,4},{3,5},{4,6},{5,7},{6,8},{7,9},{8,10},{9,11},{10,... | collective-permute-start | bytes 393224 | tf_op jit(solution)/shard_map/ppermute | solution.py:276
  36.5 4.0 %collective-permute-start.4 = (bf16[32,40,256]{2,1,0:T(8,128)(2,1)S(1)}, bf16[32,40,256]{2,1,0:T(8,128)(2,1)S(1)}, u32[]{:S(2)}, u32[]{:S(2)}) collective-permute-start(bf16[32,40,256]{2,1,0:T(8,128)(2,1)S(1)} %all-to-all-done.mine), channel_id=1, source_target_pairs={{0,1},{1,0},{2,3},{3,2},{4,5},{5,4},{6,7},{7,6},{8,9},{9,8},{10,11... | collective-permute-start | bytes 1966088 | tf_op jit(solution)/shard_map/ppermute | solution.py:279
  41.8 2.0 %collective-permute-start.7 = (bf16[128,256]{1,0:T(8,128)(2,1)S(1)}, bf16[128,256]{1,0:T(8,128)(2,1)S(1)}, u32[]{:S(2)}, u32[]{:S(2)}) collective-permute-start(bf16[128,256]{1,0:T(8,128)(2,1)S(1)} %get-tuple-element.46), channel_id=1, source_target_pairs={{449,384},{450,385},{451,386},{452,387},{453,388},{454,389},{455,3... | collective-permute-start | bytes 196616 | tf_op jit(solution)/shard_map/ppermute | solution.py:310
  42.5 1.4 collective-permute-start.6
  43.9 2.0 %collective-permute-start.10 = (bf16[128,256]{1,0:T(8,128)(2,1)S(1)}, bf16[128,256]{1,0:T(8,128)(2,1)S(1)}, u32[]{:S(2)}, u32[]{:S(2)}) collective-permute-start(bf16[128,256]{1,0:T(8,128)(2,1)S(1)} %get-tuple-element.48), channel_id=1, source_target_pairs={{385,320},{386,321},{387,322},{388,323},{389,324},{390,325},{391,3... | collective-permute-start | bytes 196616 | tf_op jit(solution)/shard_map/ppermute | solution.py:310
  44.6 1.4 collective-permute-start.9
  46.0 2.0 %collective-permute-start.13 = (bf16[128,256]{1,0:T(8,128)(2,1)S(1)}, bf16[128,256]{1,0:T(8,128)(2,1)S(1)}, u32[]{:S(2)}, u32[]{:S(2)}) collective-permute-start(bf16[128,256]{1,0:T(8,128)(2,1)S(1)} %get-tuple-element.50), channel_id=1, source_target_pairs={{321,256},{322,257},{323,258},{324,259},{325,260},{326,261},{327,2... | collective-permute-start | bytes 196616 | tf_op jit(solution)/shard_map/ppermute | solution.py:310
  46.7 1.4 collective-permute-start.12
  48.1 2.0 %collective-permute-start.16 = (bf16[128,256]{1,0:T(8,128)(2,1)S(1)}, bf16[128,256]{1,0:T(8,128)(2,1)S(1)}, u32[]{:S(2)}, u32[]{:S(2)}) collective-permute-start(bf16[128,256]{1,0:T(8,128)(2,1)S(1)} %get-tuple-element.52), channel_id=1, source_target_pairs={{257,192},{258,193},{259,194},{260,195},{261,196},{262,197},{263,1... | collective-permute-start | bytes 196616 | tf_op jit(solution)/shard_map/ppermute | solution.py:310
  48.8 1.4 collective-permute-start.15
  50.2 2.0 %collective-permute-start.19 = (bf16[128,256]{1,0:T(8,128)(2,1)S(1)}, bf16[128,256]{1,0:T(8,128)(2,1)S(1)}, u32[]{:S(2)}, u32[]{:S(2)}) collective-permute-start(bf16[128,256]{1,0:T(8,128)(2,1)S(1)} %get-tuple-element.54), channel_id=1, source_target_pairs={{193,128},{194,129},{195,130},{196,131},{197,132},{198,133},{199,1... | collective-permute-start | bytes 196616 | tf_op jit(solution)/shard_map/ppermute | solution.py:310
  52.3 2.0 %collective-permute-start.22 = (bf16[128,256]{1,0:T(8,128)(2,1)S(1)}, bf16[128,256]{1,0:T(8,128)(2,1)S(1)}, u32[]{:S(2)}, u32[]{:S(2)}) collective-permute-start(bf16[128,256]{1,0:T(8,128)(2,1)S(1)} %get-tuple-element.56), channel_id=1, source_target_pairs={{129,64},{130,65},{131,66},{132,67},{133,68},{134,69},{135,70},{13... | collective-permute-start | bytes 196616 | tf_op jit(solution)/shard_map/ppermute | solution.py:310
  54.4 46.4 %collective-permute-start.25 = (bf16[128,256]{1,0:T(8,128)(2,1)S(1)}, bf16[128,256]{1,0:T(8,128)(2,1)S(1)}, u32[]{:S(2)}, u32[]{:S(2)}) collective-permute-start(bf16[128,256]{1,0:T(8,128)(2,1)S(1)} %get-tuple-element.58), channel_id=1, source_target_pairs={{65,0},{66,1},{67,2},{68,3},{69,4},{70,5},{71,6},{72,7},{73,8},{74... | collective-permute-start | bytes 196616 | tf_op jit(solution)/shard_map/ppermute | solution.py:310
  55.7 45.8 %collective-permute-start.24 = (bf16[128,256]{1,0:T(8,128)(2,1)S(1)}, bf16[128,256]{1,0:T(8,128)(2,1)S(1)}, u32[]{:S(2)}, u32[]{:S(2)}) collective-permute-start(bf16[128,256]{1,0:T(8,128)(2,1)S(1)} %get-tuple-element.58), channel_id=1, source_target_pairs={{64,0},{65,1},{66,2},{67,3},{68,4},{69,5},{70,6},{71,7},{72,8},{73... | collective-permute-start | bytes 196616 | tf_op jit(solution)/shard_map/ppermute | solution.py:310
  57.0 44.5 %collective-permute-start.23 = (bf16[128,256]{1,0:T(8,128)(2,1)S(1)}, bf16[128,256]{1,0:T(8,128)(2,1)S(1)}, u32[]{:S(2)}, u32[]{:S(2)}) collective-permute-start(bf16[128,256]{1,0:T(8,128)(2,1)S(1)} %get-tuple-element.58), channel_id=1, source_target_pairs={{64,1},{65,2},{66,3},{67,4},{68,5},{69,6},{70,7},{71,8},{72,9},{73... | collective-permute-start | bytes 196616 | tf_op jit(solution)/shard_map/ppermute | solution.py:310
  102.1 9.9 %collective-permute-start.28 = (bf16[128,256]{1,0:T(8,128)(2,1)S(1)}, bf16[128,256]{1,0:T(8,128)(2,1)S(1)}, u32[]{:S(2)}, u32[]{:S(2)}) collective-permute-start(bf16[128,256]{1,0:T(8,128)(2,1)S(1)} %get-tuple-element.60), channel_id=1, source_target_pairs={{65,0},{66,1},{67,2},{68,3},{69,4},{70,5},{71,6},{72,7},{73,8},{74... | collective-permute-start | bytes 196616 | tf_op jit(solution)/shard_map/ppermute | solution.py:310
  103.4 8.6 %collective-permute-start.27 = (bf16[128,256]{1,0:T(8,128)(2,1)S(1)}, bf16[128,256]{1,0:T(8,128)(2,1)S(1)}, u32[]{:S(2)}, u32[]{:S(2)}) collective-permute-start(bf16[128,256]{1,0:T(8,128)(2,1)S(1)} %get-tuple-element.60), channel_id=1, source_target_pairs={{64,0},{65,1},{66,2},{67,3},{68,4},{69,5},{70,6},{71,7},{72,8},{73... | collective-permute-start | bytes 196616 | tf_op jit(solution)/shard_map/ppermute | solution.py:310
  104.7 7.3 %collective-permute-start.26 = (bf16[128,256]{1,0:T(8,128)(2,1)S(1)}, bf16[128,256]{1,0:T(8,128)(2,1)S(1)}, u32[]{:S(2)}, u32[]{:S(2)}) collective-permute-start(bf16[128,256]{1,0:T(8,128)(2,1)S(1)} %get-tuple-element.60), channel_id=1, source_target_pairs={{64,1},{65,2},{66,3},{67,4},{68,5},{69,6},{70,7},{71,8},{72,9},{73... | collective-permute-start | bytes 196616 | tf_op jit(solution)/shard_map/ppermute | solution.py:310
  114.3 6.0 %collective-permute-start.29 = (bf16[32,40,256]{2,1,0:T(8,128)(2,1)S(1)}, bf16[32,40,256]{2,1,0:T(8,128)(2,1)S(1)}, u32[]{:S(2)}, u32[]{:S(2)}) collective-permute-start(bf16[32,40,256]{2,1,0:T(8,128)(2,1)S(1)} %get-tuple-element.64), channel_id=1, source_target_pairs={{0,1},{1,0},{2,3},{3,2},{4,5},{5,4},{6,7},{7,6},{8,9},{9,8},{10,11... | collective-permute-start | bytes 1966088 | tf_op jit(solution)/shard_map/ppermute | solution.py:322
  121.4 38.5 %all-to-all-start.1 = ((bf16[32,40,256]{2,1,0:T(8,128)(2,1)}), bf16[32,40,256]{2,1,0:T(8,128)(2,1)S(1)}, u32[]{:S(2)}, u32[]{:S(2)}) async-start(bf16[32,40,256]{2,1,0:T(8,128)(2,1)} %shard_map.108), calls=%async_computation.1 | async-start | bytes 1310720 | tf_op jit(solution)/shard_map/all_to_all | solution.py:331
  (14 other events, 104.5 us)

commit v4 on v3

--- a/solution.py
+++ b/solution.py
@@ -58,24 +58,60 @@
         wide[k] = part
 
 
-def pack_kernel(order, count, tiles, x, cot, pack, xs, mask, state):
+def pack_kernel(order, count, tiles, x, cot, send, keep, state):
     state[...] = jnp.zeros_like(state)
+    core = lax.axis_index("c")
     most = tiles.shape[1]
+    on = []
     for tile in range(COLS // TILE):
         live = jnp.int32(0)
         for k in range(most):
             live = live | ((tiles[0, k] == tile) & (k < count[0])).astype(jnp.int32)
-        value = live.astype(F32)
-        mask[tile * TILE : (tile + 1) * TILE, :] = jnp.full((TILE, CH), value, F32)
-    on = mask[...]
-    for slot in range(2):
-        image = x[order[slot]]
-        xs[slot] = image
-        pack[slot] = image
-        pack[2 + slot] = (cot[slot].astype(F32) * on).astype(BF)
-
-
-def prep_kernel(mine, other, bias, own, up1, down1, up2, down2, deriv, weights):
+        on.append(live.astype(F32))
+    row = lax.broadcasted_iota(jnp.int32, (TILE, CH), 0)
+    marks = jnp.zeros((TILE, CH), F32)
+    for tile, value in enumerate(on):
+        marks = jnp.where(row == tile, value, marks)
+    for target, slot in ((keep, core), (send, 1 - core)):
+        target[:COLS] = x[order[slot]]
+        for tile, value in enumerate(on):
+            rows = cot[slot, tile * TILE : (tile + 1) * TILE].astype(F32) * value
+            target[COLS + tile * TILE : COLS + (tile + 1) * TILE] = rows.astype(BF)
+        target[2 * COLS :] = marks.astype(BF)
+
+
+def arrange_kernel(keep, got, block, both, first):
+    core = lax.axis_index("c")
+
+    def place(one, two):
+        for j, rows in enumerate((one, two)):
+            block[j * COLS : (j + 1) * COLS] = rows[:COLS]
+            both[j * COLS : (j + 1) * COLS] = rows[:COLS]
+            block[(2 + j) * COLS : (3 + j) * COLS] = rows[COLS : 2 * COLS]
+            block[4 * COLS + j * TILE : 4 * COLS + (j + 1) * TILE] = rows[2 * COLS :]
+        first[...] = one[:COLS]
+
+    @pl.when(core == 0)
+    def _():
+        place(keep, got)
+
+    @pl.when(core == 1)
+    def _():
+        place(got, keep)
+
+
+def position():
+    chip = lax.axis_index("x") * lax.axis_size("z") + lax.axis_index("z")
+    odd = lax.axis_index("y") % 2 == 1
+    return chip, odd
+
+
+def keep_factor(chips):
+    chip, odd = position()
+    return jnp.where(odd & (chip == chips - 1), 0.0, 1.0).astype(BF)
+
+
+def prep_kernel(mine, other, bias, block, before, after, second, deriv, weights, x6, mask):
     core = lax.axis_index("c")
 
     def assemble(even, odd):
@@ -94,86 +130,134 @@
     def _():
         assemble(other, mine)
 
+    chip, odd = position()
+    even = jnp.logical_not(odd)
+    last = GROUPS - 1
+
+    def rows(ref, j):
+        return ref[j * COLS : (j + 1) * COLS]
+
+    own0, own1 = rows(block, 0), rows(block, 1)
+    next0, next1 = rows(after, 0), rows(after, 1)
+    prev0, prev1 = rows(before, 0), rows(before, 1)
+    zero = jnp.zeros((COLS, CH), BF)
+    start = even & (chip == 0)
+    end = even & (chip == last)
+    cut0 = start | (odd & (chip == 0))
+    cut5 = end | (odd & (chip == last - 1))
+    x6[0] = jnp.where(cut0, zero, jnp.where(odd, prev1, prev0))
+    x6[1] = jnp.where(start, zero, jnp.where(odd, own0, prev1))
+    x6[2] = jnp.where(odd, own1, own0)
+    x6[3] = jnp.where(odd, next0, own1)
+    x6[4] = jnp.where(end, zero, jnp.where(odd, next1, next0))
+    x6[5] = jnp.where(cut5, zero, jnp.where(odd, second[...], next1))
+
+    own_marks = block[4 * COLS :].astype(F32)
+    next_marks = after[4 * COLS :].astype(F32)
+    for j in range(2):
+        here = own_marks[j * TILE : (j + 1) * TILE]
+        there = own_marks[TILE:] if j == 0 else next_marks[:TILE]
+        marks = jnp.where(odd, there, here)
+        for tile in range(COLS // TILE):
+            mask[j * COLS + tile * TILE : j * COLS + (tile + 1) * TILE] = jnp.broadcast_to(
+                marks[tile : tile + 1], (TILE, CH)
+            )
+
+    keep = keep_factor(GROUPS)
+    lhs = [
+        jnp.concatenate([x6[0], x6[1], x6[2] * keep, x6[3]], axis=0),
+        jnp.concatenate([x6[1], x6[2], x6[3], x6[4]], axis=0),
+        jnp.concatenate([x6[2], x6[3] * keep, x6[4], x6[5]], axis=0),
+    ]
     shift = jnp.broadcast_to(bias[...], (COLS, CH))
-    for slot in range(2):
-        x = jnp.concatenate([up2[slot], up1[slot], own[slot], down1[slot], down2[slot]], axis=0)
-        sums = []
-        for b in range(3):
-            total = None
-            for a in range(3):
-                tap = (3 * a + b) * CH
-                term = jnp.dot(
-                    x[a * COLS : (a + 3) * COLS],
-                    weights[tap : tap + CH],
-                    preferred_element_type=F32,
-                )
-                total = term if total is None else total + term
-            sums.append(total)
-        for r in range(3):
-            rows = slice(r * COLS, (r + 1) * COLS)
-            pre = from_left(sums[0][rows]) + sums[1][rows] + from_right(sums[2][rows]) + shift
-            sig = jax.nn.sigmoid(pre)
-            deriv[slot, r] = sig * (1.0 + pre * (1.0 - sig))
-
-
-def step_kernel(step, sections, *refs):
-    mask, deriv, weights = refs[:3]
-    rest = refs[3:]
-    if step <= 1:
-        cots, rest = rest[:3], rest[3:]
-    if step >= 1:
-        got, rest = rest[:3], rest[3:]
-    state_in, back, state = rest
+    sums = []
+    for b in range(3):
+        total = None
+        for a in range(3):
+            tap = (3 * a + b) * CH
+            term = jnp.dot(lhs[a], weights[tap : tap + CH], preferred_element_type=F32)
+            total = term if total is None else total + term
+        sums.append(total)
+    for r in range(4):
+        part = slice(r * COLS, (r + 1) * COLS)
+        pre = from_left(sums[0][part]) + sums[1][part] + from_right(sums[2][part]) + shift
+        sig = jax.nn.sigmoid(pre)
+        value = sig * (1.0 + pre * (1.0 - sig))
+        if r == 0:
+            value = jnp.where(start, 0.0, value)
+        if r == 3:
+            value = jnp.where(end, 0.0, value)
+        deriv[r] = value
+
+
+def step_kernel(step, sections, mask, deriv, weights, low, high, state_in, *outs):
+    state = outs[0]
     state[...] = state_in[...]
-    section = lax.axis_index("y")
-    slot = step - (sections - 1 - section)
-
-    @pl.when((slot >= 0) & (slot < 2))
+
+    @pl.when(lax.axis_index("y") == sections - 1 - step)
     def _():
+        base = 2 * COLS if step == 0 else 0
+        keep = keep_factor(GROUPS)
         gpre = []
-        for r in range(3):
-            if step == 0:
-                upstream = cots[r][2]
-            elif step == 1:
-                upstream = jnp.where(section == sections - 1, cots[r][3], got[r][...])
-            else:
-                upstream = got[r][...]
-            gpre.append((upstream.astype(F32) * deriv[slot, r]).astype(BF))
-        state[slot] = gpre[1]
+        for r in range(4):
+            at = base + (r % 2) * COLS
+            upstream = (low if r < 2 else high)[at : at + COLS]
+            gpre.append((upstream.astype(F32) * deriv[r]).astype(BF))
+        state[0] = gpre[1]
+        state[1] = gpre[2]
+        lhs = [
+            jnp.concatenate([gpre[2] * keep, gpre[3]], axis=0),
+            jnp.concatenate([gpre[1], gpre[2]], axis=0),
+            jnp.concatenate([gpre[0], gpre[1] * keep], axis=0),
+        ]
         sums = []
         for b in range(3):
             total = None
             for a in range(3):
                 tap = (3 * a + b) * CH
                 term = lax.dot_general(
-                    gpre[2 - a],
+                    lhs[a],
                     weights[tap : tap + CH],
                     (((1,), (1,)), ((), ())),
                     preferred_element_type=F32,
                 )
                 total = term if total is None else total + term
             sums.append(total)
-        value = from_right(sums[0]) + sums[1] + from_left(sums[2])
-        value = (value * mask[...]).astype(BF)
-        back[...] = value
-        state[2 + slot] = value
-
-
-def grads_kernel(order, state, grads):
-    for slot in range(2):
-        grads[order[slot]] = state[2 + slot]
-
-
-def wgrad_kernel(own, up, down, gacc, mine, theirs, total):
-    core = lax.axis_index("c")
-    g = [gacc[slot].astype(F32) for slot in range(2)]
+        for j in range(2):
+            part = slice(j * COLS, (j + 1) * COLS)
+            value = from_right(sums[0][part]) + sums[1][part] + from_left(sums[2][part])
+            value = (value * mask[part]).astype(BF)
+            state[2 + j] = value
+            if len(outs) > 1:
+                outs[1][part] = value
+
+
+def grads_kernel(order, state, got, other, grads):
+    core = lax.axis_index("c")
+    _, odd = position()
+    grads[order[1 - core]] = got[...]
+    mine = jnp.where(core == 0, other[...], state[2])
+    grads[order[core]] = jnp.where(odd, mine, state[2 + core])
+
+
+def wgrad_kernel(x6, state, mine, theirs, send, spill, total):
+    core = lax.axis_index("c")
+    _, odd = position()
+    send[...] = jnp.where(odd == (core == 1), state[3], state[2])
+    spill[...] = state[3]
+    keep = keep_factor(GROUPS)
+    g = [state[j].astype(F32) for j in range(2)]
     shifted = [
         jnp.concatenate([from_right(g[0]), from_right(g[1])], axis=0).astype(BF),
-        jnp.concatenate([gacc[0], gacc[1]], axis=0),
+        jnp.concatenate([state[0], state[1]], axis=0),
         jnp.concatenate([from_left(g[0]), from_left(g[1])], axis=0).astype(BF),
     ]
-    for a, rows in enumerate((up, own, down)):
-        x = jnp.concatenate([rows[0], rows[1]], axis=0)
+    lhs = [
+        jnp.concatenate([x6[1], x6[2] * keep], axis=0),
+        jnp.concatenate([x6[2], x6[3]], axis=0),
+        jnp.concatenate([x6[3] * keep, x6[4]], axis=0),
+    ]
+    for a, x in enumerate(lhs):
         for b in range(3):
             tap = (3 * a + b) * CH
             total[tap : tap + CH] = lax.dot_general(
@@ -232,22 +316,29 @@
     bgrad[...] = result
 
 
-def shift_pairs(size, by):
-    return [(s, s + by) for s in range(size) if 0 <= s + by < size]
-
-
-def hop_pairs(planes, size, by):
+def chip_pairs(planes, by, down=0):
     return [
-        (p * size + s, (p - 1) * size + s + by)
+        (p * 64 + 2 * k + c, (p - down) * 64 + 2 * ((k + by) % GROUPS) + c)
         for p in planes
-        for s in range(size)
-        if 0 <= s + by < size
+        for k in range(GROUPS)
+        for c in range(2)
     ]
+
+
+def return_pairs(sections):
+    pairs = []
+    for p in range(sections):
+        for k in range(GROUPS):
+            one, two = p * 64 + 2 * k, p * 64 + 2 * k + 1
+            pairs.append((one, two))
+            pairs.append((two, p * 64 + 2 * ((k + 1) % GROUPS)) if p % 2 else (two, one))
+    return pairs
 
 
 def body(saved_inputs, weights, biases, cotangent, tile_list, tile_count, order):
     sections = lax.axis_size("y")
-    size = 64
+    every = range(sections)
+    odds = range(1, sections, 2)
     image = (2, COLS, CH)
     inputs = saved_inputs.reshape(image)
     cot = cotangent.reshape(image)
@@ -258,69 +349,88 @@
     swap = [(0, 1), (1, 0)]
     mine = lax.all_to_all(wide, ("x", "z"), 0, 0)
 
-    pack, xs, mask, state = call(
+    send, keep, state = call(
         pack_kernel,
         [SMEM] * 3 + [VMEM] * 2,
-        [
-            out((4, COLS, CH), BF),
-            out(image, BF),
-            out((COLS, CH), F32),
-            out((4, COLS, CH), BF),
-        ],
+        [out((2 * COLS + TILE, CH), BF)] * 2 + [out((4, COLS, CH), BF)],
         (order, tile_count, tile_list, inputs, cot),
         flops=1 << 28,
         moved=3 << 20,
     )
-    up1 = lax.ppermute(pack, SEC, shift_pairs(size, 1))
-    down1 = lax.ppermute(pack, SEC, shift_pairs(size, -1))
-    up2 = lax.ppermute(xs, SEC, shift_pairs(size, 2))
-    down2 = lax.ppermute(xs, SEC, shift_pairs(size, -2))
-    mine, up1, down1, up2, down2 = lax.optimization_barrier((mine, up1, down1, up2, down2))
+    got = lax.ppermute(send, "c", swap)
+    block, both, first = call(
+        arrange_kernel,
+        [VMEM] * 2,
+        [
+            out((4 * COLS + 2 * TILE, CH), BF),
+            out((2 * COLS, CH), BF),
+            out((COLS, CH), BF),
+        ],
+        (keep, got),
+        flops=1 << 26,
+        moved=1 << 20,
+    )
+    after = lax.ppermute(block, ALL, chip_pairs(every, -1))
+    before = lax.ppermute(both, ALL, chip_pairs(every, 1))
+    second = lax.ppermute(first, ALL, chip_pairs(odds, -2))
+    mine, after, before, second = lax.optimization_barrier((mine, after, before, second))
     other = lax.ppermute(mine, "c", swap)
 
-    deriv, wfull = call(
+    deriv, wfull, x6, mask = call(
         prep_kernel,
-        [VMEM] * 8,
-        [out((2, 3, COLS, CH), F32), out((9 * CH, CH), BF)],
-        (mine, other, biases, pack, up1, down1, up2, down2),
+        [VMEM] * 7,
+        [
+            out((4, COLS, CH), F32),
+            out((9 * CH, CH), BF),
+            out((6, COLS, CH), BF),
+            out((2 * COLS, CH), F32),
+        ],
+        (mine, other, biases, block, before, after, second),
         flops=1 << 30,
         moved=4 << 20,
     )
 
-    got = None
-    for step in range(sections + 1):
-        operands = [mask, deriv, wfull]
-        if step <= 1:
-            operands += [up1, pack, down1]
-        if step >= 1:
-            operands += got
-        count = len(operands)
-        back, state = call(
+    low, high = block, after
+    for step in range(sections):
+        live = step < sections - 1
+        state, *back = call(
             lambda *refs, step=step: step_kernel(step, sections, *refs),
-            [VMEM] * (count + 1),
-            [out((COLS, CH), BF), out((4, COLS, CH), BF)],
-            (*operands, state),
-            aliases={count: 1},
+            [VMEM] * 6,
+            [out((4, COLS, CH), BF)] + [out((2 * COLS, CH), BF)] * live,
+            (mask, deriv, wfull, low, high, state),
+            aliases={5: 0},
             flops=1 << 27,
             moved=2 << 20,
         )
-        if step < sections:
-            planes = [p for p in (sections - 1 - step, sections - step) if 0 < p < sections]
-            got = [
-                lax.ppermute(back, ALL, hop_pairs(planes, size, by)) for by in (1, 0, -1)
-            ]
-
-    mine, theirs = call(
+        if live:
+            plane = sections - 1 - step
+            straight = lax.ppermute(back[0], ALL, chip_pairs([plane], 0, 1))
+            if plane % 2:
+                side = lax.ppermute(back[0], ALL, chip_pairs([plane], 1, 1))
+                low, high = side, straight
+            else:
+                side = lax.ppermute(back[0], ALL, chip_pairs([plane], -1, 1))
+                low, high = straight, side
+
+    mine, theirs, send, spill = call(
         wgrad_kernel,
-        [VMEM] * 4,
-        [out((GROUPS, WIN, CH), F32), out((GROUPS, WIN, CH), BF)],
-        (pack, up1, down1, state),
+        [VMEM] * 2,
+        [out((GROUPS, WIN, CH), F32), out((GROUPS, WIN, CH), BF)] + [out((COLS, CH), BF)] * 2,
+        (x6, state),
         scratch=[pltpu.VMEM((9 * CH, CH), F32)],
         flops=1 << 28,
         moved=4 << 20,
     )
     received = lax.ppermute(theirs, "c", swap)
-    (grads,) = call(grads_kernel, [SMEM, VMEM], [out(image, BF)], (order, state), moved=1 << 18)
+    got = lax.ppermute(send, ALL, return_pairs(sections))
+    spilled = lax.ppermute(spill, ALL, chip_pairs(odds, 1))
+    (grads,) = call(
+        grads_kernel,
+        [SMEM] + [VMEM] * 3,
+        [out(image, BF)],
+        (order, state, got, spilled),
+        moved=1 << 18,
+    )
     (both,) = call(
         pair_kernel,
         [VMEM] * 2,

time: 162 us -> 148 us (0.914)
  starting transfers between devices: 66.7 us -> 45.1 us
  waiting for transfers between devices: 82.3 us -> 91.6 us
    ppermute x28 -> x20, waiting for transfers between devices: 59.1 us -> 70.8 us  [the longest x7 54 us: body(): straight = lax.ppermute(back[0], ALL, chip_pairs([plane], 0, 1))]
    all_to_all x1, starting transfers between devices: 17.9 us -> 6.93 us  [body(): parts = lax.all_to_all(both, ('x', 'z'), 0, 0)]
    ppermute x28 -> x20, starting transfers between devices: 29.9 us -> 21.6 us  [the longest x7 5.31 us: body(): straight = lax.ppermute(back[0], ALL, chip_pairs([plane], 0, 1))]
    all_to_all x1, waiting for transfers between devices: 19.4 us -> 16.7 us  [body(): parts = lax.all_to_all(both, ('x', 'z'), 0, 0)]
    ppermute x1, starting transfers between devices: 4.26 us -> 1.92 us  [body(): received = lax.ppermute(theirs, 'c', swap)]
  transfers between devices with their start and end apart: 32 -> 24, of which waited for: 7 -> 9; matrix products, arithmetic and copies ran while one was open for 0% -> 0% of each run, Pallas kernels for 1% -> 1%
where the time goes in v4:
time: 148 us; the launch traced here: 147 us
  waiting for transfers between devices  91.6 us (62%)
  starting transfers between devices  45.1 us (30%)
  Pallas kernels  7.43 us (5%)
  between operations  1.73 us (1%)
    ppermute x7, waiting for transfers between devices, body(): straight = lax.ppermute(back[0], ALL, chip_pairs([plane], 0, 1))  54 us
    all_to_all x1, waiting for transfers between devices, body(): parts = lax.all_to_all(both, ('x', 'z'), 0, 0)  16.7 us
    all_to_all x1, starting transfers between devices, body(): mine = lax.all_to_all(wide, ('x', 'z'), 0, 0)  12.7 us
    pallas_call x16, Pallas kernels, call(): pl.pallas_call(kernel, out_shape=outs, in_specs=ins, out_specs=[VMEM] * l...  7.43 us
    all_to_all x1, starting transfers between devices, body(): parts = lax.all_to_all(both, ('x', 'z'), 0, 0)  6.93 us
    ppermute x1, waiting for transfers between devices, body(): before = lax.ppermute(both, ALL, chip_pairs(every, 1))  6.85 us
    ppermute x7, starting transfers between devices, body(): straight = lax.ppermute(back[0], ALL, chip_pairs([plane], 0, 1))  5.31 us
    ppermute x4, waiting for transfers between devices, body(): side = lax.ppermute(back[0], ALL, chip_pairs([plane], 1, 1))  4.23 us
  transfers between devices with their start and end apart: 24, of which 9 were waited for; matrix products, arithmetic and copies ran while one was open for 0% of the time, Pallas kernels for 1%

profile of v4, /device:TPU:64, one launch (start us, length us, event | category | flops | bytes accessed | tf_op | source)
XLA Modules:
  0.0 147.2 jit_solution(17573776661617566369)
XLA Ops:
  0.7 0.7 copy-done
  1.4 0.9 shard_map.94
  2.3 12.7 %all-to-all-start = ((bf16[32,40,256]{2,1,0:T(8,128)(2,1)}), bf16[32,40,256]{2,1,0:T(8,128)(2,1)S(1)}, u32[]{:S(2)}, u32[]{:S(2)}) async-start(bf16[32,40,256]{2,1,0:T(8,128)(2,1)} %shard_map.94), calls=%async_computation | async-start | bytes 1310720 | tf_op jit(solution)/shard_map/all_to_all | solution.py:350
  16.3 1.9 %collective-permute-start = (bf16[272,256]{1,0:T(8,128)(2,1)S(1)}, bf16[272,256]{1,0:T(8,128)(2,1)S(1)}, u32[]{:S(2)}, u32[]{:S(2)}) collective-permute-start(bf16[272,256]{1,0:T(8,128)(2,1)S(1)} %get-tuple-element.38), channel_id=1, source_target_pairs={{0,1},{1,0},{2,3},{3,2},{4,5},{5,4},{6,7},{7,6},{8,9},{9,8},{10,11... | collective-permute-start | bytes 417800 | tf_op jit(solution)/shard_map/ppermute | solution.py:360
  18.3 1.3 collective-permute-done.got
  19.6 2.1 %collective-permute-start.1 = (bf16[544,256]{1,0:T(8,128)(2,1)S(1)}, bf16[544,256]{1,0:T(8,128)(2,1)S(1)}, u32[]{:S(2)}, u32[]{:S(2)}) collective-permute-start(bf16[544,256]{1,0:T(8,128)(2,1)S(1)} %get-tuple-element.39.block.refs_3_), channel_id=1, source_target_pairs={{0,62},{1,63},{2,0},{3,1},{4,2},{5,3},{6,4},{7,5},{8,6},{9,7},{10,... | collective-permute-start | bytes 835592 | tf_op jit(solution)/shard_map/ppermute | solution.py:373
  21.8 3.7 %collective-permute-start.2 = (bf16[256,256]{1,0:T(8,128)(2,1)S(1)}, bf16[256,256]{1,0:T(8,128)(2,1)S(1)}, u32[]{:S(2)}, u32[]{:S(2)}) collective-permute-start(bf16[256,256]{1,0:T(8,128)(2,1)S(1)} %get-tuple-element.40), channel_id=1, source_target_pairs={{0,2},{1,3},{2,4},{3,5},{4,6},{5,7},{6,8},{7,9},{8,10},{9,11},{10,... | collective-permute-start | bytes 393224 | tf_op jit(solution)/shard_map/ppermute | solution.py:374
  26.2 6.8 %collective-permute-done.2.before = bf16[256,256]{1,0:T(8,128)(2,1)S(1)} collective-permute-done((bf16[256,256]{1,0:T(8,128)(2,1)S(1)}, bf16[256,256]{1,0:T(8,128)(2,1)S(1)}, u32[]{:S(2)}, u32[]{:S(2)}) %collective-permute-start.2) | collective-permute-done | bytes 131104 | tf_op jit(solution)/shard_map/ppermute | solution.py:374
  33.0 3.8 %collective-permute-done.1.after.refs_4_ = bf16[544,256]{1,0:T(8,128)(2,1)S(1)} collective-permute-done((bf16[544,256]{1,0:T(8,128)(2,1)S(1)}, bf16[544,256]{1,0:T(8,128)(2,1)S(1)}, u32[]{:S(2)}, u32[]{:S(2)}) %collective-permute-start.1) | collective-permute-done | bytes 278560 | tf_op jit(solution)/shard_map/ppermute | solution.py:373
  36.8 1.9 %collective-permute-start.4 = (bf16[32,40,256]{2,1,0:T(8,128)(2,1)S(1)}, bf16[32,40,256]{2,1,0:T(8,128)(2,1)S(1)}, u32[]{:S(2)}, u32[]{:S(2)}) collective-permute-start(bf16[32,40,256]{2,1,0:T(8,128)(2,1)S(1)} %all-to-all-done.mine), channel_id=1, source_target_pairs={{0,1},{1,0},{2,3},{3,2},{4,5},{5,4},{6,7},{7,6},{8,9},{9,8},{10,11... | collective-permute-start | bytes 1966088 | tf_op jit(solution)/shard_map/ppermute | solution.py:377
  38.7 2.1 %collective-permute-done.4.other = bf16[32,40,256]{2,1,0:T(8,128)(2,1)S(1)} collective-permute-done((bf16[32,40,256]{2,1,0:T(8,128)(2,1)S(1)}, bf16[32,40,256]{2,1,0:T(8,128)(2,1)S(1)}, u32[]{:S(2)}, u32[]{:S(2)}) %collective-permute-start.4) | collective-permute-done | bytes 655392 | tf_op jit(solution)/shard_map/ppermute | solution.py:377
  40.8 1.0 shard_map.97
  50.4 1.3 collective-permute-start.18
  51.7 1.3 collective-permute-start.17
  53.0 54.0 %collective-permute-done.18.refs_4_ = bf16[256,256]{1,0:T(8,128)(2,1)S(1)} collective-permute-done((bf16[256,256]{1,0:T(8,128)(2,1)S(1)}, bf16[256,256]{1,0:T(8,128)(2,1)S(1)}, u32[]{:S(2)}, u32[]{:S(2)}) %collective-permute-start.18) | collective-permute-done | bytes 131104 | tf_op jit(solution)/shard_map/ppermute | solution.py:407
  107.0 4.2 %collective-permute-done.17.refs_3_ = bf16[256,256]{1,0:T(8,128)(2,1)S(1)} collective-permute-done((bf16[256,256]{1,0:T(8,128)(2,1)S(1)}, bf16[256,256]{1,0:T(8,128)(2,1)S(1)}, u32[]{:S(2)}, u32[]{:S(2)}) %collective-permute-start.17) | collective-permute-done | bytes 131104 | tf_op jit(solution)/shard_map/ppermute | solution.py:409
  111.8 1.1 shard_map.106
  112.9 1.9 %collective-permute-start.21 = (bf16[32,40,256]{2,1,0:T(8,128)(2,1)S(1)}, bf16[32,40,256]{2,1,0:T(8,128)(2,1)S(1)}, u32[]{:S(2)}, u32[]{:S(2)}) collective-permute-start(bf16[32,40,256]{2,1,0:T(8,128)(2,1)S(1)} %get-tuple-element.68), channel_id=1, source_target_pairs={{0,1},{1,0},{2,3},{3,2},{4,5},{5,4},{6,7},{7,6},{8,9},{9,8},{10,11... | collective-permute-start | bytes 1966088 | tf_op jit(solution)/shard_map/ppermute | solution.py:424
  114.8 2.1 %collective-permute-done.21.got = bf16[32,40,256]{2,1,0:T(8,128)(2,1)S(1)} collective-permute-done((bf16[32,40,256]{2,1,0:T(8,128)(2,1)S(1)}, bf16[32,40,256]{2,1,0:T(8,128)(2,1)S(1)}, u32[]{:S(2)}, u32[]{:S(2)}) %collective-permute-start.21) | collective-permute-done | bytes 655392 | tf_op jit(solution)/shard_map/ppermute | solution.py:424
  116.9 1.0 shard_map.108
  117.9 6.9 %all-to-all-start.1 = ((bf16[32,40,256]{2,1,0:T(8,128)(2,1)}), bf16[32,40,256]{2,1,0:T(8,128)(2,1)S(1)}, u32[]{:S(2)}, u32[]{:S(2)}) async-start(bf16[32,40,256]{2,1,0:T(8,128)(2,1)} %shard_map.108), calls=%async_computation.1 | async-start | bytes 1310720 | tf_op jit(solution)/shard_map/all_to_all | solution.py:441
  124.9 1.9 %collective-permute-start.19 = (bf16[128,256]{1,0:T(8,128)(2,1)S(1)}, bf16[128,256]{1,0:T(8,128)(2,1)S(1)}, u32[]{:S(2)}, u32[]{:S(2)}) collective-permute-start(bf16[128,256]{1,0:T(8,128)(2,1)S(1)} %get-tuple-element.65), channel_id=1, source_target_pairs={{0,1},{1,0},{2,3},{3,2},{4,5},{5,4},{6,7},{7,6},{8,9},{9,8},{10,11... | collective-permute-start | bytes 196616 | tf_op jit(solution)/shard_map/ppermute | solution.py:425
  128.0 1.2 shard_map.107
  129.2 16.7 %all-to-all-done.1.parts = bf16[32,40,256]{2,1,0:T(8,128)(2,1)S(1)} async-done(((bf16[32,40,256]{2,1,0:T(8,128)(2,1)}), bf16[32,40,256]{2,1,0:T(8,128)(2,1)S(1)}, u32[]{:S(2)}, u32[]{:S(2)}) %all-to-all-start.1) | async-done | bytes 655392 | tf_op jit(solution)/shard_map/all_to_all | solution.py:441
  (53 shorter events, 12.9 us)
Async XLA Ops:
  2.3 34.5 %all-to-all-start = ((bf16[32,40,256]{2,1,0:T(8,128)(2,1)}), bf16[32,40,256]{2,1,0:T(8,128)(2,1)S(1)}, u32[]{:S(2)}, u32[]{:S(2)}) async-start(bf16[32,40,256]{2,1,0:T(8,128)(2,1)} %shard_map.94), calls=%async_computation | async-start | bytes 1310720 | tf_op jit(solution)/shard_map/all_to_all | solution.py:350
  16.3 3.3 %collective-permute-start = (bf16[272,256]{1,0:T(8,128)(2,1)S(1)}, bf16[272,256]{1,0:T(8,128)(2,1)S(1)}, u32[]{:S(2)}, u32[]{:S(2)}) collective-permute-start(bf16[272,256]{1,0:T(8,128)(2,1)S(1)} %get-tuple-element.38), channel_id=1, source_target_pairs={{0,1},{1,0},{2,3},{3,2},{4,5},{5,4},{6,7},{7,6},{8,9},{9,8},{10,11... | collective-permute-start | bytes 417800 | tf_op jit(solution)/shard_map/ppermute | solution.py:360
  19.6 17.2 %collective-permute-start.1 = (bf16[544,256]{1,0:T(8,128)(2,1)S(1)}, bf16[544,256]{1,0:T(8,128)(2,1)S(1)}, u32[]{:S(2)}, u32[]{:S(2)}) collective-permute-start(bf16[544,256]{1,0:T(8,128)(2,1)S(1)} %get-tuple-element.39.block.refs_3_), channel_id=1, source_target_pairs={{0,62},{1,63},{2,0},{3,1},{4,2},{5,3},{6,4},{7,5},{8,6},{9,7},{10,... | collective-permute-start | bytes 835592 | tf_op jit(solution)/shard_map/ppermute | solution.py:373
  21.8 11.2 %collective-permute-start.2 = (bf16[256,256]{1,0:T(8,128)(2,1)S(1)}, bf16[256,256]{1,0:T(8,128)(2,1)S(1)}, u32[]{:S(2)}, u32[]{:S(2)}) collective-permute-start(bf16[256,256]{1,0:T(8,128)(2,1)S(1)} %get-tuple-element.40), channel_id=1, source_target_pairs={{0,2},{1,3},{2,4},{3,5},{4,6},{5,7},{6,8},{7,9},{8,10},{9,11},{10,... | collective-permute-start | bytes 393224 | tf_op jit(solution)/shard_map/ppermute | solution.py:374
  25.5 0.7 collective-permute-start.3
  36.8 4.0 %collective-permute-start.4 = (bf16[32,40,256]{2,1,0:T(8,128)(2,1)S(1)}, bf16[32,40,256]{2,1,0:T(8,128)(2,1)S(1)}, u32[]{:S(2)}, u32[]{:S(2)}) collective-permute-start(bf16[32,40,256]{2,1,0:T(8,128)(2,1)S(1)} %all-to-all-done.mine), channel_id=1, source_target_pairs={{0,1},{1,0},{2,3},{3,2},{4,5},{5,4},{6,7},{7,6},{8,9},{9,8},{10,11... | collective-permute-start | bytes 1966088 | tf_op jit(solution)/shard_map/ppermute | solution.py:377
  41.8 1.4 collective-permute-start.6
  42.5 0.7 collective-permute-start.5
  43.2 1.4 collective-permute-start.8
  43.9 0.7 collective-permute-start.7
  44.7 1.4 collective-permute-start.10
  45.3 0.7 collective-permute-start.9
  46.1 1.4 collective-permute-start.12
  46.8 0.7 collective-permute-start.11
  47.5 1.4 collective-permute-start.14
  48.2 0.7 collective-permute-start.13
  48.9 1.4 collective-permute-start.16
  49.6 0.7 collective-permute-start.15
  50.4 56.6 %collective-permute-start.18 = (bf16[256,256]{1,0:T(8,128)(2,1)S(1)}, bf16[256,256]{1,0:T(8,128)(2,1)S(1)}, u32[]{:S(2)}, u32[]{:S(2)}) collective-permute-start(bf16[256,256]{1,0:T(8,128)(2,1)S(1)} %get-tuple-element.62), channel_id=1, source_target_pairs={{64,0},{65,1},{66,2},{67,3},{68,4},{69,5},{70,6},{71,7},{72,8},{73... | collective-permute-start | bytes 393224 | tf_op jit(solution)/shard_map/ppermute | solution.py:407
  51.7 59.6 %collective-permute-start.17 = (bf16[256,256]{1,0:T(8,128)(2,1)S(1)}, bf16[256,256]{1,0:T(8,128)(2,1)S(1)}, u32[]{:S(2)}, u32[]{:S(2)}) collective-permute-start(bf16[256,256]{1,0:T(8,128)(2,1)S(1)} %get-tuple-element.62), channel_id=1, source_target_pairs={{64,2},{65,3},{66,4},{67,5},{68,6},{69,7},{70,8},{71,9},{72,10},{7... | collective-permute-start | bytes 393224 | tf_op jit(solution)/shard_map/ppermute | solution.py:409
  112.9 4.0 %collective-permute-start.21 = (bf16[32,40,256]{2,1,0:T(8,128)(2,1)S(1)}, bf16[32,40,256]{2,1,0:T(8,128)(2,1)S(1)}, u32[]{:S(2)}, u32[]{:S(2)}) collective-permute-start(bf16[32,40,256]{2,1,0:T(8,128)(2,1)S(1)} %get-tuple-element.68), channel_id=1, source_target_pairs={{0,1},{1,0},{2,3},{3,2},{4,5},{5,4},{6,7},{7,6},{8,9},{9,8},{10,11... | collective-permute-start | bytes 1966088 | tf_op jit(solution)/shard_map/ppermute | solution.py:424
  117.9 28.0 %all-to-all-start.1 = ((bf16[32,40,256]{2,1,0:T(8,128)(2,1)}), bf16[32,40,256]{2,1,0:T(8,128)(2,1)S(1)}, u32[]{:S(2)}, u32[]{:S(2)}) async-start(bf16[32,40,256]{2,1,0:T(8,128)(2,1)} %shard_map.108), calls=%async_computation.1 | async-start | bytes 1310720 | tf_op jit(solution)/shard_map/all_to_all | solution.py:441
  124.9 3.1 %collective-permute-start.19 = (bf16[128,256]{1,0:T(8,128)(2,1)S(1)}, bf16[128,256]{1,0:T(8,128)(2,1)S(1)}, u32[]{:S(2)}, u32[]{:S(2)}) collective-permute-start(bf16[128,256]{1,0:T(8,128)(2,1)S(1)} %get-tuple-element.65), channel_id=1, source_target_pairs={{0,1},{1,0},{2,3},{3,2},{4,5},{5,4},{6,7},{7,6},{8,9},{9,8},{10,11... | collective-permute-start | bytes 196616 | tf_op jit(solution)/shard_map/ppermute | solution.py:425
  126.8 1.2 collective-permute-start.20
  (6 other events, 97.9 us)

commit v5 on v4

--- a/solution.py
+++ b/solution.py
@@ -80,15 +80,22 @@
         target[2 * COLS :] = marks.astype(BF)
 
 
-def arrange_kernel(keep, got, block, both, first):
+def arrange_kernel(keep, got, block, up, down, first):
     core = lax.axis_index("c")
 
     def place(one, two):
-        for j, rows in enumerate((one, two)):
-            block[j * COLS : (j + 1) * COLS] = rows[:COLS]
-            both[j * COLS : (j + 1) * COLS] = rows[:COLS]
-            block[(2 + j) * COLS : (3 + j) * COLS] = rows[COLS : 2 * COLS]
-            block[4 * COLS + j * TILE : 4 * COLS + (j + 1) * TILE] = rows[2 * COLS :]
+        block[:COLS] = one[:COLS]
+        block[COLS : 2 * COLS] = two[:COLS]
+        block[2 * COLS : 3 * COLS] = one[COLS : 2 * COLS]
+        block[3 * COLS : 4 * COLS] = two[COLS : 2 * COLS]
+        block[4 * COLS : 4 * COLS + TILE] = one[2 * COLS :]
+        block[4 * COLS + TILE :] = two[2 * COLS :]
+        for target in (up, down):
+            target[:COLS] = one[:COLS]
+            target[COLS : 2 * COLS] = two[:COLS]
+        down[2 * COLS : 3 * COLS] = one[COLS : 2 * COLS]
+        down[3 * COLS : 4 * COLS] = two[COLS : 2 * COLS]
+        down[4 * COLS :] = one[2 * COLS :]
         first[...] = one[:COLS]
 
     @pl.when(core == 0)
@@ -102,13 +109,13 @@
 
 def position():
     chip = lax.axis_index("x") * lax.axis_size("z") + lax.axis_index("z")
-    odd = lax.axis_index("y") % 2 == 1
-    return chip, odd
+    shifted = lax.axis_index("y") % 2 == 1
+    return chip, shifted
 
 
 def keep_factor(chips):
-    chip, odd = position()
-    return jnp.where(odd & (chip == chips - 1), 0.0, 1.0).astype(BF)
+    chip, shifted = position()
+    return jnp.where(shifted & (chip == chips - 1), 0.0, 1.0).astype(BF)
 
 
 def prep_kernel(mine, other, bias, block, before, after, second, deriv, weights, x6, mask):
@@ -130,8 +137,8 @@
     def _():
         assemble(other, mine)
 
-    chip, odd = position()
-    even = jnp.logical_not(odd)
+    chip, shifted = position()
+    aligned = jnp.logical_not(shifted)
     last = GROUPS - 1
 
     def rows(ref, j):
@@ -141,23 +148,23 @@
     next0, next1 = rows(after, 0), rows(after, 1)
     prev0, prev1 = rows(before, 0), rows(before, 1)
     zero = jnp.zeros((COLS, CH), BF)
-    start = even & (chip == 0)
-    end = even & (chip == last)
-    cut0 = start | (odd & (chip == 0))
-    cut5 = end | (odd & (chip == last - 1))
-    x6[0] = jnp.where(cut0, zero, jnp.where(odd, prev1, prev0))
-    x6[1] = jnp.where(start, zero, jnp.where(odd, own0, prev1))
-    x6[2] = jnp.where(odd, own1, own0)
-    x6[3] = jnp.where(odd, next0, own1)
-    x6[4] = jnp.where(end, zero, jnp.where(odd, next1, next0))
-    x6[5] = jnp.where(cut5, zero, jnp.where(odd, second[...], next1))
+    start = aligned & (chip == 0)
+    end = aligned & (chip == last)
+    cut0 = start | (shifted & (chip == 0))
+    cut5 = end | (shifted & (chip == last - 1))
+    x6[0] = jnp.where(cut0, zero, jnp.where(shifted, prev1, prev0))
+    x6[1] = jnp.where(start, zero, jnp.where(shifted, own0, prev1))
+    x6[2] = jnp.where(shifted, own1, own0)
+    x6[3] = jnp.where(shifted, next0, own1)
+    x6[4] = jnp.where(end, zero, jnp.where(shifted, next1, next0))
+    x6[5] = jnp.where(cut5, zero, jnp.where(shifted, second[...], next1))
 
     own_marks = block[4 * COLS :].astype(F32)
     next_marks = after[4 * COLS :].astype(F32)
     for j in range(2):
         here = own_marks[j * TILE : (j + 1) * TILE]
-        there = own_marks[TILE:] if j == 0 else next_marks[:TILE]
-        marks = jnp.where(odd, there, here)
+        there = own_marks[TILE:] if j == 0 else next_marks
+        marks = jnp.where(shifted, there, here)
         for tile in range(COLS // TILE):
             mask[j * COLS + tile * TILE : j * COLS + (tile + 1) * TILE] = jnp.broadcast_to(
                 marks[tile : tile + 1], (TILE, CH)
@@ -190,18 +197,24 @@
         deriv[r] = value
 
 
-def step_kernel(step, sections, mask, deriv, weights, low, high, state_in, *outs):
+def step_kernel(step, sections, mask, deriv, weights, *refs):
+    arrived, state_in, outs = refs[:2], refs[2], refs[3:]
     state = outs[0]
     state[...] = state_in[...]
 
     @pl.when(lax.axis_index("y") == sections - 1 - step)
     def _():
-        base = 2 * COLS if step == 0 else 0
         keep = keep_factor(GROUPS)
+        if step == 0:
+            block, after = arrived
+            sources = [(block, 2), (block, 3), (after, 2), (after, 3)]
+        else:
+            straight, side = arrived
+            low, high = (side, straight) if step % 2 else (straight, side)
+            sources = [(low, 0), (low, 1), (high, 0), (high, 1)]
         gpre = []
-        for r in range(4):
-            at = base + (r % 2) * COLS
-            upstream = (low if r < 2 else high)[at : at + COLS]
+        for r, (ref, at) in enumerate(sources):
+            upstream = ref[at * COLS : (at + 1) * COLS]
             gpre.append((upstream.astype(F32) * deriv[r]).astype(BF))
         state[0] = gpre[1]
         state[1] = gpre[2]
@@ -234,20 +247,20 @@
 
 def grads_kernel(order, state, got, other, grads):
     core = lax.axis_index("c")
-    _, odd = position()
+    _, shifted = position()
     grads[order[1 - core]] = got[...]
     mine = jnp.where(core == 0, other[...], state[2])
-    grads[order[core]] = jnp.where(odd, mine, state[2 + core])
+    grads[order[core]] = jnp.where(shifted, mine, state[2 + core])
 
 
 def wgrad_kernel(x6, state, mine, theirs, send, spill, total):
     core = lax.axis_index("c")
-    _, odd = position()
-    send[...] = jnp.where(odd == (core == 1), state[3], state[2])
+    _, shifted = position()
+    send[...] = jnp.where(shifted == (core == 1), state[3], state[2])
     spill[...] = state[3]
     keep = keep_factor(GROUPS)
     g = [state[j].astype(F32) for j in range(2)]
-    shifted = [
+    moved = [
         jnp.concatenate([from_right(g[0]), from_right(g[1])], axis=0).astype(BF),
         jnp.concatenate([state[0], state[1]], axis=0),
         jnp.concatenate([from_left(g[0]), from_left(g[1])], axis=0).astype(BF),
@@ -261,7 +274,7 @@
         for b in range(3):
             tap = (3 * a + b) * CH
             total[tap : tap + CH] = lax.dot_general(
-                x, shifted[b], (((0,), (0,)), ((), ())), preferred_element_type=F32
+                x, moved[b], (((0,), (0,)), ((), ())), preferred_element_type=F32
             )
     bias = jnp.sum(g[0] + g[1], axis=0, keepdims=True)
     high = bias.astype(BF).astype(F32)
@@ -302,7 +315,10 @@
     value = parts[0].astype(F32)
     for k in range(1, GROUPS):
         value = value + parts[k].astype(F32)
-    wgrad[...] = jnp.where(core == 0, value[:PART], value[WIN - PART :])
+    result = jnp.where(core == 0, value[:PART], value[WIN - PART :])
+    half = CH // 2
+    for j in range(2):
+        wgrad[pl.ds(j, PART, stride=2), :] = result[:, j * half : (j + 1) * half]
     row = lax.broadcasted_iota(jnp.int32, (WIN, CH), 0)
     at = jnp.where(core == 0, PART, 0)
     here = (row == at) | (row == at + 1)
@@ -338,7 +354,7 @@
 def body(saved_inputs, weights, biases, cotangent, tile_list, tile_count, order):
     sections = lax.axis_size("y")
     every = range(sections)
-    odds = range(1, sections, 2)
+    shifts = range(1, sections, 2)
     image = (2, COLS, CH)
     inputs = saved_inputs.reshape(image)
     cot = cotangent.reshape(image)
@@ -358,21 +374,22 @@
         moved=3 << 20,
     )
     got = lax.ppermute(send, "c", swap)
-    block, both, first = call(
+    block, up, down, first = call(
         arrange_kernel,
         [VMEM] * 2,
         [
             out((4 * COLS + 2 * TILE, CH), BF),
             out((2 * COLS, CH), BF),
+            out((4 * COLS + TILE, CH), BF),
             out((COLS, CH), BF),
         ],
         (keep, got),
         flops=1 << 26,
         moved=1 << 20,
     )
-    after = lax.ppermute(block, ALL, chip_pairs(every, -1))
-    before = lax.ppermute(both, ALL, chip_pairs(every, 1))
-    second = lax.ppermute(first, ALL, chip_pairs(odds, -2))
+    after = lax.ppermute(down, ALL, chip_pairs(every, -1))
+    before = lax.ppermute(up, ALL, chip_pairs(every, 1))
+    second = lax.ppermute(first, ALL, chip_pairs(shifts, -2))
     mine, after, before, second = lax.optimization_barrier((mine, after, before, second))
     other = lax.ppermute(mine, "c", swap)
 
@@ -390,27 +407,23 @@
         moved=4 << 20,
     )
 
-    low, high = block, after
+    arrived = [block, after]
     for step in range(sections):
         live = step < sections - 1
         state, *back = call(
             lambda *refs, step=step: step_kernel(step, sections, *refs),
-            [VMEM] * 6,
+            [VMEM] * (4 + len(arrived)),
             [out((4, COLS, CH), BF)] + [out((2 * COLS, CH), BF)] * live,
-            (mask, deriv, wfull, low, high, state),
-            aliases={5: 0},
+            (mask, deriv, wfull, *arrived, state),
+            aliases={3 + len(arrived): 0},
             flops=1 << 27,
             moved=2 << 20,
         )
         if live:
             plane = sections - 1 - step
             straight = lax.ppermute(back[0], ALL, chip_pairs([plane], 0, 1))
-            if plane % 2:
-                side = lax.ppermute(back[0], ALL, chip_pairs([plane], 1, 1))
-                low, high = side, straight
-            else:
-                side = lax.ppermute(back[0], ALL, chip_pairs([plane], -1, 1))
-                low, high = straight, side
+            side = lax.ppermute(back[0], ALL, chip_pairs([plane], 1 if plane % 2 else -1, 1))
+            arrived = [straight, side]
 
     mine, theirs, send, spill = call(
         wgrad_kernel,
@@ -423,7 +436,7 @@
     )
     received = lax.ppermute(theirs, "c", swap)
     got = lax.ppermute(send, ALL, return_pairs(sections))
-    spilled = lax.ppermute(spill, ALL, chip_pairs(odds, 1))
+    spilled = lax.ppermute(spill, ALL, chip_pairs(shifts, 1))
     (grads,) = call(
         grads_kernel,
         [SMEM] + [VMEM] * 3,
@@ -442,11 +455,11 @@
     wgrad, bgrad = call(
         total_kernel,
         [VMEM],
-        [out((PART, CH), F32), out((1, 4), F32)],
+        [out((2 * PART, CH // 2), F32), out((1, 4), F32)],
         (parts,),
         moved=1 << 20,
     )
-    return grads.reshape(1, 2, 1, COLS, CH), wgrad[None], bgrad
+    return grads.reshape(1, 2, 1, COLS, CH), wgrad.reshape(1, PART, CH), bgrad
 
 
 def solution(mesh):

time: 148 us -> 142 us (0.959)
  waiting for transfers between devices: 91.6 us -> 86.1 us
    ppermute x7, waiting for transfers between devices: 54 us -> 0.02 us  [body(): straight = lax.ppermute(back[0], ALL, chip_pairs([plane], 0, 1))]
    ppermute x11, waiting for transfers between devices: 14.9 us -> 63.4 us  [the longest x7 53 us: body(): lax.ppermute(back[0], ALL, chip_pairs([plane], 1 if plane % 2 else -1, 1))]
  transfers between devices with their start and end apart: 24 -> 24, of which waited for: 9 -> 8; matrix products, arithmetic and copies ran while one was open for 0% -> 0% of each run, Pallas kernels for 1% -> 1%
where the time goes in v5:
time: 142 us; the launch traced here: 141 us
  waiting for transfers between devices  86.1 us (61%)
  starting transfers between devices  45.1 us (32%)
  Pallas kernels  7.48 us (5%)
  between operations  1.73 us (1%)
    ppermute x7, waiting for transfers between devices, body(): lax.ppermute(back[0], ALL, chip_pairs([plane], 1 if plane % 2 else -1, 1))  53 us
    all_to_all x1, waiting for transfers between devices, body(): parts = lax.all_to_all(both, ('x', 'z'), 0, 0)  16.7 us
    all_to_all x1, starting transfers between devices, body(): mine = lax.all_to_all(wide, ('x', 'z'), 0, 0)  12.7 us
    pallas_call x16, Pallas kernels, call(): pl.pallas_call(kernel, out_shape=outs, in_specs=ins, out_specs=[VMEM] * l...  7.48 us
    all_to_all x1, starting transfers between devices, body(): parts = lax.all_to_all(both, ('x', 'z'), 0, 0)  6.93 us
    ppermute x1, waiting for transfers between devices, body(): before = lax.ppermute(up, ALL, chip_pairs(every, 1))  6.84 us
    ppermute x7, starting transfers between devices, body(): lax.ppermute(back[0], ALL, chip_pairs([plane], 1 if plane % 2 else -1, 1))  5.31 us
    ppermute x7, starting transfers between devices, body(): straight = lax.ppermute(back[0], ALL, chip_pairs([plane], 0, 1))  5.31 us
  transfers between devices with their start and end apart: 24, of which 8 were waited for; matrix products, arithmetic and copies ran while one was open for 0% of the time, Pallas kernels for 1%

profile of v5, /device:TPU:64, one launch (start us, length us, event | category | flops | bytes accessed | tf_op | source)
XLA Modules:
  0.0 141.1 jit_solution(13987004719220916155)
XLA Ops:
  0.7 0.7 copy-done
  1.4 0.9 shard_map.94
  2.3 12.7 %all-to-all-start = ((bf16[32,40,256]{2,1,0:T(8,128)(2,1)}), bf16[32,40,256]{2,1,0:T(8,128)(2,1)S(1)}, u32[]{:S(2)}, u32[]{:S(2)}) async-start(bf16[32,40,256]{2,1,0:T(8,128)(2,1)} %shard_map.94), calls=%async_computation | async-start | bytes 1310720 | tf_op jit(solution)/shard_map/all_to_all | solution.py:366
  16.3 1.9 %collective-permute-start = (bf16[272,256]{1,0:T(8,128)(2,1)S(1)}, bf16[272,256]{1,0:T(8,128)(2,1)S(1)}, u32[]{:S(2)}, u32[]{:S(2)}) collective-permute-start(bf16[272,256]{1,0:T(8,128)(2,1)S(1)} %get-tuple-element.39), channel_id=1, source_target_pairs={{0,1},{1,0},{2,3},{3,2},{4,5},{5,4},{6,7},{7,6},{8,9},{9,8},{10,11... | collective-permute-start | bytes 417800 | tf_op jit(solution)/shard_map/ppermute | solution.py:376
  18.3 1.3 collective-permute-done.got
  19.6 2.1 %collective-permute-start.1 = (bf16[528,256]{1,0:T(8,128)(2,1)S(1)}, bf16[528,256]{1,0:T(8,128)(2,1)S(1)}, u32[]{:S(2)}, u32[]{:S(2)}) collective-permute-start(bf16[528,256]{1,0:T(8,128)(2,1)S(1)} %get-tuple-element.40), channel_id=1, source_target_pairs={{0,62},{1,63},{2,0},{3,1},{4,2},{5,3},{6,4},{7,5},{8,6},{9,7},{10,... | collective-permute-start | bytes 811016 | tf_op jit(solution)/shard_map/ppermute | solution.py:390
  21.8 3.7 %collective-permute-start.2 = (bf16[256,256]{1,0:T(8,128)(2,1)S(1)}, bf16[256,256]{1,0:T(8,128)(2,1)S(1)}, u32[]{:S(2)}, u32[]{:S(2)}) collective-permute-start(bf16[256,256]{1,0:T(8,128)(2,1)S(1)} %get-tuple-element.41), channel_id=1, source_target_pairs={{0,2},{1,3},{2,4},{3,5},{4,6},{5,7},{6,8},{7,9},{8,10},{9,11},{10,... | collective-permute-start | bytes 393224 | tf_op jit(solution)/shard_map/ppermute | solution.py:391
  26.2 6.8 %collective-permute-done.2.before = bf16[256,256]{1,0:T(8,128)(2,1)S(1)} collective-permute-done((bf16[256,256]{1,0:T(8,128)(2,1)S(1)}, bf16[256,256]{1,0:T(8,128)(2,1)S(1)}, u32[]{:S(2)}, u32[]{:S(2)}) %collective-permute-start.2) | collective-permute-done | bytes 131104 | tf_op jit(solution)/shard_map/ppermute | solution.py:391
  33.0 3.6 %collective-permute-done.1.after.refs_4_ = bf16[528,256]{1,0:T(8,128)(2,1)S(1)} collective-permute-done((bf16[528,256]{1,0:T(8,128)(2,1)S(1)}, bf16[528,256]{1,0:T(8,128)(2,1)S(1)}, u32[]{:S(2)}, u32[]{:S(2)}) %collective-permute-start.1) | collective-permute-done | bytes 270368 | tf_op jit(solution)/shard_map/ppermute | solution.py:390
  36.6 1.9 %collective-permute-start.4 = (bf16[32,40,256]{2,1,0:T(8,128)(2,1)S(1)}, bf16[32,40,256]{2,1,0:T(8,128)(2,1)S(1)}, u32[]{:S(2)}, u32[]{:S(2)}) collective-permute-start(bf16[32,40,256]{2,1,0:T(8,128)(2,1)S(1)} %all-to-all-done.mine), channel_id=1, source_target_pairs={{0,1},{1,0},{2,3},{3,2},{4,5},{5,4},{6,7},{7,6},{8,9},{9,8},{10,11... | collective-permute-start | bytes 1966088 | tf_op jit(solution)/shard_map/ppermute | solution.py:394
  38.5 2.1 %collective-permute-done.4.other = bf16[32,40,256]{2,1,0:T(8,128)(2,1)S(1)} collective-permute-done((bf16[32,40,256]{2,1,0:T(8,128)(2,1)S(1)}, bf16[32,40,256]{2,1,0:T(8,128)(2,1)S(1)}, u32[]{:S(2)}, u32[]{:S(2)}) %collective-permute-start.4) | collective-permute-done | bytes 655392 | tf_op jit(solution)/shard_map/ppermute | solution.py:394
  40.6 1.0 shard_map.97
  50.2 1.3 collective-permute-start.18
  51.5 1.3 collective-permute-start.17
  52.8 52.9 %collective-permute-done.18.refs_4_ = bf16[256,256]{1,0:T(8,128)(2,1)S(1)} collective-permute-done((bf16[256,256]{1,0:T(8,128)(2,1)S(1)}, bf16[256,256]{1,0:T(8,128)(2,1)S(1)}, u32[]{:S(2)}, u32[]{:S(2)}) %collective-permute-start.18) | collective-permute-done | bytes 131104 | tf_op jit(solution)/shard_map/ppermute | solution.py:425
  106.3 1.1 shard_map.106
  107.4 1.9 %collective-permute-start.21 = (bf16[32,40,256]{2,1,0:T(8,128)(2,1)S(1)}, bf16[32,40,256]{2,1,0:T(8,128)(2,1)S(1)}, u32[]{:S(2)}, u32[]{:S(2)}) collective-permute-start(bf16[32,40,256]{2,1,0:T(8,128)(2,1)S(1)} %get-tuple-element.70), channel_id=1, source_target_pairs={{0,1},{1,0},{2,3},{3,2},{4,5},{5,4},{6,7},{7,6},{8,9},{9,8},{10,11... | collective-permute-start | bytes 1966088 | tf_op jit(solution)/shard_map/ppermute | solution.py:437
  109.3 2.1 %collective-permute-done.21.got = bf16[32,40,256]{2,1,0:T(8,128)(2,1)S(1)} collective-permute-done((bf16[32,40,256]{2,1,0:T(8,128)(2,1)S(1)}, bf16[32,40,256]{2,1,0:T(8,128)(2,1)S(1)}, u32[]{:S(2)}, u32[]{:S(2)}) %collective-permute-start.21) | collective-permute-done | bytes 655392 | tf_op jit(solution)/shard_map/ppermute | solution.py:437
  111.4 1.0 shard_map.108
  112.4 6.9 %all-to-all-start.1 = ((bf16[32,40,256]{2,1,0:T(8,128)(2,1)}), bf16[32,40,256]{2,1,0:T(8,128)(2,1)S(1)}, u32[]{:S(2)}, u32[]{:S(2)}) async-start(bf16[32,40,256]{2,1,0:T(8,128)(2,1)} %shard_map.108), calls=%async_computation.1 | async-start | bytes 1310720 | tf_op jit(solution)/shard_map/all_to_all | solution.py:454
  119.4 1.9 %collective-permute-start.19 = (bf16[128,256]{1,0:T(8,128)(2,1)S(1)}, bf16[128,256]{1,0:T(8,128)(2,1)S(1)}, u32[]{:S(2)}, u32[]{:S(2)}) collective-permute-start(bf16[128,256]{1,0:T(8,128)(2,1)S(1)} %get-tuple-element.67), channel_id=1, source_target_pairs={{0,1},{1,0},{2,3},{3,2},{4,5},{5,4},{6,7},{7,6},{8,9},{9,8},{10,11... | collective-permute-start | bytes 196616 | tf_op jit(solution)/shard_map/ppermute | solution.py:438
  122.5 1.2 shard_map.107
  123.7 16.7 %all-to-all-done.1.parts = bf16[32,40,256]{2,1,0:T(8,128)(2,1)S(1)} async-done(((bf16[32,40,256]{2,1,0:T(8,128)(2,1)}), bf16[32,40,256]{2,1,0:T(8,128)(2,1)S(1)}, u32[]{:S(2)}, u32[]{:S(2)}) %all-to-all-start.1) | async-done | bytes 655392 | tf_op jit(solution)/shard_map/all_to_all | solution.py:454
  140.4 0.7 shard_map.109
  (52 shorter events, 11.6 us)
Async XLA Ops:
  2.3 34.3 %all-to-all-start = ((bf16[32,40,256]{2,1,0:T(8,128)(2,1)}), bf16[32,40,256]{2,1,0:T(8,128)(2,1)S(1)}, u32[]{:S(2)}, u32[]{:S(2)}) async-start(bf16[32,40,256]{2,1,0:T(8,128)(2,1)} %shard_map.94), calls=%async_computation | async-start | bytes 1310720 | tf_op jit(solution)/shard_map/all_to_all | solution.py:366
  16.3 3.3 %collective-permute-start = (bf16[272,256]{1,0:T(8,128)(2,1)S(1)}, bf16[272,256]{1,0:T(8,128)(2,1)S(1)}, u32[]{:S(2)}, u32[]{:S(2)}) collective-permute-start(bf16[272,256]{1,0:T(8,128)(2,1)S(1)} %get-tuple-element.39), channel_id=1, source_target_pairs={{0,1},{1,0},{2,3},{3,2},{4,5},{5,4},{6,7},{7,6},{8,9},{9,8},{10,11... | collective-permute-start | bytes 417800 | tf_op jit(solution)/shard_map/ppermute | solution.py:376
  19.6 17.0 %collective-permute-start.1 = (bf16[528,256]{1,0:T(8,128)(2,1)S(1)}, bf16[528,256]{1,0:T(8,128)(2,1)S(1)}, u32[]{:S(2)}, u32[]{:S(2)}) collective-permute-start(bf16[528,256]{1,0:T(8,128)(2,1)S(1)} %get-tuple-element.40), channel_id=1, source_target_pairs={{0,62},{1,63},{2,0},{3,1},{4,2},{5,3},{6,4},{7,5},{8,6},{9,7},{10,... | collective-permute-start | bytes 811016 | tf_op jit(solution)/shard_map/ppermute | solution.py:390
  21.8 11.2 %collective-permute-start.2 = (bf16[256,256]{1,0:T(8,128)(2,1)S(1)}, bf16[256,256]{1,0:T(8,128)(2,1)S(1)}, u32[]{:S(2)}, u32[]{:S(2)}) collective-permute-start(bf16[256,256]{1,0:T(8,128)(2,1)S(1)} %get-tuple-element.41), channel_id=1, source_target_pairs={{0,2},{1,3},{2,4},{3,5},{4,6},{5,7},{6,8},{7,9},{8,10},{9,11},{10,... | collective-permute-start | bytes 393224 | tf_op jit(solution)/shard_map/ppermute | solution.py:391
  25.5 0.7 collective-permute-start.3
  36.6 4.0 %collective-permute-start.4 = (bf16[32,40,256]{2,1,0:T(8,128)(2,1)S(1)}, bf16[32,40,256]{2,1,0:T(8,128)(2,1)S(1)}, u32[]{:S(2)}, u32[]{:S(2)}) collective-permute-start(bf16[32,40,256]{2,1,0:T(8,128)(2,1)S(1)} %all-to-all-done.mine), channel_id=1, source_target_pairs={{0,1},{1,0},{2,3},{3,2},{4,5},{5,4},{6,7},{7,6},{8,9},{9,8},{10,11... | collective-permute-start | bytes 1966088 | tf_op jit(solution)/shard_map/ppermute | solution.py:394
  41.6 1.4 collective-permute-start.6
  42.3 0.7 collective-permute-start.5
  43.0 1.4 collective-permute-start.8
  43.7 0.7 collective-permute-start.7
  44.5 1.4 collective-permute-start.10
  45.2 0.7 collective-permute-start.9
  45.9 1.4 collective-permute-start.12
  46.6 0.7 collective-permute-start.11
  47.3 1.4 collective-permute-start.14
  48.0 0.7 collective-permute-start.13
  48.8 1.4 collective-permute-start.16
  49.4 0.7 collective-permute-start.15
  50.2 55.5 %collective-permute-start.18 = (bf16[256,256]{1,0:T(8,128)(2,1)S(1)}, bf16[256,256]{1,0:T(8,128)(2,1)S(1)}, u32[]{:S(2)}, u32[]{:S(2)}) collective-permute-start(bf16[256,256]{1,0:T(8,128)(2,1)S(1)} %get-tuple-element.64), channel_id=1, source_target_pairs={{64,2},{65,3},{66,4},{67,5},{68,6},{69,7},{70,8},{71,9},{72,10},{7... | collective-permute-start | bytes 393224 | tf_op jit(solution)/shard_map/ppermute | solution.py:425
  51.5 54.2 %collective-permute-start.17 = (bf16[256,256]{1,0:T(8,128)(2,1)S(1)}, bf16[256,256]{1,0:T(8,128)(2,1)S(1)}, u32[]{:S(2)}, u32[]{:S(2)}) collective-permute-start(bf16[256,256]{1,0:T(8,128)(2,1)S(1)} %get-tuple-element.64), channel_id=1, source_target_pairs={{64,0},{65,1},{66,2},{67,3},{68,4},{69,5},{70,6},{71,7},{72,8},{73... | collective-permute-start | bytes 393224 | tf_op jit(solution)/shard_map/ppermute | solution.py:424
  107.4 4.0 %collective-permute-start.21 = (bf16[32,40,256]{2,1,0:T(8,128)(2,1)S(1)}, bf16[32,40,256]{2,1,0:T(8,128)(2,1)S(1)}, u32[]{:S(2)}, u32[]{:S(2)}) collective-permute-start(bf16[32,40,256]{2,1,0:T(8,128)(2,1)S(1)} %get-tuple-element.70), channel_id=1, source_target_pairs={{0,1},{1,0},{2,3},{3,2},{4,5},{5,4},{6,7},{7,6},{8,9},{9,8},{10,11... | collective-permute-start | bytes 1966088 | tf_op jit(solution)/shard_map/ppermute | solution.py:437
  112.4 28.0 %all-to-all-start.1 = ((bf16[32,40,256]{2,1,0:T(8,128)(2,1)}), bf16[32,40,256]{2,1,0:T(8,128)(2,1)S(1)}, u32[]{:S(2)}, u32[]{:S(2)}) async-start(bf16[32,40,256]{2,1,0:T(8,128)(2,1)} %shard_map.108), calls=%async_computation.1 | async-start | bytes 1310720 | tf_op jit(solution)/shard_map/all_to_all | solution.py:454
  119.4 3.1 %collective-permute-start.19 = (bf16[128,256]{1,0:T(8,128)(2,1)S(1)}, bf16[128,256]{1,0:T(8,128)(2,1)S(1)}, u32[]{:S(2)}, u32[]{:S(2)}) collective-permute-start(bf16[128,256]{1,0:T(8,128)(2,1)S(1)} %get-tuple-element.67), channel_id=1, source_target_pairs={{0,1},{1,0},{2,3},{3,2},{4,5},{5,4},{6,7},{7,6},{8,9},{9,8},{10,11... | collective-permute-start | bytes 196616 | tf_op jit(solution)/shard_map/ppermute | solution.py:438
  121.3 1.2 collective-permute-start.20
  (6 other events, 97.7 us)

commit v6 on v5

--- a/solution.py
+++ b/solution.py
@@ -118,7 +118,7 @@
     return jnp.where(shifted & (chip == chips - 1), 0.0, 1.0).astype(BF)
 
 
-def prep_kernel(mine, other, bias, block, before, after, second, deriv, weights, x6, mask):
+def prep_kernel(mine, other, bias, block, before, after, second, deriv, weights, x4, mask, x6):
     core = lax.axis_index("c")
 
     def assemble(even, odd):
@@ -170,6 +170,8 @@
                 marks[tile : tile + 1], (TILE, CH)
             )
 
+    for j in range(4):
+        x4[j] = x6[1 + j]
     keep = keep_factor(GROUPS)
     lhs = [
         jnp.concatenate([x6[0], x6[1], x6[2] * keep, x6[3]], axis=0),
@@ -241,8 +243,12 @@
             value = from_right(sums[0][part]) + sums[1][part] + from_left(sums[2][part])
             value = (value * mask[part]).astype(BF)
             state[2 + j] = value
-            if len(outs) > 1:
+            if step < sections - 1:
                 outs[1][part] = value
+
+    if step == sections - 1:
+        for j in range(2):
+            outs[1][j * COLS : (j + 1) * COLS] = state[j]
 
 
 def grads_kernel(order, state, got, other, grads):
@@ -253,22 +259,24 @@
     grads[order[core]] = jnp.where(shifted, mine, state[2 + core])
 
 
-def wgrad_kernel(x6, state, mine, theirs, send, spill, total):
+def wgrad_kernel(x_own, x_other, state, g_other, parts, send, spill, total):
     core = lax.axis_index("c")
     _, shifted = position()
     send[...] = jnp.where(shifted == (core == 1), state[3], state[2])
     spill[...] = state[3]
     keep = keep_factor(GROUPS)
-    g = [state[j].astype(F32) for j in range(2)]
+    rows = [state[0], state[1], g_other[:COLS], g_other[COLS:]]
+    g = [value.astype(F32) for value in rows]
     moved = [
-        jnp.concatenate([from_right(g[0]), from_right(g[1])], axis=0).astype(BF),
-        jnp.concatenate([state[0], state[1]], axis=0),
-        jnp.concatenate([from_left(g[0]), from_left(g[1])], axis=0).astype(BF),
+        jnp.concatenate([from_right(value) for value in g], axis=0).astype(BF),
+        jnp.concatenate(rows, axis=0),
+        jnp.concatenate([from_left(value) for value in g], axis=0).astype(BF),
     ]
+    pairs = (x_own, x_other)
     lhs = [
-        jnp.concatenate([x6[1], x6[2] * keep], axis=0),
-        jnp.concatenate([x6[2], x6[3]], axis=0),
-        jnp.concatenate([x6[3] * keep, x6[4]], axis=0),
+        jnp.concatenate([v for x in pairs for v in (x[0], x[1] * keep)], axis=0),
+        jnp.concatenate([v for x in pairs for v in (x[1], x[2])], axis=0),
+        jnp.concatenate([v for x in pairs for v in (x[2] * keep, x[3])], axis=0),
     ]
     for a, x in enumerate(lhs):
         for b in range(3):
@@ -276,37 +284,15 @@
             total[tap : tap + CH] = lax.dot_general(
                 x, moved[b], (((0,), (0,)), ((), ())), preferred_element_type=F32
             )
-    bias = jnp.sum(g[0] + g[1], axis=0, keepdims=True)
+    bias = jnp.sum((g[0] + g[1]) + (g[2] + g[3]), axis=0, keepdims=True)
     high = bias.astype(BF).astype(F32)
-    low = (bias - high).astype(BF).astype(F32)
-    row = lax.broadcasted_iota(jnp.int32, (WIN, CH), 0)
-
-    def window(which, start):
-        at = jnp.where(which == 0, PART, 0)
-        return total[pl.ds(pl.multiple_of(start, 8), WIN), :], at
-
-    for k in range(GROUPS):
-        value, at = window(core, 72 * k + 32 * core)
-        value = jnp.where(row == at, bias, value)
-        mine[k] = jnp.where(row == at + 1, 0.0, value)
-        value, at = window(1 - core, 72 * k + 32 * (1 - core))
-        value = jnp.where(row == at, high, value)
-        theirs[k] = jnp.where(row == at + 1, low, value).astype(BF)
-
-
-def pair_kernel(mine, got, both):
-    core = lax.axis_index("c")
+    low = bias - high
     row = lax.broadcasted_iota(jnp.int32, (WIN, CH), 0)
     at = jnp.where(core == 0, PART, 0)
-    lead = mine[0] + got[0].astype(F32)
-    here = (row == at) | (row == at + 1)
-    bias = jnp.sum(jnp.where(here, lead, 0.0), axis=0, keepdims=True)
-    high = bias.astype(BF).astype(F32)
-    low = bias - high
     for k in range(GROUPS):
-        value = mine[k] + got[k].astype(F32)
+        value = total[pl.ds(pl.multiple_of(72 * k + 32 * core, 8), WIN), :]
         value = jnp.where(row == at, high, value)
-        both[k] = jnp.where(row == at + 1, low, value).astype(BF)
+        parts[k] = jnp.where(row == at + 1, low, value).astype(BF)
 
 
 def total_kernel(parts, wgrad, bgrad):
@@ -393,16 +379,17 @@
     mine, after, before, second = lax.optimization_barrier((mine, after, before, second))
     other = lax.ppermute(mine, "c", swap)
 
-    deriv, wfull, x6, mask = call(
+    deriv, wfull, x4, mask = call(
         prep_kernel,
         [VMEM] * 7,
         [
             out((4, COLS, CH), F32),
             out((9 * CH, CH), BF),
-            out((6, COLS, CH), BF),
+            out((4, COLS, CH), BF),
             out((2 * COLS, CH), F32),
         ],
         (mine, other, biases, block, before, after, second),
+        scratch=[pltpu.VMEM((6, COLS, CH), BF)],
         flops=1 << 30,
         moved=4 << 20,
     )
@@ -410,10 +397,10 @@
     arrived = [block, after]
     for step in range(sections):
         live = step < sections - 1
-        state, *back = call(
+        state, back = call(
             lambda *refs, step=step: step_kernel(step, sections, *refs),
             [VMEM] * (4 + len(arrived)),
-            [out((4, COLS, CH), BF)] + [out((2 * COLS, CH), BF)] * live,
+            [out((4, COLS, CH), BF), out((2 * COLS, CH), BF)],
             (mask, deriv, wfull, *arrived, state),
             aliases={3 + len(arrived): 0},
             flops=1 << 27,
@@ -421,20 +408,23 @@
         )
         if live:
             plane = sections - 1 - step
-            straight = lax.ppermute(back[0], ALL, chip_pairs([plane], 0, 1))
-            side = lax.ppermute(back[0], ALL, chip_pairs([plane], 1 if plane % 2 else -1, 1))
+            straight = lax.ppermute(back, ALL, chip_pairs([plane], 0, 1))
+            side = lax.ppermute(back, ALL, chip_pairs([plane], 1 if plane % 2 else -1, 1))
             arrived = [straight, side]
-
-    mine, theirs, send, spill = call(
+        if step == 2:
+            late, _ = lax.optimization_barrier((x4, back))
+            x_other = lax.ppermute(late, "c", swap)
+
+    g_other = lax.ppermute(back, "c", swap)
+    both, send, spill = call(
         wgrad_kernel,
-        [VMEM] * 2,
-        [out((GROUPS, WIN, CH), F32), out((GROUPS, WIN, CH), BF)] + [out((COLS, CH), BF)] * 2,
-        (x6, state),
+        [VMEM] * 4,
+        [out((GROUPS, WIN, CH), BF)] + [out((COLS, CH), BF)] * 2,
+        (x4, x_other, state, g_other),
         scratch=[pltpu.VMEM((9 * CH, CH), F32)],
         flops=1 << 28,
         moved=4 << 20,
     )
-    received = lax.ppermute(theirs, "c", swap)
     got = lax.ppermute(send, ALL, return_pairs(sections))
     spilled = lax.ppermute(spill, ALL, chip_pairs(shifts, 1))
     (grads,) = call(
@@ -443,13 +433,6 @@
         [out(image, BF)],
         (order, state, got, spilled),
         moved=1 << 18,
-    )
-    (both,) = call(
-        pair_kernel,
-        [VMEM] * 2,
-        [out((GROUPS, WIN, CH), BF)],
-        (mine, received),
-        moved=3 << 20,
     )
     parts = lax.all_to_all(both, ("x", "z"), 0, 0)
     wgrad, bgrad = call(

time: 142 us -> 141 us (level)
  waiting for transfers between devices: 86.1 us -> 83.3 us
  starting transfers between devices: 45.1 us -> 47.1 us
    ppermute x15 -> x16, waiting for transfers between devices: 55 us -> 52.2 us  [the longest x7 50.9 us: body(): lax.ppermute(back, ALL, chip_pairs([plane], 1 if plane % 2 else -1, 1))]
    ppermute x15 -> x16, starting transfers between devices: 12.5 us -> 14.6 us  [the longest x7 5.31 us: body(): lax.ppermute(back, ALL, chip_pairs([plane], 1 if plane % 2 else -1, 1))]
    pallas_call x16 -> x15, Pallas kernels: 7.48 us -> 7.39 us  [call(): pl.pallas_call(kernel, out_shape=outs, in_specs=ins, out_specs=[VMEM] * l...]
  transfers between devices with their start and end apart: 24 -> 25, of which waited for: 8 -> 8; matrix products, arithmetic and copies ran while one was open for 0% -> 0% of each run, Pallas kernels for 1% -> 2%
where the time goes in v6:
time: 141 us; the launch traced here: 140 us
  waiting for transfers between devices  83.3 us (59%)
  starting transfers between devices  47.1 us (33%)
  Pallas kernels  7.39 us (5%)
  between operations  1.74 us (1%)
    ppermute x7, waiting for transfers between devices, body(): lax.ppermute(back, ALL, chip_pairs([plane], 1 if plane % 2 else -1, 1))  50.9 us
    all_to_all x1, waiting for transfers between devices, body(): parts = lax.all_to_all(both, ('x', 'z'), 0, 0)  16.8 us
    all_to_all x1, starting transfers between devices, body(): mine = lax.all_to_all(wide, ('x', 'z'), 0, 0)  12.7 us
    pallas_call x15, Pallas kernels, call(): pl.pallas_call(kernel, out_shape=outs, in_specs=ins, out_specs=[VMEM] * l...  7.39 us
    all_to_all x1, starting transfers between devices, body(): parts = lax.all_to_all(both, ('x', 'z'), 0, 0)  6.93 us
    ppermute x1, waiting for transfers between devices, body(): before = lax.ppermute(up, ALL, chip_pairs(every, 1))  6.84 us
    ppermute x7, starting transfers between devices, body(): lax.ppermute(back, ALL, chip_pairs([plane], 1 if plane % 2 else -1, 1))  5.31 us
    ppermute x7, starting transfers between devices, body(): straight = lax.ppermute(back, ALL, chip_pairs([plane], 0, 1))  5.31 us
  transfers between devices with their start and end apart: 25, of which 8 were waited for; matrix products, arithmetic and copies ran while one was open for 0% of the time, Pallas kernels for 2%

profile of v6, /device:TPU:64, one launch (start us, length us, event | category | flops | bytes accessed | tf_op | source)
XLA Modules:
  0.0 140.3 jit_solution(12937680545164511249)
XLA Ops:
  0.7 0.7 copy-done
  1.4 0.9 shard_map.94
  2.3 12.7 %all-to-all-start = ((bf16[32,40,256]{2,1,0:T(8,128)(2,1)}), bf16[32,40,256]{2,1,0:T(8,128)(2,1)S(1)}, u32[]{:S(2)}, u32[]{:S(2)}) async-start(bf16[32,40,256]{2,1,0:T(8,128)(2,1)} %shard_map.94), calls=%async_computation | async-start | bytes 1310720 | tf_op jit(solution)/shard_map/all_to_all | solution.py:352
  16.3 1.9 %collective-permute-start = (bf16[272,256]{1,0:T(8,128)(2,1)S(1)}, bf16[272,256]{1,0:T(8,128)(2,1)S(1)}, u32[]{:S(2)}, u32[]{:S(2)}) collective-permute-start(bf16[272,256]{1,0:T(8,128)(2,1)S(1)} %get-tuple-element.41), channel_id=1, source_target_pairs={{0,1},{1,0},{2,3},{3,2},{4,5},{5,4},{6,7},{7,6},{8,9},{9,8},{10,11... | collective-permute-start | bytes 417800 | tf_op jit(solution)/shard_map/ppermute | solution.py:362
  18.3 1.3 collective-permute-done.got
  19.6 2.1 %collective-permute-start.1 = (bf16[528,256]{1,0:T(8,128)(2,1)S(1)}, bf16[528,256]{1,0:T(8,128)(2,1)S(1)}, u32[]{:S(2)}, u32[]{:S(2)}) collective-permute-start(bf16[528,256]{1,0:T(8,128)(2,1)S(1)} %get-tuple-element.42), channel_id=1, source_target_pairs={{0,62},{1,63},{2,0},{3,1},{4,2},{5,3},{6,4},{7,5},{8,6},{9,7},{10,... | collective-permute-start | bytes 811016 | tf_op jit(solution)/shard_map/ppermute | solution.py:376
  21.8 3.7 %collective-permute-start.2 = (bf16[256,256]{1,0:T(8,128)(2,1)S(1)}, bf16[256,256]{1,0:T(8,128)(2,1)S(1)}, u32[]{:S(2)}, u32[]{:S(2)}) collective-permute-start(bf16[256,256]{1,0:T(8,128)(2,1)S(1)} %get-tuple-element.43), channel_id=1, source_target_pairs={{0,2},{1,3},{2,4},{3,5},{4,6},{5,7},{6,8},{7,9},{8,10},{9,11},{10,... | collective-permute-start | bytes 393224 | tf_op jit(solution)/shard_map/ppermute | solution.py:377
  26.2 6.8 %collective-permute-done.2.before = bf16[256,256]{1,0:T(8,128)(2,1)S(1)} collective-permute-done((bf16[256,256]{1,0:T(8,128)(2,1)S(1)}, bf16[256,256]{1,0:T(8,128)(2,1)S(1)}, u32[]{:S(2)}, u32[]{:S(2)}) %collective-permute-start.2) | collective-permute-done | bytes 131104 | tf_op jit(solution)/shard_map/ppermute | solution.py:377
  33.0 3.6 %collective-permute-done.1.after.refs_4_ = bf16[528,256]{1,0:T(8,128)(2,1)S(1)} collective-permute-done((bf16[528,256]{1,0:T(8,128)(2,1)S(1)}, bf16[528,256]{1,0:T(8,128)(2,1)S(1)}, u32[]{:S(2)}, u32[]{:S(2)}) %collective-permute-start.1) | collective-permute-done | bytes 270368 | tf_op jit(solution)/shard_map/ppermute | solution.py:376
  36.6 1.9 %collective-permute-start.4 = (bf16[32,40,256]{2,1,0:T(8,128)(2,1)S(1)}, bf16[32,40,256]{2,1,0:T(8,128)(2,1)S(1)}, u32[]{:S(2)}, u32[]{:S(2)}) collective-permute-start(bf16[32,40,256]{2,1,0:T(8,128)(2,1)S(1)} %all-to-all-done.mine), channel_id=1, source_target_pairs={{0,1},{1,0},{2,3},{3,2},{4,5},{5,4},{6,7},{7,6},{8,9},{9,8},{10,11... | collective-permute-start | bytes 1966088 | tf_op jit(solution)/shard_map/ppermute | solution.py:380
  38.5 2.1 %collective-permute-done.4.other = bf16[32,40,256]{2,1,0:T(8,128)(2,1)S(1)} collective-permute-done((bf16[32,40,256]{2,1,0:T(8,128)(2,1)S(1)}, bf16[32,40,256]{2,1,0:T(8,128)(2,1)S(1)}, u32[]{:S(2)}, u32[]{:S(2)}) %collective-permute-start.4) | collective-permute-done | bytes 655392 | tf_op jit(solution)/shard_map/ppermute | solution.py:380
  40.6 0.9 shard_map.97
  50.2 1.3 collective-permute-start.18
  51.5 1.3 collective-permute-start.17
  52.8 2.0 %collective-permute-start.19 = (bf16[4,128,256]{2,1,0:T(8,128)(2,1)S(1)}, bf16[4,128,256]{2,1,0:T(8,128)(2,1)S(1)}, u32[]{:S(2)}, u32[]{:S(2)}) collective-permute-start(bf16[4,128,256]{2,1,0:T(8,128)(2,1)S(1)} %get-tuple-element.70.x_own), channel_id=1, source_target_pairs={{0,1},{1,0},{2,3},{3,2},{4,5},{5,4},{6,7},{7,6},{8,9},{9,8},{10,11... | collective-permute-start | bytes 786440 | tf_op jit(solution)/shard_map/ppermute | solution.py:416
  54.8 50.9 %collective-permute-done.18.refs_4_ = bf16[256,256]{1,0:T(8,128)(2,1)S(1)} collective-permute-done((bf16[256,256]{1,0:T(8,128)(2,1)S(1)}, bf16[256,256]{1,0:T(8,128)(2,1)S(1)}, u32[]{:S(2)}, u32[]{:S(2)}) %collective-permute-start.18) | collective-permute-done | bytes 131104 | tf_op jit(solution)/shard_map/ppermute | solution.py:412
  106.3 1.9 %collective-permute-start.20 = (bf16[256,256]{1,0:T(8,128)(2,1)S(1)}, bf16[256,256]{1,0:T(8,128)(2,1)S(1)}, u32[]{:S(2)}, u32[]{:S(2)}) collective-permute-start(bf16[256,256]{1,0:T(8,128)(2,1)S(1)} %get-tuple-element.71), channel_id=1, source_target_pairs={{0,1},{1,0},{2,3},{3,2},{4,5},{5,4},{6,7},{7,6},{8,9},{9,8},{10,11... | collective-permute-start | bytes 393224 | tf_op jit(solution)/shard_map/ppermute | solution.py:418
  108.2 1.3 collective-permute-done.20.g_other
  109.5 2.0 %shard_map.106 = (bf16[32,40,256]{2,1,0:T(8,128)(2,1)}, bf16[128,256]{1,0:T(8,128)(2,1)S(1)}, bf16[128,256]{1,0:T(8,128)(2,1)S(1)}) custom-call(bf16[4,128,256]{2,1,0:T(8,128)(2,1)S(1)} %get-tuple-element.70.x_own, bf16[4,128,256]{2,1,0:T(8,128)(2,1)S(1)} %collective-permute-done.19.x_other, bf16[4,128,256]{2,1,0:T(8,128)(2,1)S(1)} %get-tuple-element.68.state, ...), custom_call_target="tpu_custom_call" | custom-call | flops 268435456 | bytes 4194304 | tf_op jit(solution)/shard_map/pallas_call | solution.py:26
  111.6 6.9 %all-to-all-start.1 = ((bf16[32,40,256]{2,1,0:T(8,128)(2,1)}), bf16[32,40,256]{2,1,0:T(8,128)(2,1)S(1)}, u32[]{:S(2)}, u32[]{:S(2)}) async-start(bf16[32,40,256]{2,1,0:T(8,128)(2,1)} %get-tuple-element.74), calls=%async_computation.1 | async-start | bytes 1310720 | tf_op jit(solution)/shard_map/all_to_all | solution.py:437
  118.5 1.9 %collective-permute-start.21 = (bf16[128,256]{1,0:T(8,128)(2,1)S(1)}, bf16[128,256]{1,0:T(8,128)(2,1)S(1)}, u32[]{:S(2)}, u32[]{:S(2)}) collective-permute-start(bf16[128,256]{1,0:T(8,128)(2,1)S(1)} %get-tuple-element.72), channel_id=1, source_target_pairs={{0,1},{1,0},{2,3},{3,2},{4,5},{5,4},{6,7},{7,6},{8,9},{9,8},{10,11... | collective-permute-start | bytes 196616 | tf_op jit(solution)/shard_map/ppermute | solution.py:428
  121.6 1.2 shard_map.107
  122.9 16.8 %all-to-all-done.1.parts = bf16[32,40,256]{2,1,0:T(8,128)(2,1)S(1)} async-done(((bf16[32,40,256]{2,1,0:T(8,128)(2,1)}), bf16[32,40,256]{2,1,0:T(8,128)(2,1)S(1)}, u32[]{:S(2)}, u32[]{:S(2)}) %all-to-all-start.1) | async-done | bytes 655392 | tf_op jit(solution)/shard_map/all_to_all | solution.py:437
  139.6 0.7 shard_map.108
  (53 shorter events, 11.6 us)
Async XLA Ops:
  2.3 34.3 %all-to-all-start = ((bf16[32,40,256]{2,1,0:T(8,128)(2,1)}), bf16[32,40,256]{2,1,0:T(8,128)(2,1)S(1)}, u32[]{:S(2)}, u32[]{:S(2)}) async-start(bf16[32,40,256]{2,1,0:T(8,128)(2,1)} %shard_map.94), calls=%async_computation | async-start | bytes 1310720 | tf_op jit(solution)/shard_map/all_to_all | solution.py:352
  16.3 3.3 %collective-permute-start = (bf16[272,256]{1,0:T(8,128)(2,1)S(1)}, bf16[272,256]{1,0:T(8,128)(2,1)S(1)}, u32[]{:S(2)}, u32[]{:S(2)}) collective-permute-start(bf16[272,256]{1,0:T(8,128)(2,1)S(1)} %get-tuple-element.41), channel_id=1, source_target_pairs={{0,1},{1,0},{2,3},{3,2},{4,5},{5,4},{6,7},{7,6},{8,9},{9,8},{10,11... | collective-permute-start | bytes 417800 | tf_op jit(solution)/shard_map/ppermute | solution.py:362
  19.6 17.0 %collective-permute-start.1 = (bf16[528,256]{1,0:T(8,128)(2,1)S(1)}, bf16[528,256]{1,0:T(8,128)(2,1)S(1)}, u32[]{:S(2)}, u32[]{:S(2)}) collective-permute-start(bf16[528,256]{1,0:T(8,128)(2,1)S(1)} %get-tuple-element.42), channel_id=1, source_target_pairs={{0,62},{1,63},{2,0},{3,1},{4,2},{5,3},{6,4},{7,5},{8,6},{9,7},{10,... | collective-permute-start | bytes 811016 | tf_op jit(solution)/shard_map/ppermute | solution.py:376
  21.8 11.2 %collective-permute-start.2 = (bf16[256,256]{1,0:T(8,128)(2,1)S(1)}, bf16[256,256]{1,0:T(8,128)(2,1)S(1)}, u32[]{:S(2)}, u32[]{:S(2)}) collective-permute-start(bf16[256,256]{1,0:T(8,128)(2,1)S(1)} %get-tuple-element.43), channel_id=1, source_target_pairs={{0,2},{1,3},{2,4},{3,5},{4,6},{5,7},{6,8},{7,9},{8,10},{9,11},{10,... | collective-permute-start | bytes 393224 | tf_op jit(solution)/shard_map/ppermute | solution.py:377
  36.6 4.0 %collective-permute-start.4 = (bf16[32,40,256]{2,1,0:T(8,128)(2,1)S(1)}, bf16[32,40,256]{2,1,0:T(8,128)(2,1)S(1)}, u32[]{:S(2)}, u32[]{:S(2)}) collective-permute-start(bf16[32,40,256]{2,1,0:T(8,128)(2,1)S(1)} %all-to-all-done.mine), channel_id=1, source_target_pairs={{0,1},{1,0},{2,3},{3,2},{4,5},{5,4},{6,7},{7,6},{8,9},{9,8},{10,11... | collective-permute-start | bytes 1966088 | tf_op jit(solution)/shard_map/ppermute | solution.py:380
  41.6 1.4 collective-permute-start.6
  42.3 0.7 collective-permute-start.5
  43.0 1.4 collective-permute-start.8
  43.7 0.7 collective-permute-start.7
  44.5 1.4 collective-permute-start.10
  45.1 0.7 collective-permute-start.9
  45.9 1.4 collective-permute-start.12
  46.6 0.7 collective-permute-start.11
  47.3 1.4 collective-permute-start.14
  48.0 0.7 collective-permute-start.13
  48.8 1.4 collective-permute-start.16
  49.4 0.7 collective-permute-start.15
  50.2 55.5 %collective-permute-start.18 = (bf16[256,256]{1,0:T(8,128)(2,1)S(1)}, bf16[256,256]{1,0:T(8,128)(2,1)S(1)}, u32[]{:S(2)}, u32[]{:S(2)}) collective-permute-start(bf16[256,256]{1,0:T(8,128)(2,1)S(1)} %get-tuple-element.66), channel_id=1, source_target_pairs={{64,2},{65,3},{66,4},{67,5},{68,6},{69,7},{70,8},{71,9},{72,10},{7... | collective-permute-start | bytes 393224 | tf_op jit(solution)/shard_map/ppermute | solution.py:412
  51.5 54.2 %collective-permute-start.17 = (bf16[256,256]{1,0:T(8,128)(2,1)S(1)}, bf16[256,256]{1,0:T(8,128)(2,1)S(1)}, u32[]{:S(2)}, u32[]{:S(2)}) collective-permute-start(bf16[256,256]{1,0:T(8,128)(2,1)S(1)} %get-tuple-element.66), channel_id=1, source_target_pairs={{64,0},{65,1},{66,2},{67,3},{68,4},{69,5},{70,6},{71,7},{72,8},{73... | collective-permute-start | bytes 393224 | tf_op jit(solution)/shard_map/ppermute | solution.py:411
  52.8 55.4 %collective-permute-start.19 = (bf16[4,128,256]{2,1,0:T(8,128)(2,1)S(1)}, bf16[4,128,256]{2,1,0:T(8,128)(2,1)S(1)}, u32[]{:S(2)}, u32[]{:S(2)}) collective-permute-start(bf16[4,128,256]{2,1,0:T(8,128)(2,1)S(1)} %get-tuple-element.70.x_own), channel_id=1, source_target_pairs={{0,1},{1,0},{2,3},{3,2},{4,5},{5,4},{6,7},{7,6},{8,9},{9,8},{10,11... | collective-permute-start | bytes 786440 | tf_op jit(solution)/shard_map/ppermute | solution.py:416
  106.3 3.2 %collective-permute-start.20 = (bf16[256,256]{1,0:T(8,128)(2,1)S(1)}, bf16[256,256]{1,0:T(8,128)(2,1)S(1)}, u32[]{:S(2)}, u32[]{:S(2)}) collective-permute-start(bf16[256,256]{1,0:T(8,128)(2,1)S(1)} %get-tuple-element.71), channel_id=1, source_target_pairs={{0,1},{1,0},{2,3},{3,2},{4,5},{5,4},{6,7},{7,6},{8,9},{9,8},{10,11... | collective-permute-start | bytes 393224 | tf_op jit(solution)/shard_map/ppermute | solution.py:418
  111.6 28.1 %all-to-all-start.1 = ((bf16[32,40,256]{2,1,0:T(8,128)(2,1)}), bf16[32,40,256]{2,1,0:T(8,128)(2,1)S(1)}, u32[]{:S(2)}, u32[]{:S(2)}) async-start(bf16[32,40,256]{2,1,0:T(8,128)(2,1)} %get-tuple-element.74), calls=%async_computation.1 | async-start | bytes 1310720 | tf_op jit(solution)/shard_map/all_to_all | solution.py:437
  118.5 3.1 %collective-permute-start.21 = (bf16[128,256]{1,0:T(8,128)(2,1)S(1)}, bf16[128,256]{1,0:T(8,128)(2,1)S(1)}, u32[]{:S(2)}, u32[]{:S(2)}) collective-permute-start(bf16[128,256]{1,0:T(8,128)(2,1)S(1)} %get-tuple-element.72), channel_id=1, source_target_pairs={{0,1},{1,0},{2,3},{3,2},{4,5},{5,4},{6,7},{7,6},{8,9},{9,8},{10,11... | collective-permute-start | bytes 196616 | tf_op jit(solution)/shard_map/ppermute | solution.py:428
  120.4 1.2 collective-permute-start.22
  (7 other events, 98.3 us)

commit v7 on v6

--- a/solution.py
+++ b/solution.py
@@ -202,9 +202,13 @@
 def step_kernel(step, sections, mask, deriv, weights, *refs):
     arrived, state_in, outs = refs[:2], refs[2], refs[3:]
     state = outs[0]
-    state[...] = state_in[...]
-
-    @pl.when(lax.axis_index("y") == sections - 1 - step)
+    active = lax.axis_index("y") == sections - 1 - step
+
+    @pl.when(jnp.logical_not(active))
+    def _():
+        state[...] = state_in[...]
+
+    @pl.when(active)
     def _():
         keep = keep_factor(GROUPS)
         if step == 0:

time: 141 us -> 141 us (level)
  no operation moved by 1% of the time
where the time goes in v7:
time: 141 us; the launch traced here: 140 us
  waiting for transfers between devices  83.1 us (59%)
  starting transfers between devices  47.1 us (33%)
  Pallas kernels  7.4 us (5%)
  between operations  1.74 us (1%)
    ppermute x7, waiting for transfers between devices, body(): lax.ppermute(back, ALL, chip_pairs([plane], 1 if plane % 2 else -1, 1))  50.6 us
    all_to_all x1, waiting for transfers between devices, body(): parts = lax.all_to_all(both, ('x', 'z'), 0, 0)  16.8 us
    all_to_all x1, starting transfers between devices, body(): mine = lax.all_to_all(wide, ('x', 'z'), 0, 0)  12.7 us
    pallas_call x15, Pallas kernels, call(): pl.pallas_call(kernel, out_shape=outs, in_specs=ins, out_specs=[VMEM] * l...  7.4 us
    all_to_all x1, starting transfers between devices, body(): parts = lax.all_to_all(both, ('x', 'z'), 0, 0)  6.92 us
    ppermute x1, waiting for transfers between devices, body(): before = lax.ppermute(up, ALL, chip_pairs(every, 1))  6.84 us
    ppermute x7, starting transfers between devices, body(): lax.ppermute(back, ALL, chip_pairs([plane], 1 if plane % 2 else -1, 1))  5.31 us
    ppermute x7, starting transfers between devices, body(): straight = lax.ppermute(back, ALL, chip_pairs([plane], 0, 1))  5.31 us
  transfers between devices with their start and end apart: 25, of which 8 were waited for; matrix products, arithmetic and copies ran while one was open for 0% of the time, Pallas kernels for 2%

profile of v7, /device:TPU:64, one launch (start us, length us, event | category | flops | bytes accessed | tf_op | source)
XLA Modules:
  0.0 140.1 jit_solution(13562253336066064381)
XLA Ops:
  0.7 0.7 copy-done
  1.4 0.9 shard_map.94
  2.3 12.7 %all-to-all-start = ((bf16[32,40,256]{2,1,0:T(8,128)(2,1)}), bf16[32,40,256]{2,1,0:T(8,128)(2,1)S(1)}, u32[]{:S(2)}, u32[]{:S(2)}) async-start(bf16[32,40,256]{2,1,0:T(8,128)(2,1)} %shard_map.94), calls=%async_computation | async-start | bytes 1310720 | tf_op jit(solution)/shard_map/all_to_all | solution.py:356
  16.3 1.9 %collective-permute-start = (bf16[272,256]{1,0:T(8,128)(2,1)S(1)}, bf16[272,256]{1,0:T(8,128)(2,1)S(1)}, u32[]{:S(2)}, u32[]{:S(2)}) collective-permute-start(bf16[272,256]{1,0:T(8,128)(2,1)S(1)} %get-tuple-element.41), channel_id=1, source_target_pairs={{0,1},{1,0},{2,3},{3,2},{4,5},{5,4},{6,7},{7,6},{8,9},{9,8},{10,11... | collective-permute-start | bytes 417800 | tf_op jit(solution)/shard_map/ppermute | solution.py:366
  18.3 1.3 collective-permute-done.got
  19.6 2.1 %collective-permute-start.1 = (bf16[528,256]{1,0:T(8,128)(2,1)S(1)}, bf16[528,256]{1,0:T(8,128)(2,1)S(1)}, u32[]{:S(2)}, u32[]{:S(2)}) collective-permute-start(bf16[528,256]{1,0:T(8,128)(2,1)S(1)} %get-tuple-element.42), channel_id=1, source_target_pairs={{0,62},{1,63},{2,0},{3,1},{4,2},{5,3},{6,4},{7,5},{8,6},{9,7},{10,... | collective-permute-start | bytes 811016 | tf_op jit(solution)/shard_map/ppermute | solution.py:380
  21.8 3.7 %collective-permute-start.2 = (bf16[256,256]{1,0:T(8,128)(2,1)S(1)}, bf16[256,256]{1,0:T(8,128)(2,1)S(1)}, u32[]{:S(2)}, u32[]{:S(2)}) collective-permute-start(bf16[256,256]{1,0:T(8,128)(2,1)S(1)} %get-tuple-element.43), channel_id=1, source_target_pairs={{0,2},{1,3},{2,4},{3,5},{4,6},{5,7},{6,8},{7,9},{8,10},{9,11},{10,... | collective-permute-start | bytes 393224 | tf_op jit(solution)/shard_map/ppermute | solution.py:381
  26.2 6.8 %collective-permute-done.2.before = bf16[256,256]{1,0:T(8,128)(2,1)S(1)} collective-permute-done((bf16[256,256]{1,0:T(8,128)(2,1)S(1)}, bf16[256,256]{1,0:T(8,128)(2,1)S(1)}, u32[]{:S(2)}, u32[]{:S(2)}) %collective-permute-start.2) | collective-permute-done | bytes 131104 | tf_op jit(solution)/shard_map/ppermute | solution.py:381
  33.0 3.6 %collective-permute-done.1.after.refs_4_ = bf16[528,256]{1,0:T(8,128)(2,1)S(1)} collective-permute-done((bf16[528,256]{1,0:T(8,128)(2,1)S(1)}, bf16[528,256]{1,0:T(8,128)(2,1)S(1)}, u32[]{:S(2)}, u32[]{:S(2)}) %collective-permute-start.1) | collective-permute-done | bytes 270368 | tf_op jit(solution)/shard_map/ppermute | solution.py:380
  36.6 1.9 %collective-permute-start.4 = (bf16[32,40,256]{2,1,0:T(8,128)(2,1)S(1)}, bf16[32,40,256]{2,1,0:T(8,128)(2,1)S(1)}, u32[]{:S(2)}, u32[]{:S(2)}) collective-permute-start(bf16[32,40,256]{2,1,0:T(8,128)(2,1)S(1)} %all-to-all-done.mine), channel_id=1, source_target_pairs={{0,1},{1,0},{2,3},{3,2},{4,5},{5,4},{6,7},{7,6},{8,9},{9,8},{10,11... | collective-permute-start | bytes 1966088 | tf_op jit(solution)/shard_map/ppermute | solution.py:384
  38.5 2.1 %collective-permute-done.4.other = bf16[32,40,256]{2,1,0:T(8,128)(2,1)S(1)} collective-permute-done((bf16[32,40,256]{2,1,0:T(8,128)(2,1)S(1)}, bf16[32,40,256]{2,1,0:T(8,128)(2,1)S(1)}, u32[]{:S(2)}, u32[]{:S(2)}) %collective-permute-start.4) | collective-permute-done | bytes 655392 | tf_op jit(solution)/shard_map/ppermute | solution.py:384
  40.6 0.9 shard_map.97
  50.2 1.3 collective-permute-start.18
  51.5 1.3 collective-permute-start.17
  52.8 2.0 %collective-permute-start.19 = (bf16[4,128,256]{2,1,0:T(8,128)(2,1)S(1)}, bf16[4,128,256]{2,1,0:T(8,128)(2,1)S(1)}, u32[]{:S(2)}, u32[]{:S(2)}) collective-permute-start(bf16[4,128,256]{2,1,0:T(8,128)(2,1)S(1)} %get-tuple-element.70.x_own), channel_id=1, source_target_pairs={{0,1},{1,0},{2,3},{3,2},{4,5},{5,4},{6,7},{7,6},{8,9},{9,8},{10,11... | collective-permute-start | bytes 786440 | tf_op jit(solution)/shard_map/ppermute | solution.py:420
  54.9 50.6 %collective-permute-done.18.refs_4_ = bf16[256,256]{1,0:T(8,128)(2,1)S(1)} collective-permute-done((bf16[256,256]{1,0:T(8,128)(2,1)S(1)}, bf16[256,256]{1,0:T(8,128)(2,1)S(1)}, u32[]{:S(2)}, u32[]{:S(2)}) %collective-permute-start.18) | collective-permute-done | bytes 131104 | tf_op jit(solution)/shard_map/ppermute | solution.py:416
  106.0 1.9 %collective-permute-start.20 = (bf16[256,256]{1,0:T(8,128)(2,1)S(1)}, bf16[256,256]{1,0:T(8,128)(2,1)S(1)}, u32[]{:S(2)}, u32[]{:S(2)}) collective-permute-start(bf16[256,256]{1,0:T(8,128)(2,1)S(1)} %get-tuple-element.71), channel_id=1, source_target_pairs={{0,1},{1,0},{2,3},{3,2},{4,5},{5,4},{6,7},{7,6},{8,9},{9,8},{10,11... | collective-permute-start | bytes 393224 | tf_op jit(solution)/shard_map/ppermute | solution.py:422
  108.0 1.3 collective-permute-done.20.g_other
  109.3 2.0 %shard_map.106 = (bf16[32,40,256]{2,1,0:T(8,128)(2,1)}, bf16[128,256]{1,0:T(8,128)(2,1)S(1)}, bf16[128,256]{1,0:T(8,128)(2,1)S(1)}) custom-call(bf16[4,128,256]{2,1,0:T(8,128)(2,1)S(1)} %get-tuple-element.70.x_own, bf16[4,128,256]{2,1,0:T(8,128)(2,1)S(1)} %collective-permute-done.19.x_other, bf16[4,128,256]{2,1,0:T(8,128)(2,1)S(1)} %get-tuple-element.68.state, ...), custom_call_target="tpu_custom_call" | custom-call | flops 268435456 | bytes 4194304 | tf_op jit(solution)/shard_map/pallas_call | solution.py:26
  111.3 6.9 %all-to-all-start.1 = ((bf16[32,40,256]{2,1,0:T(8,128)(2,1)}), bf16[32,40,256]{2,1,0:T(8,128)(2,1)S(1)}, u32[]{:S(2)}, u32[]{:S(2)}) async-start(bf16[32,40,256]{2,1,0:T(8,128)(2,1)} %get-tuple-element.74), calls=%async_computation.1 | async-start | bytes 1310720 | tf_op jit(solution)/shard_map/all_to_all | solution.py:441
  118.2 1.9 %collective-permute-start.21 = (bf16[128,256]{1,0:T(8,128)(2,1)S(1)}, bf16[128,256]{1,0:T(8,128)(2,1)S(1)}, u32[]{:S(2)}, u32[]{:S(2)}) collective-permute-start(bf16[128,256]{1,0:T(8,128)(2,1)S(1)} %get-tuple-element.72), channel_id=1, source_target_pairs={{0,1},{1,0},{2,3},{3,2},{4,5},{5,4},{6,7},{7,6},{8,9},{9,8},{10,11... | collective-permute-start | bytes 196616 | tf_op jit(solution)/shard_map/ppermute | solution.py:432
  121.4 1.2 shard_map.107
  122.6 16.8 %all-to-all-done.1.parts = bf16[32,40,256]{2,1,0:T(8,128)(2,1)S(1)} async-done(((bf16[32,40,256]{2,1,0:T(8,128)(2,1)}), bf16[32,40,256]{2,1,0:T(8,128)(2,1)S(1)}, u32[]{:S(2)}, u32[]{:S(2)}) %all-to-all-start.1) | async-done | bytes 655392 | tf_op jit(solution)/shard_map/all_to_all | solution.py:441
  139.4 0.7 shard_map.108
  (53 shorter events, 11.6 us)
Async XLA Ops:
  2.3 34.3 %all-to-all-start = ((bf16[32,40,256]{2,1,0:T(8,128)(2,1)}), bf16[32,40,256]{2,1,0:T(8,128)(2,1)S(1)}, u32[]{:S(2)}, u32[]{:S(2)}) async-start(bf16[32,40,256]{2,1,0:T(8,128)(2,1)} %shard_map.94), calls=%async_computation | async-start | bytes 1310720 | tf_op jit(solution)/shard_map/all_to_all | solution.py:356
  16.3 3.3 %collective-permute-start = (bf16[272,256]{1,0:T(8,128)(2,1)S(1)}, bf16[272,256]{1,0:T(8,128)(2,1)S(1)}, u32[]{:S(2)}, u32[]{:S(2)}) collective-permute-start(bf16[272,256]{1,0:T(8,128)(2,1)S(1)} %get-tuple-element.41), channel_id=1, source_target_pairs={{0,1},{1,0},{2,3},{3,2},{4,5},{5,4},{6,7},{7,6},{8,9},{9,8},{10,11... | collective-permute-start | bytes 417800 | tf_op jit(solution)/shard_map/ppermute | solution.py:366
  19.6 17.0 %collective-permute-start.1 = (bf16[528,256]{1,0:T(8,128)(2,1)S(1)}, bf16[528,256]{1,0:T(8,128)(2,1)S(1)}, u32[]{:S(2)}, u32[]{:S(2)}) collective-permute-start(bf16[528,256]{1,0:T(8,128)(2,1)S(1)} %get-tuple-element.42), channel_id=1, source_target_pairs={{0,62},{1,63},{2,0},{3,1},{4,2},{5,3},{6,4},{7,5},{8,6},{9,7},{10,... | collective-permute-start | bytes 811016 | tf_op jit(solution)/shard_map/ppermute | solution.py:380
  21.8 11.2 %collective-permute-start.2 = (bf16[256,256]{1,0:T(8,128)(2,1)S(1)}, bf16[256,256]{1,0:T(8,128)(2,1)S(1)}, u32[]{:S(2)}, u32[]{:S(2)}) collective-permute-start(bf16[256,256]{1,0:T(8,128)(2,1)S(1)} %get-tuple-element.43), channel_id=1, source_target_pairs={{0,2},{1,3},{2,4},{3,5},{4,6},{5,7},{6,8},{7,9},{8,10},{9,11},{10,... | collective-permute-start | bytes 393224 | tf_op jit(solution)/shard_map/ppermute | solution.py:381
  36.6 4.0 %collective-permute-start.4 = (bf16[32,40,256]{2,1,0:T(8,128)(2,1)S(1)}, bf16[32,40,256]{2,1,0:T(8,128)(2,1)S(1)}, u32[]{:S(2)}, u32[]{:S(2)}) collective-permute-start(bf16[32,40,256]{2,1,0:T(8,128)(2,1)S(1)} %all-to-all-done.mine), channel_id=1, source_target_pairs={{0,1},{1,0},{2,3},{3,2},{4,5},{5,4},{6,7},{7,6},{8,9},{9,8},{10,11... | collective-permute-start | bytes 1966088 | tf_op jit(solution)/shard_map/ppermute | solution.py:384
  41.6 1.4 collective-permute-start.6
  42.3 0.7 collective-permute-start.5
  43.0 1.4 collective-permute-start.8
  43.7 0.7 collective-permute-start.7
  44.5 1.4 collective-permute-start.10
  45.2 0.7 collective-permute-start.9
  45.9 1.4 collective-permute-start.12
  46.6 0.7 collective-permute-start.11
  47.4 1.4 collective-permute-start.14
  48.0 0.7 collective-permute-start.13
  48.8 1.4 collective-permute-start.16
  49.5 0.7 collective-permute-start.15
  50.2 55.2 %collective-permute-start.18 = (bf16[256,256]{1,0:T(8,128)(2,1)S(1)}, bf16[256,256]{1,0:T(8,128)(2,1)S(1)}, u32[]{:S(2)}, u32[]{:S(2)}) collective-permute-start(bf16[256,256]{1,0:T(8,128)(2,1)S(1)} %get-tuple-element.66), channel_id=1, source_target_pairs={{64,2},{65,3},{66,4},{67,5},{68,6},{69,7},{70,8},{71,9},{72,10},{7... | collective-permute-start | bytes 393224 | tf_op jit(solution)/shard_map/ppermute | solution.py:416
  51.5 54.0 %collective-permute-start.17 = (bf16[256,256]{1,0:T(8,128)(2,1)S(1)}, bf16[256,256]{1,0:T(8,128)(2,1)S(1)}, u32[]{:S(2)}, u32[]{:S(2)}) collective-permute-start(bf16[256,256]{1,0:T(8,128)(2,1)S(1)} %get-tuple-element.66), channel_id=1, source_target_pairs={{64,0},{65,1},{66,2},{67,3},{68,4},{69,5},{70,6},{71,7},{72,8},{73... | collective-permute-start | bytes 393224 | tf_op jit(solution)/shard_map/ppermute | solution.py:415
  52.8 55.1 %collective-permute-start.19 = (bf16[4,128,256]{2,1,0:T(8,128)(2,1)S(1)}, bf16[4,128,256]{2,1,0:T(8,128)(2,1)S(1)}, u32[]{:S(2)}, u32[]{:S(2)}) collective-permute-start(bf16[4,128,256]{2,1,0:T(8,128)(2,1)S(1)} %get-tuple-element.70.x_own), channel_id=1, source_target_pairs={{0,1},{1,0},{2,3},{3,2},{4,5},{5,4},{6,7},{7,6},{8,9},{9,8},{10,11... | collective-permute-start | bytes 786440 | tf_op jit(solution)/shard_map/ppermute | solution.py:420
  106.0 3.2 %collective-permute-start.20 = (bf16[256,256]{1,0:T(8,128)(2,1)S(1)}, bf16[256,256]{1,0:T(8,128)(2,1)S(1)}, u32[]{:S(2)}, u32[]{:S(2)}) collective-permute-start(bf16[256,256]{1,0:T(8,128)(2,1)S(1)} %get-tuple-element.71), channel_id=1, source_target_pairs={{0,1},{1,0},{2,3},{3,2},{4,5},{5,4},{6,7},{7,6},{8,9},{9,8},{10,11... | collective-permute-start | bytes 393224 | tf_op jit(solution)/shard_map/ppermute | solution.py:422
  111.3 28.1 %all-to-all-start.1 = ((bf16[32,40,256]{2,1,0:T(8,128)(2,1)}), bf16[32,40,256]{2,1,0:T(8,128)(2,1)S(1)}, u32[]{:S(2)}, u32[]{:S(2)}) async-start(bf16[32,40,256]{2,1,0:T(8,128)(2,1)} %get-tuple-element.74), calls=%async_computation.1 | async-start | bytes 1310720 | tf_op jit(solution)/shard_map/all_to_all | solution.py:441
  118.2 3.1 %collective-permute-start.21 = (bf16[128,256]{1,0:T(8,128)(2,1)S(1)}, bf16[128,256]{1,0:T(8,128)(2,1)S(1)}, u32[]{:S(2)}, u32[]{:S(2)}) collective-permute-start(bf16[128,256]{1,0:T(8,128)(2,1)S(1)} %get-tuple-element.72), channel_id=1, source_target_pairs={{0,1},{1,0},{2,3},{3,2},{4,5},{5,4},{6,7},{7,6},{8,9},{9,8},{10,11... | collective-permute-start | bytes 196616 | tf_op jit(solution)/shard_map/ppermute | solution.py:432
  120.2 1.2 collective-permute-start.22
  (7 other events, 98.3 us)
